TPU v7x, 256 devices: a whole 4x4x8 slice. The times are simulated.
256 devices in a mesh: section: 8 (over x, core), patch: 32 (over y, z).
Axes of the slice: x: 4, y: 4, z: 8, core: 2. Of those that a mesh axis runs over, the one named last changes fastest.
Arguments:
- arriving: bfloat16 [8, 32, 384, 1536], P('section', 'patch'), may hold values from -6 to 6
- modulation: float32 [8, 2, 1536], P('section'), may hold values from -3 to 3
- gate: float32 [8, 1536], P('section'), may hold values from 1 to 4
- w_query: bfloat16 [8, 1536, 1536], P('section', 'patch'), may hold values from -0.15625 to 0.15625
- w_kv: bfloat16 [8, 1536, 3072], P('section'), may hold values from -0.15625 to 0.15625
- w_out: bfloat16 [8, 1536, 1536], P('section', 'patch'), may hold values from -0.15625 to 0.15625
- qk_gain: float32 [8, 2, 1536], P('section'), may hold values from 0.56 to 6
- neighbors: int32 [32, 4], P('patch'), may hold values from 0 to 31, as said below
- live: int32 [32], P('patch'), may hold values from 2 to 4, as said below
Outputs:
- handed: bfloat16 [8, 32, 384, 1536], P('section', 'patch')
Inputs may be any that keep to these rules, and one draw needn't show every extreme that they name: `neighbors`: row i names tile i in slot 0 and, in slots 1 to live[i] - 1, distinct other tiles j with |i - j| <= 2; slots from live[i] on name i. `live`: some tile uses all 4 slots.
All inputs are finite; a program needn't handle non-finite values.
Results may differ from a plain program's by a relative error of at most 0.0065.
The roundings to bfloat16 on the way count: a program that leaves them out, or rounds other values in their place, can miss the bound.
Values may be sent and summed in bfloat16 or wider, within the bound.
No kernel may reach another device: no remote copies, remote signals or barrier semaphores. Data moves between devices by JAX's collectives and lax.ppermute only.
A program may use at most 128 MiB of HBM per device.

v0:
```python
import math

import jax
import jax.numpy as jnp
from jax import lax
from jax.sharding import PartitionSpec as P

HEADS = 12
HEAD_DIM = 128
SPAN = 2
NB = 4


def shifted(value, axis, steps):
    count = lax.axis_size(axis)
    leading, last = (max(0, -steps), min(count, count - steps))
    return lax.ppermute(value, axis, [(source, source + steps) for source in range(leading, last)])


def from_behind(block, axis, distance):
    devices = range(lax.axis_size(axis))
    route = [((i - distance) % len(devices), i) for i in devices]
    return lax.ppermute(block, axis, route)


def layer_norm(values):
    average = jnp.mean(values, axis=-1, keepdims=True)
    centered = values - average
    variance = jnp.mean(centered * centered, axis=-1, keepdims=True)
    return centered * lax.rsqrt(variance + 1e-06)


def head_norm(values, gains):
    count_rows = values.shape[0]
    shaped = values.reshape(count_rows, HEADS, HEAD_DIM)
    square = jnp.mean(shaped * shaped, axis=-1, keepdims=True)
    normed = (shaped * lax.rsqrt(square + 1e-06)).reshape(count_rows, HEADS * HEAD_DIM)
    return (normed * gains).astype(jnp.bfloat16)


def on_device(arriving, modulation, gate, w_query, w_kv, w_out, qk_gain, neighbors, live):
    tiles_here = arriving.shape[1]
    tile_len = arriving.shape[2]
    width = arriving.shape[3]
    inner = qk_gain.shape[2]
    rows_count = tiles_here * tile_len
    residual = arriving[0].reshape(rows_count, width).astype(jnp.float32)
    normed = (layer_norm(residual) * (1.0 + modulation[0, 1]) + modulation[0, 0]).astype(
        jnp.bfloat16
    )
    query_shard = w_query[0]
    out_shard = w_out[0]
    raw_kv = jnp.dot(normed, w_kv[0], preferred_element_type=jnp.float32)
    columns = normed
    raw_query = jnp.dot(
        columns,
        lax.all_gather(query_shard, "patch", axis=0, tiled=True),
        preferred_element_type=jnp.float32,
    )
    query = head_norm(raw_query, qk_gain[0, 0]).reshape(tiles_here, tile_len, HEADS, HEAD_DIM)
    key_rows = head_norm(raw_kv[:, :inner], qk_gain[0, 1])
    value_rows = raw_kv[:, inner:].astype(jnp.bfloat16)
    kv_tiles = jnp.concatenate([key_rows, value_rows], axis=1).reshape(
        tiles_here, tile_len, 2 * inner
    )
    reach = (SPAN + tiles_here - 1) // tiles_here
    lower = []
    upper = []
    for distance in range(1, reach + 1):
        for toward in (1, -1):
            moved = shifted(kv_tiles, "patch", toward * distance)
            if toward == 1:
                lower.append(moved)
            else:
                upper.append(moved)
    window = jnp.concatenate(list(reversed(lower)) + [kv_tiles] + upper, axis=0)
    position = lax.axis_index("patch")
    first_tile = (position - reach) * tiles_here
    local_slots = neighbors - first_tile
    gathered = jnp.take(window, local_slots, axis=0).reshape(
        tiles_here, NB * tile_len, 2, HEADS, HEAD_DIM
    )
    key_block = gathered[:, :, 0]
    value_block = gathered[:, :, 1]
    key_live = (jnp.arange(NB * tile_len, dtype=jnp.int32) // tile_len)[None, :] < live[:, None]
    scale = 1.0 / math.sqrt(HEAD_DIM)

    def per_head(head_index):
        head_query = lax.dynamic_index_in_dim(query, head_index, 2, keepdims=False)
        head_keys = lax.dynamic_index_in_dim(key_block, head_index, 2, keepdims=False)
        head_values = lax.dynamic_index_in_dim(value_block, head_index, 2, keepdims=False)
        scores = (
            jnp.einsum("tqd,tkd->tqk", head_query, head_keys, preferred_element_type=jnp.float32)
            * scale
        )
        scores = jnp.where(key_live[:, None, :], scores, -1e30)
        highest = jnp.max(scores, axis=-1, keepdims=True)
        exponent = jnp.exp(scores - highest)
        total = jnp.sum(exponent, axis=-1, keepdims=True)
        prob_bf = (exponent / total).astype(jnp.bfloat16)
        mixed = jnp.einsum("tqk,tkd->tqd", prob_bf, head_values, preferred_element_type=jnp.float32)
        return mixed.astype(jnp.bfloat16)

    per_heads = lax.map(per_head, jnp.arange(HEADS, dtype=jnp.int32))
    attended = jnp.transpose(per_heads, (1, 2, 0, 3)).reshape(rows_count, inner)
    columns = attended
    branch = jnp.dot(
        columns,
        lax.all_gather(out_shard, "patch", axis=0, tiled=True),
        preferred_element_type=jnp.float32,
    )
    layer_out = (
        (residual + gate[0] * branch).astype(jnp.bfloat16).reshape(1, tiles_here, tile_len, width)
    )
    return from_behind(layer_out, "section", 1)


def solution(mesh):
    placed = (
        P("section", "patch", None, None),
        P("section", None, None),
        P("section", None),
        P("section", "patch", None),
        P("section", None, None),
        P("section", "patch", None),
        P("section", None, None),
        P("patch", None),
        P("patch"),
    )
    return jax.shard_map(
        on_device,
        mesh=mesh,
        in_specs=placed,
        out_specs=P("section", "patch", None, None),
        check_vma=False,
    )
```

profile of v0, /device:TPU:24, one launch (start us, length us, event | category | flops | bytes accessed | tf_op | source)
XLA Modules:
  0.0 434.2 jit_solution(1671464410865841318)
XLA Ops:
  9.7 1.7 fusion.33
  11.4 6.5 %fusion.15 = f32[384,3072]{1,0:T(8,128)S(1)} fusion(bf16[1,1536,3072]{2,1,0:T(8,128)(2,1)} %param.15, bf16[1,1,384,1536]{3,2,1,0:T(8,128)(2,1)S(1)} %copy-done.1, f32[1536]{0:T(1024)S(1)} %get-tuple-element.77, f32[1536]{0:T(1024)S(1)} %get-tuple-element.76, f32[384]{0:T(512)S(1)} %add_rsqrt_fusion.2, f32[384]{0:T(512)S(1)} %broadcast_multiply_fusion), kind=kOutput, calls=%fused_computation.26 | convolution fusion | flops 3627417600 | bytes 15350784 | tf_op jit(solution)/shard_map/dot_general | solution.py:53
  18.1 2.0 copy-done
  20.1 1.7 slice_multiply_fusion
  21.7 2.0 copy.15
  25.4 2.0 copy.16
  27.4 2.9 multiply_convert_fusion
  30.4 1.7 maximum_bitcast_fusion
  32.1 5.2 %collective-permute-start = (bf16[1,384,3072]{2,1,0:T(8,128)(2,1)}, bf16[1,384,3072]{2,1,0:T(8,128)(2,1)}, u32[]{:S(2)}, u32[]{:S(2)}) collective-permute-start(bf16[1,384,3072]{2,1,0:T(8,128)(2,1)} %maximum_bitcast_fusion), channel_id=1, source_target_pairs={{0,2},{1,3},{2,4},{3,5},{4,6},{5,7},{6,8},{7,9},{8,10},{9,11},{10,... | collective-permute-start | bytes 7077896 | tf_op jit(solution)/shard_map/ppermute | solution.py:17
  37.3 3.8 collective-permute-start.1
  41.1 4.2 collective-permute-start.2
  45.3 3.6 collective-permute-start.3
  49.1 63.5 %collective-permute-done = bf16[1,384,3072]{2,1,0:T(8,128)(2,1)} collective-permute-done((bf16[1,384,3072]{2,1,0:T(8,128)(2,1)}, bf16[1,384,3072]{2,1,0:T(8,128)(2,1)}, u32[]{:S(2)}, u32[]{:S(2)}) %collective-permute-start) | collective-permute-done | bytes 2359328 | tf_op jit(solution)/shard_map/ppermute | solution.py:17
  112.6 1.8 constant_dynamic-update-slice_fusion.5
  114.5 102.9 %collective-permute-done.1 = bf16[1,384,3072]{2,1,0:T(8,128)(2,1)} collective-permute-done((bf16[1,384,3072]{2,1,0:T(8,128)(2,1)}, bf16[1,384,3072]{2,1,0:T(8,128)(2,1)}, u32[]{:S(2)}, u32[]{:S(2)}) %collective-permute-start.1) | collective-permute-done | bytes 2359328 | tf_op jit(solution)/shard_map/ppermute | solution.py:17
  217.3 1.8 constant_dynamic-update-slice_fusion.4
  219.4 1.8 constant_dynamic-update-slice_fusion.2
  221.3 1.7 collective-permute-done.3
  222.9 1.8 constant_dynamic-update-slice_fusion.1
  224.8 4.6 %fusion.45 = (bf16[5,384,1536]{2,1,0:T(8,128)(2,1)}, bf16[5,384,1536]{2,1,0:T(8,128)(2,1)}) fusion(bf16[5,384,3072]{2,1,0:T(8,128)(2,1)S(1)} %constant_dynamic-update-slice_fusion.1), kind=kLoop, calls=%fused_computation.74 | loop fusion | bytes 23592960 | tf_op jit(solution)/shard_map/jit(_take)/gather | solution.py:80
  229.4 5.6 %gather_fusion = bf16[4,384,1536]{2,1,0:T(8,128)(2,1)} fusion(bf16[5,384,1536]{2,1,0:T(8,128)(2,1)} %get-tuple-element.96, s32[1024]{0:T(1024)S(1)} %pad_clamp_fusion), kind=kCustom, calls=%fused_computation | custom fusion | bytes 9437200 | tf_op jit(solution)/shard_map/jit(_take)/gather | solution.py:80
  235.0 5.8 %gather_fusion.1 = bf16[4,384,1536]{2,1,0:T(8,128)(2,1)} fusion(bf16[5,384,1536]{2,1,0:T(8,128)(2,1)} %get-tuple-element.97, s32[1024]{0:T(1024)S(1)} %pad_clamp_fusion), kind=kCustom, calls=%fused_computation.1 | custom fusion | bytes 9437200 | tf_op jit(solution)/shard_map/jit(_take)/gather | solution.py:80
  240.8 9.1 %pad_maximum_fusion = bf16[1,4,384,3072]{3,2,1,0:T(8,128)(2,1)} fusion(bf16[1,4,384,1536]{3,2,1,0:T(8,128)(2,1)} %bitcast.99, bf16[1,4,384,1536]{3,2,1,0:T(8,128)(2,1)} %bitcast.98), kind=kLoop, calls=%fused_computation.25 | loop fusion | flops 18874368 | bytes 18874368
  250.0 15.4 %copy.17 = bf16[1,4,384,3072]{2,1,3,0:T(4,128)(2,1)} copy(bf16[1,4,384,3072]{3,2,1,0:T(8,128)(2,1)} %pad_maximum_fusion) | data formatting | bytes 18874368
  265.4 16.1 %gather.7 = bf16[1,1536,2,12,128]{1,4,3,2,0:T(8,128)(2,1)} reshape(bf16[1,4,384,3072]{2,1,3,0:T(4,128)(2,1)} %copy.17) | data formatting | bytes 18874368 | tf_op jit(solution)/shard_map/jit(_take)/gather | solution.py:80
  281.4 8.2 %broadcast_select_fusion = bf16[1,1536,2,12,128]{1,4,3,2,0:T(8,128)(2,1)} fusion(bf16[1,1536,2,12,128]{1,4,3,2,0:T(8,128)(2,1)} %gather.7, pred[1536]{0:T(1024)(128)(4,1)S(1)} %broadcast_in_dim.49), kind=kLoop, calls=%fused_computation.28 | loop fusion | flops 4718592 | bytes 18875904 | tf_op jit(solution)/shard_map/jit(_take)/select_n | solution.py:80
  289.7 8.5 %slice_bitcast_fusion = (bf16[1,1536,12,128]{1,3,2,0:T(8,128)(2,1)}, bf16[1,1536,12,128]{1,3,2,0:T(8,128)(2,1)}) fusion(bf16[1,1536,2,12,128]{1,4,3,2,0:T(8,128)(2,1)} %broadcast_select_fusion), kind=kLoop, calls=%fused_computation.29 | loop fusion | bytes 18874368 | tf_op jit(solution)/shard_map/squeeze | solution.py:84
  298.2 6.7 %copy.14 = bf16[1536,1536]{1,0:T(8,128)(2,1)} copy(bf16[1536,1536]{0,1:T(8,128)(2,1)} %bitcast.102) | data formatting | bytes 9437184 | tf_op jit(solution)/shard_map/dot_general | solution.py:55
  305.0 4.8 %multiply_reduce_fusion = (f32[384,12]{0,1:T(8,128)S(1)}, f32[384,12,128]{0,2,1:T(8,128)S(1)}) fusion(bf16[12,128,1536]{2,1,0:T(8,128)(2,1)} %bitcast.103, f32[1536]{0:T(1024)S(1)} %copy-done.7, f32[1536]{0:T(1024)S(1)} %copy-done.5, f32[384]{0:T(512)S(1)} %copy-done.10, f32[384]{0:T(512)S(1)} %broadcast_multiply_fusion, ...), kind=kOutput, calls=%fused_computation.51 | convolution fusion | flops 1816653312 | bytes 8291328 | tf_op jit(solution)/shard_map/dot_general | solution.py:55
  310.1 94.6 %while.11 = (s32[]{:T(128)}, bf16[12,1,384,128]{2,3,0,1:T(8,128)(2,1)}, s32[12]{0:T(128)S(1)}, bf16[1,384,12,128]{1,3,2,0:T(8,128)(2,1)S(1)}, bf16[1,1536,12,128...) while((s32[]{:T(128)}, ...), condition=%wide.region_7.8_spmd.clone, body=%wide.region_4.7_spmd.clone.sunk | while | flops 306770688 | bytes 8467099 | solution.py:104
  313.6 1.6 fusion.53
  321.4 1.6 fusion.53
  323.5 1.6 fusion.55
  329.3 1.6 fusion.53
  331.4 1.6 fusion.55
  337.2 1.6 fusion.53
  345.1 1.6 fusion.53
  347.2 1.6 fusion.55
  353.0 1.6 fusion.53
  360.8 1.6 fusion.53
  368.7 1.6 fusion.53
  376.6 1.6 fusion.53
  378.7 1.6 fusion.55
  384.5 1.6 fusion.53
  392.3 1.6 fusion.53
  400.2 1.6 fusion.53
  404.7 4.8 %fusion.29 = bf16[1,1,384,1536]{3,2,1,0:T(8,128)(2,1)S(1)} fusion(bf16[384,1536]{0,1:T(8,128)(2,1)} %bitcast.106, bf16[1,1536,1536]{2,1,0:T(8,128)(2,1)} %all-gather.7.cloned.1.call-done, bf16[1,1,384,1536]{3,2,1,0:T(8,128)(2,1)S(1)} %copy-done.2, f32[1536]{0:T(1024)S(1)} %reduce.6), kind=kOutput, calls=%fused_computation.40 | convolution fusion | flops 1814298624 | bytes 8263680 | tf_op jit(solution)/shard_map/dot_general | solution.py:107
  409.5 16.8 %collective-permute-done.4 = bf16[1,1,384,1536]{3,2,1,0:T(8,128)(2,1)S(1)} collective-permute-done((bf16[1,1,384,1536]{3,2,1,0:T(8,128)(2,1)S(1)}, bf16[1,1,384,1536]{3,2,1,0:T(8,128)(2,1)S(1)}, u32[]{:S(2)}, u32[]{:S(2)}) %collective-permute-start.4) | collective-permute-done | bytes 1179680 | tf_op jit(solution)/shard_map/ppermute | solution.py:23
  (119 shorter events, 50.5 us)
Async XLA Ops:
  6.5 4.9 %copy-start.1 = (bf16[1,1,384,1536]{3,2,1,0:T(8,128)(2,1)S(1)}, bf16[1,1,384,1536]{3,2,1,0:T(8,128)(2,1)}, u32[]{:S(2)}) copy-start(bf16[1,1,384,1536]{3,2,1,0:T(8,128)(2,1)} %param.11) | copy-start | bytes 3538948
  6.5 291.6 %all-gather.5.cloned.1.call-start = ((), (), s32[]{:S(2)}) async-start(), calls=%async_computation | async-start | bytes 4866048 | tf_op jit(solution)/shard_map/all_gather | solution.py:57
  7.3 397.4 %all-gather.7.cloned.1.call-start = ((), (), s32[]{:S(2)}) async-start(), calls=%async_computation.1 | async-start | bytes 4866048 | tf_op jit(solution)/shard_map/all_gather | solution.py:109
  8.1 9.8 %copy-start.4 = (f32[1536]{0:T(1024)}, f32[1536]{0:T(1024)S(1)}, u32[]{:S(2)}) copy-start(f32[1536]{0:T(1024)S(1)} %get-tuple-element.76) | copy-start | bytes 18436
  8.1 9.8 %copy-start.6 = (f32[1536]{0:T(1024)}, f32[1536]{0:T(1024)S(1)}, u32[]{:S(2)}) copy-start(f32[1536]{0:T(1024)S(1)} %get-tuple-element.77) | copy-start | bytes 18436
  11.4 6.5 %copy-start.9 = (f32[384]{0:T(512)}, f32[384]{0:T(512)S(1)}, u32[]{:S(2)}) copy-start(f32[384]{0:T(512)S(1)} %add_rsqrt_fusion.2) | copy-start | bytes 4612
  17.9 2.1 copy-start
  25.4 2.0 copy-start.3
  30.3 18.7 %copy-start.11 = (s32[1,4]{1,0:T(1,128)S(1)}, s32[1,4]{1,0:T(1,128)}, u32[]{:S(2)}) copy-start(s32[1,4]{1,0:T(1,128)} %param.18) | copy-start | bytes 52
  30.3 18.8 %copy-start.8 = (f32[1,1536]{1,0:T(1,128)S(1)}, f32[1,1536]{1,0:T(1,128)}, u32[]{:S(2)}) copy-start(f32[1,1536]{1,0:T(1,128)} %param.13) | copy-start | bytes 18436
  32.1 80.5 %collective-permute-start = (bf16[1,384,3072]{2,1,0:T(8,128)(2,1)}, bf16[1,384,3072]{2,1,0:T(8,128)(2,1)}, u32[]{:S(2)}, u32[]{:S(2)}) collective-permute-start(bf16[1,384,3072]{2,1,0:T(8,128)(2,1)} %maximum_bitcast_fusion), channel_id=1, source_target_pairs={{0,2},{1,3},{2,4},{3,5},{4,6},{5,7},{6,8},{7,9},{8,10},{9,11},{10,... | collective-permute-start | bytes 7077896 | tf_op jit(solution)/shard_map/ppermute | solution.py:17
  37.3 180.0 %collective-permute-start.1 = (bf16[1,384,3072]{2,1,0:T(8,128)(2,1)}, bf16[1,384,3072]{2,1,0:T(8,128)(2,1)}, u32[]{:S(2)}, u32[]{:S(2)}) collective-permute-start(bf16[1,384,3072]{2,1,0:T(8,128)(2,1)} %maximum_bitcast_fusion), channel_id=1, source_target_pairs={{0,1},{1,2},{2,3},{3,4},{4,5},{5,6},{6,7},{7,8},{8,9},{9,10},{10,1... | collective-permute-start | bytes 7077896 | tf_op jit(solution)/shard_map/ppermute | solution.py:17
  41.1 178.3 %collective-permute-start.2 = (bf16[1,384,3072]{2,1,0:T(8,128)(2,1)}, bf16[1,384,3072]{2,1,0:T(8,128)(2,1)}, u32[]{:S(2)}, u32[]{:S(2)}) collective-permute-start(bf16[1,384,3072]{2,1,0:T(8,128)(2,1)} %maximum_bitcast_fusion), channel_id=1, source_target_pairs={{1,0},{2,1},{3,2},{4,3},{5,4},{6,5},{7,6},{8,7},{9,8},{10,9},{11,1... | collective-permute-start | bytes 7077896 | tf_op jit(solution)/shard_map/ppermute | solution.py:17
  45.3 177.6 %collective-permute-start.3 = (bf16[1,384,3072]{2,1,0:T(8,128)(2,1)}, bf16[1,384,3072]{2,1,0:T(8,128)(2,1)}, u32[]{:S(2)}, u32[]{:S(2)}) collective-permute-start(bf16[1,384,3072]{2,1,0:T(8,128)(2,1)} %maximum_bitcast_fusion), channel_id=1, source_target_pairs={{2,0},{3,1},{4,2},{5,3},{6,4},{7,5},{8,6},{9,7},{10,8},{11,9},{12,... | collective-permute-start | bytes 7077896 | tf_op jit(solution)/shard_map/ppermute | solution.py:17
  298.2 6.8 %copy-start.2 = (bf16[1,1,384,1536]{3,2,1,0:T(8,128)(2,1)S(1)}, bf16[1,1,384,1536]{3,2,1,0:T(8,128)(2,1)}, u32[]{:S(2)}) copy-start(bf16[1,1,384,1536]{3,2,1,0:T(8,128)(2,1)} %param.11) | copy-start | bytes 3538948
  298.2 6.8 %copy-start.5 = (f32[1536]{0:T(1024)S(1)}, f32[1536]{0:T(1024)}, u32[]{:S(2)}) copy-start(f32[1536]{0:T(1024)} %copy-done.4) | copy-start | bytes 18436
  298.2 6.8 %copy-start.7 = (f32[1536]{0:T(1024)S(1)}, f32[1536]{0:T(1024)}, u32[]{:S(2)}) copy-start(f32[1536]{0:T(1024)} %copy-done.6) | copy-start | bytes 18436
  298.2 6.8 %copy-start.10 = (f32[384]{0:T(512)S(1)}, f32[384]{0:T(512)}, u32[]{:S(2)}) copy-start(f32[384]{0:T(512)} %copy-done.9) | copy-start | bytes 4612
  409.5 16.8 %collective-permute-start.4 = (bf16[1,1,384,1536]{3,2,1,0:T(8,128)(2,1)S(1)}, bf16[1,1,384,1536]{3,2,1,0:T(8,128)(2,1)S(1)}, u32[]{:S(2)}, u32[]{:S(2)}) collective-permute-start(bf16[1,1,384,1536]{3,2,1,0:T(8,128)(2,1)S(1)} %fusion.29), channel_id=1, source_target_pairs={{224,0},{0,32},{32,64},{64,96},{96,128},{128,160},{160,192},{192,2... | collective-permute-start | bytes 3538952 | tf_op jit(solution)/shard_map/ppermute | solution.py:23
Sparse Core Ops, SparseCore 0:
  9.9 215.9 all-gather.4
  228.5 77.4 all-gather.6
where the time goes:
time: 437 us; the launch traced here: 434 us
  waiting for transfers between devices  186 us (43%)
  local copies, waits for them, and re-layouts  94.8 us (22%)
  matrix products  54.4 us (12%)
  other arithmetic  43.7 us (10%)
  loops' own time  25.1 us (6%)
  starting transfers between devices  16.9 us (4%)
  between operations  13.7 us (3%)
    ppermute x4, waiting for transfers between devices, shifted(): lax.ppermute(value, axis, [(source, source + steps) for source in range(l...  168 us
    gather x4, local copies, waits for them, and re-layouts, on_device(): jnp.take(window, local_slots, axis=0)  32.1 us
    another operation x1, loops' own time, on_device(): per_heads = lax.map(per_head, jnp.arange(HEADS, dtype=jnp.int32))  25.1 us
    unnamed x29, local copies, waits for them, and re-layouts  23.9 us
    dot_general x12, matrix products, per_head(): jnp.einsum('tqd,tkd->tqk', head_query, head_keys, preferred_element_type=...  19.3 us
    dot_general x12, matrix products, per_head(): jnp.einsum('tqk,tkd->tqd', prob_bf, head_values, preferred_element_type=j...  19 us
    ppermute x1, waiting for transfers between devices, from_behind(): return lax.ppermute(block, axis, route)  16.8 us
    ppermute x4, starting transfers between devices, shifted(): lax.ppermute(value, axis, [(source, source + steps) for source in range(l...  16.8 us
  transfers between devices with their start and end apart: 7, of which 4 were waited for; matrix products, arithmetic and copies ran while one was open for 43% of the time, Pallas kernels for 0%

commit v1 on v0

v1 whole, which is shorter than its diff:
```python
import math

import jax
import jax.numpy as jnp
from jax import lax
from jax.experimental import pallas as pl
from jax.experimental.pallas import tpu as pltpu
from jax.sharding import PartitionSpec as P

HEADS = 12
HEAD_DIM = 128
SPAN = 2
NB = 4
Y, Z = 4, 8
KV_COLS = 512
HEAD_GROUP = 2
LIMIT = 56 * 1024 * 1024


def shifted(value, steps):
    count = Y * Z
    return lax.ppermute(
        value, "patch", [(i, i + steps) for i in range(count) if 0 <= i + steps < count]
    )


def along_z(value, steps):
    return lax.ppermute(
        value, "patch", [(y * Z + z, y * Z + (z + steps) % Z) for y in range(Y) for z in range(Z)]
    )


def along_y(value, steps):
    return lax.ppermute(
        value, "patch", [(y * Z + z, ((y + steps) % Y) * Z + z) for y in range(Y) for z in range(Z)]
    )


def to_next_section(block):
    count = lax.axis_size("section")
    return lax.ppermute(block, "section", [(i, (i + 1) % count) for i in range(count)])


def norm_rows(x_ref, modulation_ref):
    values = x_ref[...].astype(jnp.float32)
    width = values.shape[1]
    average = jnp.sum(values, axis=-1, keepdims=True) * (1.0 / width)
    centered = values - average
    variance = jnp.sum(centered * centered, axis=-1, keepdims=True) * (1.0 / width)
    scaled = centered * lax.rsqrt(variance + 1e-06)
    return (scaled * (1.0 + modulation_ref[1:2]) + modulation_ref[0:1]).astype(jnp.bfloat16)


def head_norm(raw, gains):
    parts = []
    for h in range(raw.shape[1] // HEAD_DIM):
        piece = raw[:, h * HEAD_DIM : (h + 1) * HEAD_DIM]
        square = jnp.sum(piece * piece, axis=-1, keepdims=True) * (1.0 / HEAD_DIM)
        gain = gains[:, h * HEAD_DIM : (h + 1) * HEAD_DIM]
        parts.append((piece * lax.rsqrt(square + 1e-06) * gain).astype(jnp.bfloat16))
    return jnp.concatenate(parts, axis=1) if len(parts) > 1 else parts[0]


def kv_tiles(tiles, modulation, w_kv, gains, start, window):
    count = len(tiles)
    rows, width = tiles[0].shape
    wide = w_kv.shape[1]
    inner = wide // 2
    steps = wide // KV_COLS
    half = steps // 2
    first = window is None

    def body(*refs):
        x_refs = refs[:count]
        modulation_ref, w_ref, gain_ref = refs[count : count + 3]
        rest = refs[count + 3 :]
        if not first:
            rest = rest[1:]
        if first:
            kv_ref, normed_out, normed = rest
        else:
            kv_ref, normed = rest
        step = pl.program_id(0)

        @pl.when(step == 0)
        def _():
            for i in range(count):
                normed[i * rows : (i + 1) * rows, :] = norm_rows(x_refs[i], modulation_ref)
            if first:
                normed_out[...] = normed[...]

        for i in range(count):
            raw = jnp.dot(
                normed[i * rows : (i + 1) * rows, :], w_ref[...], preferred_element_type=jnp.float32
            )

            @pl.when(step < half)
            def _():
                kv_ref[i] = head_norm(raw, gain_ref[...])

            @pl.when(step >= half)
            def _():
                kv_ref[i] = raw.astype(jnp.bfloat16)

    in_specs = [pl.BlockSpec((rows, width), lambda j: (0, 0)) for _ in tiles]
    in_specs += [
        pl.BlockSpec((2, width), lambda j: (0, 0)),
        pl.BlockSpec((width, KV_COLS), lambda j: (0, j)),
        pl.BlockSpec((1, KV_COLS), lambda j: (0, jnp.minimum(j, half - 1))),
    ]
    operands = list(tiles) + [modulation, w_kv, gains]
    aliases = {}
    shapes = [jax.ShapeDtypeStruct((2 * SPAN + 1, rows, wide), jnp.bfloat16)]
    block_at = start // count
    out_specs = [pl.BlockSpec((count, rows, KV_COLS), lambda j: (block_at, 0, j))]
    if first:
        shapes.append(jax.ShapeDtypeStruct((rows, width), jnp.bfloat16))
        out_specs.append(pl.BlockSpec((rows, width), lambda j: (0, 0)))
    else:
        in_specs.append(pl.BlockSpec(memory_space=pl.ANY))
        operands.append(window)
        aliases = {len(operands) - 1: 0}
    return pl.pallas_call(
        body,
        grid=(steps,),
        in_specs=in_specs,
        out_specs=out_specs,
        out_shape=shapes,
        scratch_shapes=[pltpu.VMEM((count * rows, width), jnp.bfloat16)],
        input_output_aliases=aliases,
        compiler_params=pltpu.CompilerParams(vmem_limit_bytes=LIMIT),
        cost_estimate=pl.CostEstimate(
            flops=2 * count * rows * width * wide,
            transcendentals=count * rows,
            bytes_accessed=2 * width * wide + 6 * count * rows * width,
        ),
        name="kv_tiles",
    )(*operands)


def attend(slots, normed, w_blocks, gains, window):
    rows, width = normed.shape
    inner = gains.shape[1]
    cols = HEAD_GROUP * HEAD_DIM
    groups = inner // cols
    part = width // Y
    factor = math.log2(math.e) / math.sqrt(HEAD_DIM)

    def body(slot_ref, normed_ref, *refs):
        w_refs = refs[: len(w_blocks)]
        gain_ref, k_ref, v_ref, out_ref, w_all = refs[len(w_blocks) :]
        own_y = slot_ref[0]
        for w_ref, (shift, low) in zip(w_refs, [b[1:] for b in w_blocks], strict=True):
            at = pl.multiple_of(((own_y + shift) % Y) * part + low, 64)
            w_all[pl.ds(at, w_ref.shape[0]), :] = w_ref[...]
        raw = jnp.dot(normed_ref[...], w_all[...], preferred_element_type=jnp.float32)
        query = head_norm(raw, gain_ref[...])

        def heads(live):
            for h in range(HEAD_GROUP):
                span = slice(h * HEAD_DIM, (h + 1) * HEAD_DIM)
                q = query[:, span]
                scores = []
                for j in range(live):
                    k = k_ref[slot_ref[2 + j], :, span]
                    scores.append(
                        lax.dot_general(
                            q, k, (((1,), (1,)), ((), ())), preferred_element_type=jnp.float32
                        )
                    )
                highest = jnp.max(scores[0], axis=-1, keepdims=True)
                for s in scores[1:]:
                    highest = jnp.maximum(highest, jnp.max(s, axis=-1, keepdims=True))
                total = None
                mixed = None
                for j in range(live):
                    p = jnp.exp2((scores[j] - highest) * factor)
                    line = jnp.sum(p, axis=-1, keepdims=True)
                    v = v_ref[slot_ref[2 + j], :, span]
                    term = jnp.dot(p.astype(jnp.bfloat16), v, preferred_element_type=jnp.float32)
                    total = line if total is None else total + line
                    mixed = term if mixed is None else mixed + term
                out_ref[:, span] = (mixed * (1.0 / total)).astype(jnp.bfloat16)

        for live in range(2, NB + 1):

            @pl.when(slot_ref[1] == live)
            def _(live=live):
                heads(live)

    tiles = window.shape[0]
    in_specs = [pl.BlockSpec((rows, width), lambda g, s: (0, 0))]
    in_specs += [pl.BlockSpec((b[0].shape[0], cols), lambda g, s: (0, g)) for b in w_blocks]
    in_specs += [
        pl.BlockSpec((1, cols), lambda g, s: (0, g)),
        pl.BlockSpec((tiles, rows, cols), lambda g, s: (0, 0, g)),
        pl.BlockSpec((tiles, rows, cols), lambda g, s: (0, 0, groups + g)),
    ]
    return pl.pallas_call(
        body,
        grid_spec=pltpu.PrefetchScalarGridSpec(
            num_scalar_prefetch=1,
            grid=(groups,),
            in_specs=in_specs,
            out_specs=pl.BlockSpec((rows, cols), lambda g, s: (0, g)),
            scratch_shapes=[pltpu.VMEM((width, cols), jnp.bfloat16)],
        ),
        out_shape=jax.ShapeDtypeStruct((rows, inner), jnp.bfloat16),
        compiler_params=pltpu.CompilerParams(vmem_limit_bytes=LIMIT),
        cost_estimate=pl.CostEstimate(
            flops=2 * rows * width * inner + 4 * NB * rows * rows * inner,
            transcendentals=NB * rows * rows * HEADS,
            bytes_accessed=2 * width * inner + 4 * tiles * rows * inner,
        ),
        name="attend",
    )(slots, normed, *[b[0] for b in w_blocks], gains, window, window)


def project(attended, w_out, gate, residual, at, count):
    inner = attended.shape[1]
    width = w_out.shape[1]
    cols = 512

    def body(a_ref, w_ref, gate_ref, x_ref, out_ref):
        branch = jnp.dot(a_ref[...], w_ref[...], preferred_element_type=jnp.float32)
        out_ref[...] = (x_ref[...].astype(jnp.float32) + gate_ref[...] * branch).astype(
            jnp.bfloat16
        )

    block = at // count
    return pl.pallas_call(
        body,
        grid=(width // cols,),
        in_specs=[
            pl.BlockSpec((count, inner), lambda j: (block, 0)),
            pl.BlockSpec((inner, cols), lambda j: (0, j)),
            pl.BlockSpec((1, cols), lambda j: (0, j)),
            pl.BlockSpec((count, cols), lambda j: (block, j)),
        ],
        out_specs=pl.BlockSpec((count, cols), lambda j: (0, j)),
        out_shape=jax.ShapeDtypeStruct((count, width), jnp.bfloat16),
        compiler_params=pltpu.CompilerParams(vmem_limit_bytes=LIMIT),
        cost_estimate=pl.CostEstimate(
            flops=2 * count * inner * width,
            transcendentals=0,
            bytes_accessed=2 * inner * width + 6 * count * width,
        ),
        name="project",
    )(attended, w_out, gate, residual)


def gather_z(shard, z):
    rows, width = shard.shape
    block = jnp.zeros((Z, rows, width), shard.dtype)

    def put(block, piece, k):
        return lax.dynamic_update_slice(block, piece[None], ((z + k) % Z, 0, 0))

    block = put(block, shard, 0)
    up = down = shard
    for k in range(1, Z // 2 + 1):
        up = along_z(up, 1)
        block = put(block, up, Z - k)
        if k < Z - Z // 2:
            down = along_z(down, -1)
            block = put(block, down, k)
    return block.reshape(Z * rows, width)


def on_device(arriving, modulation, gate, w_query, w_kv, w_out, qk_gain, neighbors, live):
    x = arriving[0, 0]
    rows = x.shape[0]
    position = lax.axis_index("patch")
    y, z = position // Z, position % Z

    out_full = lax.all_gather(w_out[0], "patch", axis=0, tiled=True)
    up1, down1 = shifted(x, 1), shifted(x, -1)
    query_block = gather_z(w_query[0], z)
    half = query_block.shape[0] // 2
    w_blocks = [
        (query_block, 0, 0),
        (along_y(query_block, 1), Y - 1, 0),
        (along_y(query_block, -1), 1, 0),
        (along_y(query_block[:half], 2), Y - 2, 0),
        (along_y(query_block[half:], -2), 2, half),
    ]
    up2, down2 = shifted(up1, 1), shifted(down1, -1)

    window, normed = kv_tiles([x], modulation[0], w_kv[0], qk_gain[0, 1:2], 2 * SPAN, None)
    (window,) = kv_tiles([up1, down1], modulation[0], w_kv[0], qk_gain[0, 1:2], 0, window)
    (window,) = kv_tiles([up2, down2], modulation[0], w_kv[0], qk_gain[0, 1:2], 2, window)

    away = neighbors[0] - position
    place = jnp.where(away < 0, -2 * away - 2, 2 * away - 1)
    place = jnp.where(away == 0, 2 * SPAN, jnp.clip(place, 0, 2 * SPAN))
    slots = jnp.concatenate([y[None], live, place]).astype(jnp.int32)
    attended = attend(slots, normed, w_blocks, qk_gain[0, 0:1], window)
    count = rows // 2
    parts = [
        to_next_section(project(attended, out_full, gate, x, at, count)) for at in (0, count)
    ]
    return jnp.concatenate(parts, axis=0)[None, None]


def solution(mesh):
    placed = (
        P("section", "patch", None, None),
        P("section", None, None),
        P("section", None),
        P("section", "patch", None),
        P("section", None, None),
        P("section", "patch", None),
        P("section", None, None),
        P("patch", None),
        P("patch"),
    )
    return jax.shard_map(
        on_device,
        mesh=mesh,
        in_specs=placed,
        out_specs=P("section", "patch", None, None),
        check_vma=False,
    )
```

time: 437 us -> 217 us (0.50)
  the two profiles are of different devices: /device:TPU:24 before, /device:TPU:16 now
where the time goes in v1:
time: 217 us; the launch traced here: 216 us
  waiting for transfers between devices  86.6 us (40%)
  Pallas kernels  73.5 us (34%)
  starting transfers between devices  32.5 us (15%)
  between operations  14.4 us (7%)
  local copies, waits for them, and re-layouts  7.21 us (3%)
    pallas_call x3, Pallas kernels, kv_tiles(): pl.pallas_call(body, grid=(steps,), in_specs=in_specs, out_specs=out_spec...  43.5 us
    ppermute x4, waiting for transfers between devices, along_y(): lax.ppermute(value, 'patch', [(y * Z + z, (y + steps) % Y * Z + z) for y...  41.1 us
    ppermute x7, waiting for transfers between devices, along_z(): lax.ppermute(value, 'patch', [(y * Z + z, y * Z + (z + steps) % Z) for y...  21.9 us
    pallas_call x1, Pallas kernels, attend(): pl.pallas_call(body, grid_spec=pltpu.PrefetchScalarGridSpec(num_scalar_pr...  20.2 us
    ppermute x4, starting transfers between devices, shifted(): lax.ppermute(value, 'patch', [(i, i + steps) for i in range(count) if 0 <...  15.9 us
    ppermute x2, waiting for transfers between devices, to_next_section(): lax.ppermute(block, 'section', [(i, (i + 1) % count) for i in range(count)])  15.2 us
    ppermute x7, starting transfers between devices, along_z(): lax.ppermute(value, 'patch', [(y * Z + z, y * Z + (z + steps) % Z) for y...  12.8 us
    pallas_call x2, Pallas kernels, project(): pl.pallas_call(body, grid=(width // cols,), in_specs=[pl.BlockSpec((count...  9.83 us
  transfers between devices with their start and end apart: 18, of which 11 were waited for; matrix products, arithmetic and copies ran while one was open for 2% of the time, Pallas kernels for 29%

profile of v1, /device:TPU:16, one launch (start us, length us, event | category | flops | bytes accessed | tf_op | source)
XLA Modules:
  0.0 215.9 jit_solution(5775334341149745730)
XLA Ops:
  6.5 0.7 all-gather.3.cloned.1.call-update
  7.3 2.0 collective-permute-start
  9.3 4.0 %collective-permute-start.1 = (bf16[48,1536]{1,0:T(8,128)(2,1)}, bf16[48,1536]{1,0:T(8,128)(2,1)}, u32[]{:S(2)}, u32[]{:S(2)}) collective-permute-start(bf16[48,1536]{1,0:T(8,128)(2,1)} %bitcast.46), channel_id=1, source_target_pairs={{0,7},{1,0},{2,1},{3,2},{4,3},{5,4},{6,5},{7,6},{8,15},{9,8},{10,9... | collective-permute-start | bytes 442376 | tf_op jit(solution)/shard_map/ppermute | solution.py:28
  13.3 1.9 collective-permute-start.11
  15.2 6.0 %collective-permute-start.13 = (bf16[384,1536]{1,0:T(8,128)(2,1)}, bf16[384,1536]{1,0:T(8,128)(2,1)S(1)}, u32[]{:S(2)}, u32[]{:S(2)}) collective-permute-start(bf16[384,1536]{1,0:T(8,128)(2,1)} %bitcast.40), channel_id=1, source_target_pairs={{1,0},{2,1},{3,2},{4,3},{5,4},{6,5},{7,6},{8,7},{9,8},{10,9},{11,1... | collective-permute-start | bytes 3538952 | tf_op jit(solution)/shard_map/ppermute | solution.py:22
  21.3 0.1 broadcast_in_dim.36
  21.4 0.8 copy-done.9
  22.2 0.6 slice_bitcast_fusion
  22.8 11.0 %kv_tiles.3 = (bf16[5,384,3072]{2,1,0:T(8,128)(2,1)}, bf16[384,1536]{1,0:T(8,128)(2,1)}) custom-call(bf16[384,1536]{1,0:T(8,128)(2,1)} %bitcast.41, f32[2,1536]{1,0:T(2,128)} %bitcast.47, bf16[1536,3072]{1,0:T(8,128)(2,1)} %bitcast.31, f32[1,1536]{1,0:T(1,128)} %get-tuple-element.12.refs_3_.refs_4_), custom_call_target="tpu_custom_call" | custom-call | flops 3623878656 | bytes 12976128 | tf_op jit(solution)/shard_map/kv_tiles/pallas_call | solution.py:123
  34.6 0.7 pad_add_fusion.slot_ref
  35.3 0.0 collective-permute-start.2
  35.3 0.0 collective-permute-done.1
  35.3 3.2 %collective-permute-start.3 = (bf16[48,1536]{1,0:T(8,128)(2,1)}, bf16[48,1536]{1,0:T(8,128)(2,1)S(1)}, u32[]{:S(2)}, u32[]{:S(2)}) collective-permute-start(bf16[48,1536]{1,0:T(8,128)(2,1)} %collective-permute-done.1), channel_id=1, source_target_pairs={{0,7},{1,0},{2,1},{3,2},{4,3},{5,4},{6,5},{7,6},{8,15},{9,8},{10,9... | collective-permute-start | bytes 442376 | tf_op jit(solution)/shard_map/ppermute | solution.py:28
  38.5 0.9 bitcast_dynamic-update-slice_fusion.6
  39.4 0.9 bitcast_dynamic-update-slice_fusion.5
  40.4 12.9 %collective-permute-done.2 = bf16[48,1536]{1,0:T(8,128)(2,1)S(1)} collective-permute-done((bf16[48,1536]{1,0:T(8,128)(2,1)}, bf16[48,1536]{1,0:T(8,128)(2,1)S(1)}, u32[]{:S(2)}, u32[]{:S(2)}) %collective-permute-start.2) | collective-permute-done | bytes 147488 | tf_op jit(solution)/shard_map/ppermute | solution.py:28
  53.3 1.6 collective-permute-done.3
  54.9 3.6 %collective-permute-start.5 = (bf16[48,1536]{1,0:T(8,128)(2,1)S(1)}, bf16[48,1536]{1,0:T(8,128)(2,1)S(1)}, u32[]{:S(2)}, u32[]{:S(2)}) collective-permute-start(bf16[48,1536]{1,0:T(8,128)(2,1)S(1)} %collective-permute-done.3), channel_id=1, source_target_pairs={{0,7},{1,0},{2,1},{3,2},{4,3},{5,4},{6,5},{7,6},{8,15},{9,8},{10,9... | collective-permute-start | bytes 442376 | tf_op jit(solution)/shard_map/ppermute | solution.py:28
  58.5 1.1 collective-permute-done.4
  59.6 0.0 collective-permute-start.6
  59.6 1.5 collective-permute-done.5
  61.2 4.8 %collective-permute-done.6 = bf16[48,1536]{1,0:T(8,128)(2,1)S(1)} collective-permute-done((bf16[48,1536]{1,0:T(8,128)(2,1)S(1)}, bf16[48,1536]{1,0:T(8,128)(2,1)S(1)}, u32[]{:S(2)}, u32[]{:S(2)}) %collective-permute-start.6) | collective-permute-done | bytes 147488 | tf_op jit(solution)/shard_map/ppermute | solution.py:28
  66.0 0.4 collective-permute-start.7
  66.4 1.7 collective-permute-start.8
  68.1 1.9 collective-permute-start.12
  70.0 0.0 collective-permute-done.13.refs_1_
  70.0 6.0 %collective-permute-start.14 = (bf16[384,1536]{1,0:T(8,128)(2,1)S(1)}, bf16[384,1536]{1,0:T(8,128)(2,1)S(1)}, u32[]{:S(2)}, u32[]{:S(2)}) collective-permute-start(bf16[384,1536]{1,0:T(8,128)(2,1)S(1)} %collective-permute-done.13.refs_1_), channel_id=1, source_target_pairs={{1,0},{2,1},{3,2},{4,3},{5,4},{6,5},{7,6},{8,7},{9,8},{10,9},{11,1... | collective-permute-start | bytes 3538952 | tf_op jit(solution)/shard_map/ppermute | solution.py:22
  76.1 1.1 fusion.2
  77.2 0.0 collective-permute-start.10
  77.2 16.3 %kv_tiles.4.refs_5_ = bf16[5,384,3072]{2,1,0:T(8,128)(2,1)} custom-call(bf16[384,1536]{1,0:T(8,128)(2,1)} %copy-done.2, bf16[384,1536]{1,0:T(8,128)(2,1)} %copy-done.1, f32[2,1536]{1,0:T(2,128)} %bitcast.48, bf16[1536,3072]{1,0:T(8,128)(2,1)} %bitcast.32, f32[1,1536]{1,0:T(1,128)} %get-tuple-element.12.refs_3_.refs_4_, ...), custom_call_target="tpu_custom_call", output_to_operand_aliasing={{}: (5, {})} | custom-call | flops 7247757312 | bytes 16515072 | tf_op jit(solution)/shard_map/kv_tiles/pallas_call | solution.py:123
  93.5 6.2 %collective-permute-done.12.refs_0_ = bf16[384,1536]{1,0:T(8,128)(2,1)S(1)} collective-permute-done((bf16[384,1536]{1,0:T(8,128)(2,1)S(1)}, bf16[384,1536]{1,0:T(8,128)(2,1)S(1)}, u32[]{:S(2)}, u32[]{:S(2)}) %collective-permute-start.12) | collective-permute-done | bytes 1179680 | tf_op jit(solution)/shard_map/ppermute | solution.py:22
  99.7 0.0 collective-permute-start.9
  99.7 1.4 collective-permute-done.14.refs_1_
  101.1 1.1 copy-done.6
  102.2 16.3 %kv_tiles.5.refs_6_.refs_7_ = bf16[5,384,3072]{2,1,0:T(8,128)(2,1)} custom-call(bf16[384,1536]{1,0:T(8,128)(2,1)} %copy-done.5, bf16[384,1536]{1,0:T(8,128)(2,1)} %copy-done.6, f32[2,1536]{1,0:T(2,128)} %bitcast.49, bf16[1536,3072]{1,0:T(8,128)(2,1)} %bitcast.33, f32[1,1536]{1,0:T(1,128)} %get-tuple-element.12.refs_3_.refs_4_, ...), custom_call_target="tpu_custom_call", output_to_operand_aliasing={{}: (5, {})} | custom-call | flops 7247757312 | bytes 16515072 | tf_op jit(solution)/shard_map/kv_tiles/pallas_call | solution.py:123
  118.4 31.0 %collective-permute-done.10.refs_4_ = bf16[192,1536]{1,0:T(8,128)(2,1)} collective-permute-done((bf16[192,1536]{1,0:T(8,128)(2,1)}, bf16[192,1536]{1,0:T(8,128)(2,1)}, u32[]{:S(2)}, u32[]{:S(2)}) %collective-permute-start.10) | collective-permute-done | bytes 589856 | tf_op jit(solution)/shard_map/ppermute | solution.py:34
  149.5 10.1 %collective-permute-done.9.refs_3_ = bf16[192,1536]{1,0:T(8,128)(2,1)S(1)} collective-permute-done((bf16[192,1536]{1,0:T(8,128)(2,1)}, bf16[192,1536]{1,0:T(8,128)(2,1)S(1)}, u32[]{:S(2)}, u32[]{:S(2)}) %collective-permute-start.9) | collective-permute-done | bytes 589856 | tf_op jit(solution)/shard_map/ppermute | solution.py:34
  159.6 0.0 collective-permute-done.7.refs_1_
  159.6 0.8 copy-done.8
  160.4 0.5 copy-done.3
  160.8 0.3 copy-done.4
  161.2 20.2 %attend.1.a_ref = bf16[384,1536]{1,0:T(8,128)(2,1)} custom-call(s32[6]{0:T(128)} %pad_add_fusion.slot_ref, bf16[384,1536]{1,0:T(8,128)(2,1)} %get-tuple-element.7.normed_ref, bf16[384,1536]{1,0:T(8,128)(2,1)} %bitcast.38, bf16[384,1536]{1,0:T(8,128)(2,1)} %copy-done.3, bf16[384,1536]{1,0:T(8,128)(2,1)} %copy-done.4, bf16[192,1536]{1,0:T(8,128)(2,1)} %copy-done.8, ...), custom_call_target="tpu_custom_call" | custom-call | flops 5435817984 | bytes 16515072 | tf_op jit(solution)/shard_map/attend/pallas_call | solution.py:199
  181.3 4.9 %project.2 = bf16[192,1536]{1,0:T(8,128)(2,1)} custom-call(bf16[384,1536]{1,0:T(8,128)(2,1)} %attend.1.a_ref, bf16[1536,1536]{1,0:T(8,128)(2,1)} %bitcast.34, f32[1,1536]{1,0:T(1,128)} %gate_ref.3, bf16[384,1536]{1,0:T(8,128)(2,1)} %bitcast.42), custom_call_target="tpu_custom_call" | custom-call | flops 905969664 | bytes 6488064 | tf_op jit(solution)/shard_map/project/pallas_call | solution.py:231
  186.2 4.9 %project.3 = bf16[192,1536]{1,0:T(8,128)(2,1)} custom-call(bf16[384,1536]{1,0:T(8,128)(2,1)} %attend.1.a_ref, bf16[1536,1536]{1,0:T(8,128)(2,1)} %bitcast.35, f32[1,1536]{1,0:T(1,128)} %gate_ref.3, bf16[384,1536]{1,0:T(8,128)(2,1)} %bitcast.43), custom_call_target="tpu_custom_call" | custom-call | flops 905969664 | bytes 6488064 | tf_op jit(solution)/shard_map/project/pallas_call | solution.py:231
  191.2 1.6 collective-permute-start.16
  192.8 8.9 %collective-permute-done.15 = bf16[192,1536]{1,0:T(8,128)(2,1)S(1)} collective-permute-done((bf16[192,1536]{1,0:T(8,128)(2,1)S(1)}, bf16[192,1536]{1,0:T(8,128)(2,1)S(1)}, u32[]{:S(2)}, u32[]{:S(2)}) %collective-permute-start.15) | collective-permute-done | bytes 589856 | tf_op jit(solution)/shard_map/ppermute | solution.py:41
  201.7 6.3 %collective-permute-done.16 = bf16[192,1536]{1,0:T(8,128)(2,1)S(1)} collective-permute-done((bf16[192,1536]{1,0:T(8,128)(2,1)}, bf16[192,1536]{1,0:T(8,128)(2,1)S(1)}, u32[]{:S(2)}, u32[]{:S(2)}) %collective-permute-start.16) | collective-permute-done | bytes 589856 | tf_op jit(solution)/shard_map/ppermute | solution.py:41
  208.0 1.1 maximum_bitcast_fusion
  (33 shorter events, 0.1 us)
Async XLA Ops:
  6.5 15.7 %copy-start.10 = (f32[1,2,1536]{2,1,0:T(2,128)S(1)}, f32[1,2,1536]{2,1,0:T(2,128)}, u32[]{:S(2)}) copy-start(f32[1,2,1536]{2,1,0:T(2,128)} %param.15) | copy-start | bytes 36868
  6.5 174.8 %all-gather.3.cloned.1.call-start = ((), (), s32[]{:S(2)}) async-start(), calls=%async_computation | async-start | bytes 4866048 | tf_op jit(solution)/shard_map/all_gather | solution.py:276
  7.3 28.0 %collective-permute-start = (bf16[48,1536]{1,0:T(8,128)(2,1)}, bf16[48,1536]{1,0:T(8,128)(2,1)}, u32[]{:S(2)}, u32[]{:S(2)}) collective-permute-start(bf16[48,1536]{1,0:T(8,128)(2,1)} %bitcast.45), channel_id=1, source_target_pairs={{0,1},{1,2},{2,3},{3,4},{4,5},{5,6},{6,7},{7,0},{8,9},{9,10},{10,1... | collective-permute-start | bytes 442376 | tf_op jit(solution)/shard_map/ppermute | solution.py:28
  9.3 26.0 %collective-permute-start.1 = (bf16[48,1536]{1,0:T(8,128)(2,1)}, bf16[48,1536]{1,0:T(8,128)(2,1)}, u32[]{:S(2)}, u32[]{:S(2)}) collective-permute-start(bf16[48,1536]{1,0:T(8,128)(2,1)} %bitcast.46), channel_id=1, source_target_pairs={{0,7},{1,0},{2,1},{3,2},{4,3},{5,4},{6,5},{7,6},{8,15},{9,8},{10,9... | collective-permute-start | bytes 442376 | tf_op jit(solution)/shard_map/ppermute | solution.py:28
  13.3 54.8 %collective-permute-start.11 = (bf16[384,1536]{1,0:T(8,128)(2,1)}, bf16[384,1536]{1,0:T(8,128)(2,1)S(1)}, u32[]{:S(2)}, u32[]{:S(2)}) collective-permute-start(bf16[384,1536]{1,0:T(8,128)(2,1)} %bitcast.39), channel_id=1, source_target_pairs={{0,1},{1,2},{2,3},{3,4},{4,5},{5,6},{6,7},{7,8},{8,9},{9,10},{10,1... | collective-permute-start | bytes 3538952 | tf_op jit(solution)/shard_map/ppermute | solution.py:22
  15.2 54.8 %collective-permute-start.13 = (bf16[384,1536]{1,0:T(8,128)(2,1)}, bf16[384,1536]{1,0:T(8,128)(2,1)S(1)}, u32[]{:S(2)}, u32[]{:S(2)}) collective-permute-start(bf16[384,1536]{1,0:T(8,128)(2,1)} %bitcast.40), channel_id=1, source_target_pairs={{1,0},{2,1},{3,2},{4,3},{5,4},{6,5},{7,6},{8,7},{9,8},{10,9},{11,1... | collective-permute-start | bytes 3538952 | tf_op jit(solution)/shard_map/ppermute | solution.py:22
  21.3 0.9 copy-start.9
  22.8 11.0 %copy-start.11 = (s32[1,4]{1,0:T(1,128)S(1)}, s32[1,4]{1,0:T(1,128)}, u32[]{:S(2)}) copy-start(s32[1,4]{1,0:T(1,128)} %param.16) | copy-start | bytes 52
  35.3 18.0 %collective-permute-start.2 = (bf16[48,1536]{1,0:T(8,128)(2,1)}, bf16[48,1536]{1,0:T(8,128)(2,1)S(1)}, u32[]{:S(2)}, u32[]{:S(2)}) collective-permute-start(bf16[48,1536]{1,0:T(8,128)(2,1)} %collective-permute-done), channel_id=1, source_target_pairs={{0,1},{1,2},{2,3},{3,4},{4,5},{5,6},{6,7},{7,0},{8,9},{9,10},{10,1... | collective-permute-start | bytes 442376 | tf_op jit(solution)/shard_map/ppermute | solution.py:28
  35.3 19.6 %collective-permute-start.3 = (bf16[48,1536]{1,0:T(8,128)(2,1)}, bf16[48,1536]{1,0:T(8,128)(2,1)S(1)}, u32[]{:S(2)}, u32[]{:S(2)}) collective-permute-start(bf16[48,1536]{1,0:T(8,128)(2,1)} %collective-permute-done.1), channel_id=1, source_target_pairs={{0,7},{1,0},{2,1},{3,2},{4,3},{5,4},{6,5},{7,6},{8,15},{9,8},{10,9... | collective-permute-start | bytes 442376 | tf_op jit(solution)/shard_map/ppermute | solution.py:28
  53.3 6.4 %collective-permute-start.4 = (bf16[48,1536]{1,0:T(8,128)(2,1)S(1)}, bf16[48,1536]{1,0:T(8,128)(2,1)S(1)}, u32[]{:S(2)}, u32[]{:S(2)}) collective-permute-start(bf16[48,1536]{1,0:T(8,128)(2,1)S(1)} %collective-permute-done.2), channel_id=1, source_target_pairs={{0,1},{1,2},{2,3},{3,4},{4,5},{5,6},{6,7},{7,0},{8,9},{9,10},{10,1... | collective-permute-start | bytes 442376 | tf_op jit(solution)/shard_map/ppermute | solution.py:28
  54.9 6.3 %collective-permute-start.5 = (bf16[48,1536]{1,0:T(8,128)(2,1)S(1)}, bf16[48,1536]{1,0:T(8,128)(2,1)S(1)}, u32[]{:S(2)}, u32[]{:S(2)}) collective-permute-start(bf16[48,1536]{1,0:T(8,128)(2,1)S(1)} %collective-permute-done.3), channel_id=1, source_target_pairs={{0,7},{1,0},{2,1},{3,2},{4,3},{5,4},{6,5},{7,6},{8,15},{9,8},{10,9... | collective-permute-start | bytes 442376 | tf_op jit(solution)/shard_map/ppermute | solution.py:28
  59.6 6.4 %collective-permute-start.6 = (bf16[48,1536]{1,0:T(8,128)(2,1)S(1)}, bf16[48,1536]{1,0:T(8,128)(2,1)S(1)}, u32[]{:S(2)}, u32[]{:S(2)}) collective-permute-start(bf16[48,1536]{1,0:T(8,128)(2,1)S(1)} %collective-permute-done.4), channel_id=1, source_target_pairs={{0,1},{1,2},{2,3},{3,4},{4,5},{5,6},{6,7},{7,0},{8,9},{9,10},{10,1... | collective-permute-start | bytes 442376 | tf_op jit(solution)/shard_map/ppermute | solution.py:28
  66.0 11.2 %copy-start = (bf16[8,48,1536]{2,1,0:T(8,128)(2,1)}, bf16[8,48,1536]{2,1,0:T(8,128)(2,1)S(1)}, u32[]{:S(2)}) copy-start(bf16[8,48,1536]{2,1,0:T(8,128)(2,1)S(1)} %bitcast_dynamic-update-slice_fusion) | copy-start | bytes 3538948
  66.0 93.6 %collective-permute-start.7 = (bf16[384,1536]{1,0:T(8,128)(2,1)S(1)}, bf16[384,1536]{1,0:T(8,128)(2,1)S(1)}, u32[]{:S(2)}, u32[]{:S(2)}) collective-permute-start(bf16[384,1536]{1,0:T(8,128)(2,1)S(1)} %bitcast.36), channel_id=1, source_target_pairs={{0,8},{1,9},{2,10},{3,11},{4,12},{5,13},{6,14},{7,15},{8,16},{9,17... | collective-permute-start | bytes 3538952 | tf_op jit(solution)/shard_map/ppermute | solution.py:34
  66.4 93.2 %collective-permute-start.8 = (bf16[384,1536]{1,0:T(8,128)(2,1)S(1)}, bf16[384,1536]{1,0:T(8,128)(2,1)S(1)}, u32[]{:S(2)}, u32[]{:S(2)}) collective-permute-start(bf16[384,1536]{1,0:T(8,128)(2,1)S(1)} %bitcast.37), channel_id=1, source_target_pairs={{0,24},{1,25},{2,26},{3,27},{4,28},{5,29},{6,30},{7,31},{8,0},{9,1... | collective-permute-start | bytes 3538952 | tf_op jit(solution)/shard_map/ppermute | solution.py:34
  68.1 9.1 %copy-start.2 = (bf16[384,1536]{1,0:T(8,128)(2,1)}, bf16[384,1536]{1,0:T(8,128)(2,1)S(1)}, u32[]{:S(2)}) copy-start(bf16[384,1536]{1,0:T(8,128)(2,1)S(1)} %collective-permute-done.11.refs_0_) | copy-start | bytes 3538948
  68.1 31.6 %collective-permute-start.12 = (bf16[384,1536]{1,0:T(8,128)(2,1)S(1)}, bf16[384,1536]{1,0:T(8,128)(2,1)S(1)}, u32[]{:S(2)}, u32[]{:S(2)}) collective-permute-start(bf16[384,1536]{1,0:T(8,128)(2,1)S(1)} %collective-permute-done.11.refs_0_), channel_id=1, source_target_pairs={{0,1},{1,2},{2,3},{3,4},{4,5},{5,6},{6,7},{7,8},{8,9},{9,10},{10,1... | collective-permute-start | bytes 3538952 | tf_op jit(solution)/shard_map/ppermute | solution.py:22
  70.0 7.2 %copy-start.1 = (bf16[384,1536]{1,0:T(8,128)(2,1)}, bf16[384,1536]{1,0:T(8,128)(2,1)S(1)}, u32[]{:S(2)}) copy-start(bf16[384,1536]{1,0:T(8,128)(2,1)S(1)} %collective-permute-done.13.refs_1_) | copy-start | bytes 3538948
  70.0 31.1 %collective-permute-start.14 = (bf16[384,1536]{1,0:T(8,128)(2,1)S(1)}, bf16[384,1536]{1,0:T(8,128)(2,1)S(1)}, u32[]{:S(2)}, u32[]{:S(2)}) collective-permute-start(bf16[384,1536]{1,0:T(8,128)(2,1)S(1)} %collective-permute-done.13.refs_1_), channel_id=1, source_target_pairs={{1,0},{2,1},{3,2},{4,3},{5,4},{6,5},{7,6},{8,7},{9,8},{10,9},{11,1... | collective-permute-start | bytes 3538952 | tf_op jit(solution)/shard_map/ppermute | solution.py:22
  77.2 72.3 %collective-permute-start.10 = (bf16[192,1536]{1,0:T(8,128)(2,1)}, bf16[192,1536]{1,0:T(8,128)(2,1)}, u32[]{:S(2)}, u32[]{:S(2)}) collective-permute-start(bf16[192,1536]{1,0:T(8,128)(2,1)} %bitcast.16), channel_id=1, source_target_pairs={{0,16},{1,17},{2,18},{3,19},{4,20},{5,21},{6,22},{7,23},{8,24},{9,... | collective-permute-start | bytes 1769480 | tf_op jit(solution)/shard_map/ppermute | solution.py:34
  99.7 1.4 copy-start.5
  99.7 59.8 %collective-permute-start.9 = (bf16[192,1536]{1,0:T(8,128)(2,1)}, bf16[192,1536]{1,0:T(8,128)(2,1)S(1)}, u32[]{:S(2)}, u32[]{:S(2)}) collective-permute-start(bf16[192,1536]{1,0:T(8,128)(2,1)} %bitcast.44), channel_id=1, source_target_pairs={{0,16},{1,17},{2,18},{3,19},{4,20},{5,21},{6,22},{7,23},{8,24},{9,... | collective-permute-start | bytes 1769480 | tf_op jit(solution)/shard_map/ppermute | solution.py:34
  101.1 1.1 copy-start.6
  159.6 0.8 copy-start.8
  159.6 1.3 copy-start.3
  159.6 1.6 copy-start.4
  186.2 4.9 %copy-start.7 = (bf16[192,1536]{1,0:T(8,128)(2,1)S(1)}, bf16[192,1536]{1,0:T(8,128)(2,1)}, u32[]{:S(2)}) copy-start(bf16[192,1536]{1,0:T(8,128)(2,1)} %project.2) | copy-start | bytes 1769476
  191.2 10.5 %collective-permute-start.15 = (bf16[192,1536]{1,0:T(8,128)(2,1)S(1)}, bf16[192,1536]{1,0:T(8,128)(2,1)S(1)}, u32[]{:S(2)}, u32[]{:S(2)}) collective-permute-start(bf16[192,1536]{1,0:T(8,128)(2,1)S(1)} %copy-done.7), channel_id=1, source_target_pairs={{0,32},{32,64},{64,96},{96,128},{128,160},{160,192},{192,224},{224... | collective-permute-start | bytes 1769480 | tf_op jit(solution)/shard_map/ppermute | solution.py:41
  191.2 16.8 %collective-permute-start.16 = (bf16[192,1536]{1,0:T(8,128)(2,1)}, bf16[192,1536]{1,0:T(8,128)(2,1)S(1)}, u32[]{:S(2)}, u32[]{:S(2)}) collective-permute-start(bf16[192,1536]{1,0:T(8,128)(2,1)} %project.3), channel_id=1, source_target_pairs={{0,32},{32,64},{64,96},{96,128},{128,160},{160,192},{192,224},{224... | collective-permute-start | bytes 1769480 | tf_op jit(solution)/shard_map/ppermute | solution.py:41
Sparse Core Ops, SparseCore 0:
  9.9 131.5 all-gather.2

commit v2 on v0

v2 whole, which is shorter than its diff:
```python
import math

import jax
import jax.numpy as jnp
from jax import lax
from jax.experimental import pallas as pl
from jax.experimental.pallas import tpu as pltpu
from jax.sharding import PartitionSpec as P

HEADS = 12
HEAD_DIM = 128
SPAN = 2
NB = 4
Y, Z = 4, 8
COLS = 512
SMALL = 12 * 1024 * 1024
LARGE = 20 * 1024 * 1024
VMEM = pl.BlockSpec(memory_space=pltpu.VMEM)
SMEM = pl.BlockSpec(memory_space=pltpu.SMEM)
AT_Y, AT_Z, AT_LIVE, AT_SLOT, AT_NEED = 0, 1, 2, 3, 7


def shifted(value, steps):
    count = Y * Z
    return lax.ppermute(
        value, "patch", [(i, i + steps) for i in range(count) if 0 <= i + steps < count]
    )


def along_z(value, steps):
    return lax.ppermute(
        value, "patch", [(y * Z + z, y * Z + (z + steps) % Z) for y in range(Y) for z in range(Z)]
    )


def along_y(value, steps):
    return lax.ppermute(
        value, "patch", [(y * Z + z, ((y + steps) % Y) * Z + z) for y in range(Y) for z in range(Z)]
    )


def to_next_section(block):
    count = lax.axis_size("section")
    return lax.ppermute(block, "section", [(i, (i + 1) % count) for i in range(count)])


def norm_rows(x, modulation):
    values = x.astype(jnp.float32)
    width = values.shape[1]
    average = jnp.sum(values, axis=-1, keepdims=True) * (1.0 / width)
    centered = values - average
    variance = jnp.sum(centered * centered, axis=-1, keepdims=True) * (1.0 / width)
    scaled = centered * lax.rsqrt(variance + 1e-06)
    return (scaled * (1.0 + modulation[1:2]) + modulation[0:1]).astype(jnp.bfloat16)


def head_norm(raw, gains):
    parts = []
    for h in range(raw.shape[1] // HEAD_DIM):
        piece = raw[:, h * HEAD_DIM : (h + 1) * HEAD_DIM]
        square = jnp.sum(piece * piece, axis=-1, keepdims=True) * (1.0 / HEAD_DIM)
        gain = gains[:, h * HEAD_DIM : (h + 1) * HEAD_DIM]
        parts.append((piece * lax.rsqrt(square + 1e-06) * gain).astype(jnp.bfloat16))
    return jnp.concatenate(parts, axis=1) if len(parts) > 1 else parts[0]


def kernel(body, name, specs, shapes, scratch, aliases, flops, limit, operands):
    moved = sum(o.size * o.dtype.itemsize for o in operands)
    return pl.pallas_call(
        body,
        in_specs=specs,
        out_specs=[VMEM for _ in shapes],
        out_shape=shapes,
        scratch_shapes=scratch,
        input_output_aliases=aliases,
        compiler_params=pltpu.CompilerParams(vmem_limit_bytes=limit),
        cost_estimate=pl.CostEstimate(flops=flops, transcendentals=0, bytes_accessed=moved),
        name=name,
    )(*operands)


def project_kv(normed, w_ref, gain_ref, window_ref, tile):
    half = w_ref.shape[1] // 2

    @pl.loop(0, half // COLS)
    def _(j):
        cols = pl.ds(pl.multiple_of(j * COLS, COLS), COLS)
        raw = jnp.dot(normed[...], w_ref[:, cols], preferred_element_type=jnp.float32)
        window_ref[tile, :, cols] = head_norm(raw, gain_ref[:, cols])
        cols = pl.ds(pl.multiple_of(half + j * COLS, COLS), COLS)
        raw = jnp.dot(normed[...], w_ref[:, cols], preferred_element_type=jnp.float32)
        window_ref[tile, :, cols] = raw.astype(jnp.bfloat16)


def own_tile(x, modulation, w_kv, gains):
    rows, width = x.shape
    wide = w_kv.shape[1]

    def body(x_ref, modulation_ref, w_ref, gain_ref, window_ref, normed_ref):
        normed_ref[...] = norm_rows(x_ref[...], modulation_ref)
        project_kv(normed_ref, w_ref, gain_ref, window_ref, 2 * SPAN)

    shapes = [
        jax.ShapeDtypeStruct((2 * SPAN + 1, rows, wide), jnp.bfloat16),
        jax.ShapeDtypeStruct((rows, width), jnp.bfloat16),
    ]
    flops = 2 * rows * width * wide
    operands = [x, modulation, w_kv, gains]
    return kernel(body, "own_tile", [VMEM] * 4, shapes, [], {}, flops, SMALL, operands)


def near_tiles(scalars, tiles, modulation, w_kv, gains, window, start):
    count = len(tiles)
    rows, width = tiles[0].shape
    wide = w_kv.shape[1]

    def body(*refs):
        scalar_ref, x_refs = refs[0], refs[1 : 1 + count]
        modulation_ref, w_ref, gain_ref, _, window_ref, normed = refs[1 + count :]
        for i in range(count):

            @pl.when(scalar_ref[AT_NEED + start + i] > 0)
            def _(i=i):
                normed[i] = norm_rows(x_refs[i][...], modulation_ref)

        @pl.loop(0, count)
        def _(i):
            @pl.when(scalar_ref[AT_NEED + start + i] > 0)
            def _():
                project_kv(normed.at[i], w_ref, gain_ref, window_ref, start + i)

    shapes = [jax.ShapeDtypeStruct(window.shape, window.dtype)]
    specs = [SMEM] + [VMEM] * (count + 4)
    scratch = [pltpu.VMEM((count, rows, width), jnp.bfloat16)]
    operands = [scalars, *tiles, modulation, w_kv, gains, window]
    flops = 2 * count * rows * width * wide
    return kernel(
        body, "near_tiles", specs, shapes, scratch, {len(operands) - 1: 0}, flops, SMALL, operands
    )[0]


def place_rows(scalar_ref, sources, plan, low, size, target):
    for ref, (dy, zs, at) in zip(sources, plan, strict=True):
        at_y = (scalar_ref[AT_Y] + dy) % Y
        for k, dz in enumerate(zs):
            shard = at_y * Z + (scalar_ref[AT_Z] + dz) % Z
            row = pl.multiple_of(shard * size, 16)
            begin = at + k * 2 * size + low
            target[pl.ds(row, size), :] = ref[begin : begin + size, :]


def join(parts):
    count = parts[0].shape[0]

    def body(*refs):
        for k, ref in enumerate(refs[:-1]):
            refs[-1][k * count : (k + 1) * count, :] = ref[...]

    shape = (len(parts) * count, parts[0].shape[1])
    shapes = [jax.ShapeDtypeStruct(shape, parts[0].dtype)]
    return kernel(body, "join", [VMEM] * len(parts), shapes, [], {}, 1, SMALL, parts)[0]


def project_query(scalars, normed, gains, pieces, plan, size):
    rows, width = normed.shape
    inner = gains.shape[1]

    def body(scalar_ref, normed_ref, gain_ref, *refs):
        sources, (out_ref, whole) = refs[: len(pieces)], refs[len(pieces) :]
        place_rows(scalar_ref, sources, plan, 0, size, whole)
        for j in range(inner // COLS):
            cols = slice(j * COLS, (j + 1) * COLS)
            raw = jnp.dot(normed_ref[...], whole[:, cols], preferred_element_type=jnp.float32)
            out_ref[:, cols] = head_norm(raw, gain_ref[:, cols])

    shapes = [jax.ShapeDtypeStruct((rows, inner), jnp.bfloat16)]
    scratch = [pltpu.VMEM((width, inner), jnp.bfloat16)]
    specs = [SMEM] + [VMEM] * (2 + len(pieces))
    operands = [scalars, normed, gains, *pieces]
    flops = 2 * rows * width * inner
    return kernel(body, "project_query", specs, shapes, scratch, {}, flops, SMALL, operands)[0]


def whole_out(scalars, pieces, plan, size):
    width = pieces[0].shape[1]

    def body(scalar_ref, *refs):
        place_rows(scalar_ref, refs[: len(pieces)], plan, size, size, refs[-1])

    shapes = [jax.ShapeDtypeStruct((Y * Z * size, width), jnp.bfloat16)]
    specs = [SMEM] + [VMEM] * len(pieces)
    return kernel(body, "whole_out", specs, shapes, [], {}, 1, SMALL, [scalars, *pieces])[0]


def attend(scalars, query, window):
    rows, inner = query.shape
    factor = math.log2(math.e) / math.sqrt(HEAD_DIM)

    def body(scalar_ref, q_ref, window_ref, out_ref):
        def head(h, live):
            begin = pl.multiple_of(h * HEAD_DIM, HEAD_DIM)
            cols = pl.ds(begin, HEAD_DIM)
            value_cols = pl.ds(begin + inner, HEAD_DIM)
            q = q_ref[:, cols]
            scores = []
            for j in range(live):
                keys = window_ref[scalar_ref[AT_SLOT + j], :, cols]
                scores.append(
                    lax.dot_general(
                        q, keys, (((1,), (1,)), ((), ())), preferred_element_type=jnp.float32
                    )
                )
            highest = jnp.max(scores[0], axis=-1, keepdims=True)
            for s in scores[1:]:
                highest = jnp.maximum(highest, jnp.max(s, axis=-1, keepdims=True))
            total = mixed = None
            for j in range(live):
                p = jnp.exp2((scores[j] - highest) * factor)
                line = jnp.sum(p, axis=-1, keepdims=True)
                values = window_ref[scalar_ref[AT_SLOT + j], :, value_cols]
                term = jnp.dot(p.astype(jnp.bfloat16), values, preferred_element_type=jnp.float32)
                total = line if total is None else total + line
                mixed = term if mixed is None else mixed + term
            out_ref[:, cols] = (mixed * (1.0 / total)).astype(jnp.bfloat16)

        for live in range(2, NB + 1):

            @pl.when(scalar_ref[AT_LIVE] == live)
            def _(live=live):
                @pl.loop(0, HEADS // 2)
                def _(pair):
                    head(2 * pair, live)
                    head(2 * pair + 1, live)

    shapes = [jax.ShapeDtypeStruct((rows, inner), jnp.bfloat16)]
    flops = 4 * NB * rows * rows * inner
    operands = [scalars, query, window]
    specs = [SMEM, VMEM, VMEM]
    return kernel(body, "attend", specs, shapes, [], {}, flops, LARGE, operands)[0]


def project_out(attended, w_out, gate, x, at, count):
    width = w_out.shape[1]

    def body(a_ref, w_ref, gate_ref, x_ref, out_ref):
        for j in range(width // COLS):
            cols = slice(j * COLS, (j + 1) * COLS)
            branch = jnp.dot(
                a_ref[at : at + count, :], w_ref[:, cols], preferred_element_type=jnp.float32
            )
            residual = x_ref[at : at + count, cols].astype(jnp.float32)
            out_ref[:, cols] = (residual + gate_ref[:, cols] * branch).astype(jnp.bfloat16)

    shapes = [jax.ShapeDtypeStruct((count, width), jnp.bfloat16)]
    flops = 2 * count * width * w_out.shape[0]
    operands = [attended, w_out, gate, x]
    return kernel(body, "project_out", [VMEM] * 4, shapes, [], {}, flops, SMALL, operands)[0]


def on_device(arriving, modulation, gate, w_query, w_kv, w_out, qk_gain, neighbors, live):
    x = arriving[0, 0]
    rows = x.shape[0]
    size = w_query.shape[1]
    position = lax.axis_index("patch")
    away = neighbors[0] - position
    place = jnp.where(away < 0, -2 * away - 2, 2 * away - 1)
    place = jnp.where(away == 0, 2 * SPAN, jnp.clip(place, 0, 2 * SPAN))
    used = jnp.arange(NB, dtype=jnp.int32) < live[0]
    spots = jnp.arange(2 * SPAN, dtype=jnp.int32)
    need = jnp.any((place[:, None] == spots[None, :]) & used[:, None], axis=0)
    scalars = jnp.concatenate(
        [jnp.stack([position // Z, position % Z]), live, place, need.astype(jnp.int32)]
    ).astype(jnp.int32)

    shard = jnp.concatenate([w_query[0], w_out[0]], axis=0)
    up, down = [shard], [shard]
    for k in range(1, Z // 2 + 1):
        up.append(along_z(up[-1], 1))
        if k < Z // 2:
            down.append(along_z(down[-1], -1))
    low1, high1 = shifted(x, 1), shifted(x, -1)
    low2, high2 = shifted(low1, 1), shifted(high1, -1)
    groups = [
        ([-2, -1, 0, 1], [up[2], up[1], shard, down[1]], 1),
        ([-4, -3, 3, 2], [up[4], up[3], down[3], down[2]], -1),
    ]
    pieces, plan = [], []
    for zs, parts, onward in groups:
        block = join(parts)
        beside = {step: along_y(block, step) for step in (onward, -onward)}
        pieces += [block, beside[1], beside[-1], along_y(beside[onward], onward)]
        plan += [(0, zs, 0), (Y - 1, zs, 0), (1, zs, 0), (2, zs, 0)]

    gains = qk_gain[0]
    window, normed = own_tile(x, modulation[0], w_kv[0], gains[1:2])
    window = near_tiles(scalars, [low1, high1], modulation[0], w_kv[0], gains[1:2], window, 0)
    window = near_tiles(scalars, [low2, high2], modulation[0], w_kv[0], gains[1:2], window, 2)
    query = project_query(scalars, normed, gains[0:1], pieces, plan, size)
    out_whole = whole_out(scalars, pieces, plan, size)
    attended = attend(scalars, query, window)
    count = rows // 2
    parts = [
        to_next_section(project_out(attended, out_whole, gate, x, at, count)) for at in (0, count)
    ]
    return jnp.concatenate(parts, axis=0)[None, None]


def solution(mesh):
    placed = (
        P("section", "patch", None, None),
        P("section", None, None),
        P("section", None),
        P("section", "patch", None),
        P("section", None, None),
        P("section", "patch", None),
        P("section", None, None),
        P("patch", None),
        P("patch"),
    )
    return jax.shard_map(
        on_device,
        mesh=mesh,
        in_specs=placed,
        out_specs=P("section", "patch", None, None),
        check_vma=False,
    )
```

time: 437 us -> 222 us (0.51)
  the two profiles are of different devices: /device:TPU:24 before, /device:TPU:224 now
where the time goes in v2:
time: 222 us
  waiting for transfers between devices  130 us (59%)
  Pallas kernels  46.3 us (21%)
  starting transfers between devices  33.4 us (15%)
  local copies, waits for them, and re-layouts  7.9 us (4%)
  other arithmetic  4.42 us (2%)
    ppermute x7, waiting for transfers between devices, along_z(): lax.ppermute(value, 'patch', [(y * Z + z, y * Z + (z + steps) % Z) for y...  58.7 us
    ppermute x6, waiting for transfers between devices, along_y(): lax.ppermute(value, 'patch', [(y * Z + z, (y + steps) % Y * Z + z) for y...  50.1 us
    pallas_call x10, Pallas kernels, kernel(): pl.pallas_call(body, in_specs=specs, out_specs=[VMEM for _ in shapes], ou...  46.3 us
    ppermute x2, waiting for transfers between devices, to_next_section(): lax.ppermute(block, 'section', [(i, (i + 1) % count) for i in range(count)])  15.2 us
    ppermute x6, starting transfers between devices, along_y(): lax.ppermute(value, 'patch', [(y * Z + z, (y + steps) % Y * Z + z) for y...  12.1 us
    ppermute x4, starting transfers between devices, shifted(): lax.ppermute(value, 'patch', [(i, i + steps) for i in range(count) if 0 <...  10.5 us
    ppermute x7, starting transfers between devices, along_z(): lax.ppermute(value, 'patch', [(y * Z + z, y * Z + (z + steps) % Z) for y...  9.21 us
    unnamed x22, local copies, waits for them, and re-layouts  6.66 us
  transfers between devices with their start and end apart: 19, of which 11 were waited for; matrix products, arithmetic and copies ran while one was open for 2% of the time, Pallas kernels for 11%

profile of v2, /device:TPU:224, one launch (start us, length us, event | category | flops | bytes accessed | tf_op | source)
XLA Modules:
  0.0 222.5 jit_solution(2354860562719466460)
XLA Ops:
  0.0 1.0 pad_maximum_fusion.refs_2_
  1.0 0.1 collective-permute-start
  1.1 2.2 collective-permute-start.13
  3.3 1.8 collective-permute-start.2
  5.1 5.9 %collective-permute-done.refs_1_ = bf16[96,1536]{1,0:T(8,128)(2,1)S(1)} collective-permute-done((bf16[96,1536]{1,0:T(8,128)(2,1)S(1)}, bf16[96,1536]{1,0:T(8,128)(2,1)S(1)}, u32[]{:S(2)}, u32[]{:S(2)}) %collective-permute-start) | collective-permute-done | bytes 294944 | tf_op jit(solution)/shard_map/ppermute | solution.py:31
  11.0 1.2 collective-permute-start.1
  12.2 0.9 collective-permute-done.2.refs_3_
  13.1 0.5 collective-permute-start.8
  13.6 27.8 %collective-permute-done.1.refs_0_ = bf16[96,1536]{1,0:T(8,128)(2,1)S(1)} collective-permute-done((bf16[96,1536]{1,0:T(8,128)(2,1)S(1)}, bf16[96,1536]{1,0:T(8,128)(2,1)S(1)}, u32[]{:S(2)}, u32[]{:S(2)}) %collective-permute-start.1) | collective-permute-done | bytes 294944 | tf_op jit(solution)/shard_map/ppermute | solution.py:31
  41.4 1.5 collective-permute-start.6
  42.9 2.4 %collective-permute-start.15 = (bf16[384,1536]{1,0:T(8,128)(2,1)}, bf16[384,1536]{1,0:T(8,128)(2,1)}, u32[]{:S(2)}, u32[]{:S(2)}) collective-permute-start(bf16[384,1536]{1,0:T(8,128)(2,1)} %bitcast.21), channel_id=1, source_target_pairs={{1,0},{2,1},{3,2},{4,3},{5,4},{6,5},{7,6},{8,7},{9,8},{10,9},{11,1... | collective-permute-start | bytes 3538952 | tf_op jit(solution)/shard_map/ppermute | solution.py:25
  45.4 1.1 collective-permute-start.9
  46.5 2.9 %collective-permute-done.6.refs_1_ = bf16[96,1536]{1,0:T(8,128)(2,1)} collective-permute-done((bf16[96,1536]{1,0:T(8,128)(2,1)S(1)}, bf16[96,1536]{1,0:T(8,128)(2,1)}, u32[]{:S(2)}, u32[]{:S(2)}) %collective-permute-start.6) | collective-permute-done | bytes 294944 | tf_op jit(solution)/shard_map/ppermute | solution.py:31
  49.4 3.0 %collective-permute-start.7 = (bf16[96,1536]{1,0:T(8,128)(2,1)}, bf16[96,1536]{1,0:T(8,128)(2,1)}, u32[]{:S(2)}, u32[]{:S(2)}) collective-permute-start(bf16[96,1536]{1,0:T(8,128)(2,1)} %collective-permute-done.6.refs_1_), channel_id=1, source_target_pairs={{0,1},{1,2},{2,3},{3,4},{4,5},{5,6},{6,7},{7,0},{8,9},{9,10},{10,1... | collective-permute-start | bytes 884744 | tf_op jit(solution)/shard_map/ppermute | solution.py:31
  53.2 1.7 collective-permute-start.3
  54.9 21.2 %collective-permute-done.9.refs_2_ = bf16[96,1536]{1,0:T(8,128)(2,1)} collective-permute-done((bf16[96,1536]{1,0:T(8,128)(2,1)S(1)}, bf16[96,1536]{1,0:T(8,128)(2,1)}, u32[]{:S(2)}, u32[]{:S(2)}) %collective-permute-start.9) | collective-permute-done | bytes 294944 | tf_op jit(solution)/shard_map/ppermute | solution.py:31
  76.0 1.0 copy-done.5
  77.0 1.2 join.3.refs_4_
  78.2 6.8 %collective-permute-start.11 = (bf16[384,1536]{1,0:T(8,128)(2,1)S(1)}, bf16[384,1536]{1,0:T(8,128)(2,1)}, u32[]{:S(2)}, u32[]{:S(2)}) collective-permute-start(bf16[384,1536]{1,0:T(8,128)(2,1)S(1)} %join.3.refs_4_), channel_id=1, source_target_pairs={{0,24},{1,25},{2,26},{3,27},{4,28},{5,29},{6,30},{7,31},{8,0},{9,1... | collective-permute-start | bytes 3538952 | tf_op jit(solution)/shard_map/ppermute | solution.py:37
  85.0 1.9 collective-permute-start.14
  86.9 0.5 fusion.2
  87.5 3.9 %collective-permute-start.16 = (bf16[384,1536]{1,0:T(8,128)(2,1)}, bf16[384,1536]{1,0:T(8,128)(2,1)}, u32[]{:S(2)}, u32[]{:S(2)}) collective-permute-start(bf16[384,1536]{1,0:T(8,128)(2,1)} %collective-permute-done.15.refs_2_), channel_id=1, source_target_pairs={{1,0},{2,1},{3,2},{4,3},{5,4},{6,5},{7,6},{8,7},{9,8},{10,9},{11,1... | collective-permute-start | bytes 3538952 | tf_op jit(solution)/shard_map/ppermute | solution.py:25
  91.4 0.5 iota_compare_fusion.1
  91.9 0.7 fusion.1
  92.7 0.5 convert_element_type.3
  93.2 1.2 concatenate.9.scalar_ref.refs_0_
  94.4 3.7 %copy-done = bf16[1,1536,3072]{2,1,0:T(8,128)(2,1)S(1)} copy-done((bf16[1,1536,3072]{2,1,0:T(8,128)(2,1)S(1)}, bf16[1,1536,3072]{2,1,0:T(8,128)(2,1)}, u32[]{:S(2)}) %copy-start) | copy-done | bytes 9437208
  98.1 1.3 copy-done.2
  99.4 0.7 copy-done.6
  100.1 5.1 %own_tile.1 = (bf16[5,384,3072]{2,1,0:T(8,128)(2,1)S(1)}, bf16[384,1536]{1,0:T(8,128)(2,1)S(1)}) custom-call(bf16[384,1536]{1,0:T(8,128)(2,1)S(1)} %bitcast.22, f32[2,1536]{1,0:T(2,128)S(1)} %bitcast.25, bf16[1536,3072]{1,0:T(8,128)(2,1)S(1)} %bitcast.17, f32[1,1536]{1,0:T(1,128)S(1)} %get-tuple-element.10.gain_ref.refs_5_), custom_call_target="tpu_custom_call" | custom-call | flops 3623878656 | bytes 10635264 | tf_op jit(solution)/shard_map/own_tile/pallas_call | solution.py:69
  105.3 1.6 collective-permute-start.4
  106.8 0.5 collective-permute-start.10
  107.4 5.5 %collective-permute-done.14.refs_1_ = bf16[384,1536]{1,0:T(8,128)(2,1)} collective-permute-done((bf16[384,1536]{1,0:T(8,128)(2,1)}, bf16[384,1536]{1,0:T(8,128)(2,1)}, u32[]{:S(2)}, u32[]{:S(2)}) %collective-permute-start.14) | collective-permute-done | bytes 1179680 | tf_op jit(solution)/shard_map/ppermute | solution.py:25
  112.9 22.7 %collective-permute-done.11.refs_6_ = bf16[384,1536]{1,0:T(8,128)(2,1)} collective-permute-done((bf16[384,1536]{1,0:T(8,128)(2,1)S(1)}, bf16[384,1536]{1,0:T(8,128)(2,1)}, u32[]{:S(2)}, u32[]{:S(2)}) %collective-permute-start.11) | collective-permute-done | bytes 1179680 | tf_op jit(solution)/shard_map/ppermute | solution.py:37
  135.5 1.6 collective-permute-start.12
  137.1 11.9 %near_tiles.2.refs_6_ = bf16[5,384,3072]{2,1,0:T(8,128)(2,1)S(1)} custom-call(s32[11]{0:T(128)S(1)} %copy-done.8, bf16[384,1536]{1,0:T(8,128)(2,1)} %collective-permute-done.13.refs_1_, bf16[384,1536]{1,0:T(8,128)(2,1)} %collective-permute-done.15.refs_2_, f32[2,1536]{1,0:T(2,128)S(1)} %bitcast.26, ...), custom_call_target="tpu_custom_call", output_to_operand_aliasing={{}: (6, {})} | custom-call | flops 7247757312 | bytes 23611436 | tf_op jit(solution)/shard_map/near_tiles/pallas_call | solution.py:69
  149.1 6.8 %near_tiles.3.window_ref = bf16[5,384,3072]{2,1,0:T(8,128)(2,1)S(1)} custom-call(s32[11]{0:T(128)S(1)} %copy-done.8, bf16[384,1536]{1,0:T(8,128)(2,1)} %collective-permute-done.14.refs_1_, bf16[384,1536]{1,0:T(8,128)(2,1)} %collective-permute-done.16.refs_2_, f32[2,1536]{1,0:T(2,128)S(1)} %bitcast.27, ...), custom_call_target="tpu_custom_call", output_to_operand_aliasing={{}: (6, {})} | custom-call | flops 7247757312 | bytes 23611436 | tf_op jit(solution)/shard_map/near_tiles/pallas_call | solution.py:69
  155.9 4.8 %collective-permute-done.4.refs_2_ = bf16[384,1536]{1,0:T(8,128)(2,1)S(1)} collective-permute-done((bf16[384,1536]{1,0:T(8,128)(2,1)S(1)}, bf16[384,1536]{1,0:T(8,128)(2,1)S(1)}, u32[]{:S(2)}, u32[]{:S(2)}) %collective-permute-start.4) | collective-permute-done | bytes 1179680 | tf_op jit(solution)/shard_map/ppermute | solution.py:37
  160.7 22.6 %collective-permute-done.12.refs_7_ = bf16[384,1536]{1,0:T(8,128)(2,1)S(1)} collective-permute-done((bf16[384,1536]{1,0:T(8,128)(2,1)}, bf16[384,1536]{1,0:T(8,128)(2,1)S(1)}, u32[]{:S(2)}, u32[]{:S(2)}) %collective-permute-start.12) | collective-permute-done | bytes 1179680 | tf_op jit(solution)/shard_map/ppermute | solution.py:37
  183.3 3.8 %project_query.1.q_ref = bf16[384,1536]{1,0:T(8,128)(2,1)S(1)} custom-call(s32[11]{0:T(128)S(1)} %copy-done.8, bf16[384,1536]{1,0:T(8,128)(2,1)S(1)} %get-tuple-element.7.normed_ref, f32[1,1536]{1,0:T(1,128)S(1)} %get-tuple-element.9.gain_ref, bf16[384,1536]{1,0:T(8,128)(2,1)S(1)} %join.2.refs_0_, bf16[384,1536]{1,0:T(8,128)(2,1)S(1)} %collective-permute-done.3.refs_1_, ...), custom_call_target="tpu_custom_call" | custom-call | flops 1811939328 | bytes 10623020 | tf_op jit(solution)/shard_map/project_query/pallas_call | solution.py:69
  187.1 13.5 %attend.1.a_ref = bf16[384,1536]{1,0:T(8,128)(2,1)S(1)} custom-call(s32[11]{0:T(128)S(1)} %copy-done.8, bf16[384,1536]{1,0:T(8,128)(2,1)S(1)} %project_query.1.q_ref, bf16[5,384,3072]{2,1,0:T(8,128)(2,1)S(1)} %near_tiles.3.window_ref), custom_call_target="tpu_custom_call" | custom-call | flops 3623878656 | bytes 12976172 | tf_op jit(solution)/shard_map/attend/pallas_call | solution.py:69
  200.6 1.7 whole_out.1.w_ref
  202.3 1.1 project_out.2
  203.4 1.1 project_out.3
  204.6 1.6 collective-permute-start.18
  206.2 8.9 %collective-permute-done.17 = bf16[192,1536]{1,0:T(8,128)(2,1)S(1)} collective-permute-done((bf16[192,1536]{1,0:T(8,128)(2,1)S(1)}, bf16[192,1536]{1,0:T(8,128)(2,1)S(1)}, u32[]{:S(2)}, u32[]{:S(2)}) %collective-permute-start.17) | collective-permute-done | bytes 589856 | tf_op jit(solution)/shard_map/ppermute | solution.py:44
  215.1 6.3 %collective-permute-done.18 = bf16[192,1536]{1,0:T(8,128)(2,1)S(1)} collective-permute-done((bf16[192,1536]{1,0:T(8,128)(2,1)S(1)}, bf16[192,1536]{1,0:T(8,128)(2,1)S(1)}, u32[]{:S(2)}, u32[]{:S(2)}) %collective-permute-start.18) | collective-permute-done | bytes 589856 | tf_op jit(solution)/shard_map/ppermute | solution.py:44
  221.4 1.1 maximum_bitcast_fusion
  (30 shorter events, 0.2 us)
Async XLA Ops:
  1.0 10.0 %collective-permute-start = (bf16[96,1536]{1,0:T(8,128)(2,1)S(1)}, bf16[96,1536]{1,0:T(8,128)(2,1)S(1)}, u32[]{:S(2)}, u32[]{:S(2)}) collective-permute-start(bf16[96,1536]{1,0:T(8,128)(2,1)S(1)} %pad_maximum_fusion.refs_2_), channel_id=1, source_target_pairs={{0,1},{1,2},{2,3},{3,4},{4,5},{5,6},{6,7},{7,0},{8,9},{9,10},{10,1... | collective-permute-start | bytes 884744 | tf_op jit(solution)/shard_map/ppermute | solution.py:31
  1.1 83.9 %collective-permute-start.13 = (bf16[384,1536]{1,0:T(8,128)(2,1)}, bf16[384,1536]{1,0:T(8,128)(2,1)}, u32[]{:S(2)}, u32[]{:S(2)}) collective-permute-start(bf16[384,1536]{1,0:T(8,128)(2,1)} %bitcast.20), channel_id=1, source_target_pairs={{0,1},{1,2},{2,3},{3,4},{4,5},{5,6},{6,7},{7,8},{8,9},{9,10},{10,1... | collective-permute-start | bytes 3538952 | tf_op jit(solution)/shard_map/ppermute | solution.py:25
  3.3 9.8 %collective-permute-start.2 = (bf16[96,1536]{1,0:T(8,128)(2,1)S(1)}, bf16[96,1536]{1,0:T(8,128)(2,1)S(1)}, u32[]{:S(2)}, u32[]{:S(2)}) collective-permute-start(bf16[96,1536]{1,0:T(8,128)(2,1)S(1)} %pad_maximum_fusion.refs_2_), channel_id=1, source_target_pairs={{0,7},{1,0},{2,1},{3,2},{4,3},{5,4},{6,5},{7,6},{8,15},{9,8},{10,9... | collective-permute-start | bytes 884744 | tf_op jit(solution)/shard_map/ppermute | solution.py:31
  11.0 30.5 %collective-permute-start.1 = (bf16[96,1536]{1,0:T(8,128)(2,1)S(1)}, bf16[96,1536]{1,0:T(8,128)(2,1)S(1)}, u32[]{:S(2)}, u32[]{:S(2)}) collective-permute-start(bf16[96,1536]{1,0:T(8,128)(2,1)S(1)} %collective-permute-done.refs_1_), channel_id=1, source_target_pairs={{0,1},{1,2},{2,3},{3,4},{4,5},{5,6},{6,7},{7,0},{8,9},{9,10},{10,1... | collective-permute-start | bytes 884744 | tf_op jit(solution)/shard_map/ppermute | solution.py:31
  13.1 32.3 %collective-permute-start.8 = (bf16[96,1536]{1,0:T(8,128)(2,1)S(1)}, bf16[96,1536]{1,0:T(8,128)(2,1)S(1)}, u32[]{:S(2)}, u32[]{:S(2)}) collective-permute-start(bf16[96,1536]{1,0:T(8,128)(2,1)S(1)} %collective-permute-done.2.refs_3_), channel_id=1, source_target_pairs={{0,7},{1,0},{2,1},{3,2},{4,3},{5,4},{6,5},{7,6},{8,15},{9,8},{10,9... | collective-permute-start | bytes 884744 | tf_op jit(solution)/shard_map/ppermute | solution.py:31
  41.4 8.0 %collective-permute-start.6 = (bf16[96,1536]{1,0:T(8,128)(2,1)S(1)}, bf16[96,1536]{1,0:T(8,128)(2,1)}, u32[]{:S(2)}, u32[]{:S(2)}) collective-permute-start(bf16[96,1536]{1,0:T(8,128)(2,1)S(1)} %collective-permute-done.1.refs_0_), channel_id=1, source_target_pairs={{0,1},{1,2},{2,3},{3,4},{4,5},{5,6},{6,7},{7,0},{8,9},{9,10},{10,1... | collective-permute-start | bytes 884744 | tf_op jit(solution)/shard_map/ppermute | solution.py:31
  42.9 44.6 %collective-permute-start.15 = (bf16[384,1536]{1,0:T(8,128)(2,1)}, bf16[384,1536]{1,0:T(8,128)(2,1)}, u32[]{:S(2)}, u32[]{:S(2)}) collective-permute-start(bf16[384,1536]{1,0:T(8,128)(2,1)} %bitcast.21), channel_id=1, source_target_pairs={{1,0},{2,1},{3,2},{4,3},{5,4},{6,5},{7,6},{8,7},{9,8},{10,9},{11,1... | collective-permute-start | bytes 3538952 | tf_op jit(solution)/shard_map/ppermute | solution.py:25
  45.4 7.8 %copy-start.4 = (bf16[96,1536]{1,0:T(8,128)(2,1)}, bf16[96,1536]{1,0:T(8,128)(2,1)S(1)}, u32[]{:S(2)}) copy-start(bf16[96,1536]{1,0:T(8,128)(2,1)S(1)} %collective-permute-done.8.refs_3_) | copy-start | bytes 884740
  45.4 30.6 %collective-permute-start.9 = (bf16[96,1536]{1,0:T(8,128)(2,1)S(1)}, bf16[96,1536]{1,0:T(8,128)(2,1)}, u32[]{:S(2)}, u32[]{:S(2)}) collective-permute-start(bf16[96,1536]{1,0:T(8,128)(2,1)S(1)} %collective-permute-done.8.refs_3_), channel_id=1, source_target_pairs={{0,7},{1,0},{2,1},{3,2},{4,3},{5,4},{6,5},{7,6},{8,15},{9,8},{10,9... | collective-permute-start | bytes 884744 | tf_op jit(solution)/shard_map/ppermute | solution.py:31
  49.4 26.6 %collective-permute-start.7 = (bf16[96,1536]{1,0:T(8,128)(2,1)}, bf16[96,1536]{1,0:T(8,128)(2,1)}, u32[]{:S(2)}, u32[]{:S(2)}) collective-permute-start(bf16[96,1536]{1,0:T(8,128)(2,1)} %collective-permute-done.6.refs_1_), channel_id=1, source_target_pairs={{0,1},{1,2},{2,3},{3,4},{4,5},{5,6},{6,7},{7,0},{8,9},{9,10},{10,1... | collective-permute-start | bytes 884744 | tf_op jit(solution)/shard_map/ppermute | solution.py:31
  53.1 33.8 %copy-start.10 = (s32[1,4]{1,0:T(1,128)S(1)}, s32[1,4]{1,0:T(1,128)}, u32[]{:S(2)}) copy-start(s32[1,4]{1,0:T(1,128)} %param.16) | copy-start | bytes 52
  53.1 34.4 %copy-start.9 = (f32[1,2,1536]{2,1,0:T(2,128)S(1)}, f32[1,2,1536]{2,1,0:T(2,128)}, u32[]{:S(2)}) copy-start(f32[1,2,1536]{2,1,0:T(2,128)} %param.15) | copy-start | bytes 36868
  53.2 53.6 %collective-permute-start.3 = (bf16[384,1536]{1,0:T(8,128)(2,1)S(1)}, bf16[384,1536]{1,0:T(8,128)(2,1)S(1)}, u32[]{:S(2)}, u32[]{:S(2)}) collective-permute-start(bf16[384,1536]{1,0:T(8,128)(2,1)S(1)} %join.2.refs_0_), channel_id=1, source_target_pairs={{0,8},{1,9},{2,10},{3,11},{4,12},{5,13},{6,14},{7,15},{8,16},{9,17... | collective-permute-start | bytes 3538952 | tf_op jit(solution)/shard_map/ppermute | solution.py:37
  76.0 1.0 copy-start.5
  78.2 57.3 %collective-permute-start.11 = (bf16[384,1536]{1,0:T(8,128)(2,1)S(1)}, bf16[384,1536]{1,0:T(8,128)(2,1)}, u32[]{:S(2)}, u32[]{:S(2)}) collective-permute-start(bf16[384,1536]{1,0:T(8,128)(2,1)S(1)} %join.3.refs_4_), channel_id=1, source_target_pairs={{0,24},{1,25},{2,26},{3,27},{4,28},{5,29},{6,30},{7,31},{8,0},{9,1... | collective-permute-start | bytes 3538952 | tf_op jit(solution)/shard_map/ppermute | solution.py:37
  85.0 27.9 %collective-permute-start.14 = (bf16[384,1536]{1,0:T(8,128)(2,1)}, bf16[384,1536]{1,0:T(8,128)(2,1)}, u32[]{:S(2)}, u32[]{:S(2)}) collective-permute-start(bf16[384,1536]{1,0:T(8,128)(2,1)} %collective-permute-done.13.refs_1_), channel_id=1, source_target_pairs={{0,1},{1,2},{2,3},{3,4},{4,5},{5,6},{6,7},{7,8},{8,9},{9,10},{10,1... | collective-permute-start | bytes 3538952 | tf_op jit(solution)/shard_map/ppermute | solution.py:25
  87.5 61.6 %collective-permute-start.16 = (bf16[384,1536]{1,0:T(8,128)(2,1)}, bf16[384,1536]{1,0:T(8,128)(2,1)}, u32[]{:S(2)}, u32[]{:S(2)}) collective-permute-start(bf16[384,1536]{1,0:T(8,128)(2,1)} %collective-permute-done.15.refs_2_), channel_id=1, source_target_pairs={{1,0},{2,1},{3,2},{4,3},{5,4},{6,5},{7,6},{8,7},{9,8},{10,9},{11,1... | collective-permute-start | bytes 3538952 | tf_op jit(solution)/shard_map/ppermute | solution.py:25
  94.4 3.7 %copy-start = (bf16[1,1536,3072]{2,1,0:T(8,128)(2,1)S(1)}, bf16[1,1536,3072]{2,1,0:T(8,128)(2,1)}, u32[]{:S(2)}) copy-start(bf16[1,1536,3072]{2,1,0:T(8,128)(2,1)} %param.13) | copy-start | bytes 28311556
  98.1 1.3 copy-start.2
  99.4 0.7 copy-start.6
  100.1 37.0 %copy-start.1 = (bf16[1,1536,3072]{2,1,0:T(8,128)(2,1)S(1)}, bf16[1,1536,3072]{2,1,0:T(8,128)(2,1)}, u32[]{:S(2)}) copy-start(bf16[1,1536,3072]{2,1,0:T(8,128)(2,1)} %param.13) | copy-start | bytes 28311556
  100.1 37.0 %copy-start.8 = (s32[11]{0:T(128)S(1)}, s32[11]{0:T(128)}, u32[]{:S(2)}) copy-start(s32[11]{0:T(128)} %concatenate.9.scalar_ref.refs_0_) | copy-start | bytes 136
  105.3 55.4 %collective-permute-start.4 = (bf16[384,1536]{1,0:T(8,128)(2,1)S(1)}, bf16[384,1536]{1,0:T(8,128)(2,1)S(1)}, u32[]{:S(2)}, u32[]{:S(2)}) collective-permute-start(bf16[384,1536]{1,0:T(8,128)(2,1)S(1)} %join.2.refs_0_), channel_id=1, source_target_pairs={{0,24},{1,25},{2,26},{3,27},{4,28},{5,29},{6,30},{7,31},{8,0},{9,1... | collective-permute-start | bytes 3538952 | tf_op jit(solution)/shard_map/ppermute | solution.py:37
  106.8 53.9 %collective-permute-start.10 = (bf16[384,1536]{1,0:T(8,128)(2,1)S(1)}, bf16[384,1536]{1,0:T(8,128)(2,1)S(1)}, u32[]{:S(2)}, u32[]{:S(2)}) collective-permute-start(bf16[384,1536]{1,0:T(8,128)(2,1)S(1)} %join.3.refs_4_), channel_id=1, source_target_pairs={{0,8},{1,9},{2,10},{3,11},{4,12},{5,13},{6,14},{7,15},{8,16},{9,17... | collective-permute-start | bytes 3538952 | tf_op jit(solution)/shard_map/ppermute | solution.py:37
  112.9 47.8 %collective-permute-start.5 = (bf16[384,1536]{1,0:T(8,128)(2,1)S(1)}, bf16[384,1536]{1,0:T(8,128)(2,1)S(1)}, u32[]{:S(2)}, u32[]{:S(2)}) collective-permute-start(bf16[384,1536]{1,0:T(8,128)(2,1)S(1)} %collective-permute-done.3.refs_1_), channel_id=1, source_target_pairs={{0,8},{1,9},{2,10},{3,11},{4,12},{5,13},{6,14},{7,15},{8,16},{9,17... | collective-permute-start | bytes 3538952 | tf_op jit(solution)/shard_map/ppermute | solution.py:37
  135.5 47.8 %collective-permute-start.12 = (bf16[384,1536]{1,0:T(8,128)(2,1)}, bf16[384,1536]{1,0:T(8,128)(2,1)S(1)}, u32[]{:S(2)}, u32[]{:S(2)}) collective-permute-start(bf16[384,1536]{1,0:T(8,128)(2,1)} %collective-permute-done.11.refs_6_), channel_id=1, source_target_pairs={{0,24},{1,25},{2,26},{3,27},{4,28},{5,29},{6,30},{7,31},{8,0},{9,1... | collective-permute-start | bytes 3538952 | tf_op jit(solution)/shard_map/ppermute | solution.py:37
  200.6 1.7 copy-start.3
  200.6 1.7 copy-start.7
  204.5 10.5 %collective-permute-start.17 = (bf16[192,1536]{1,0:T(8,128)(2,1)S(1)}, bf16[192,1536]{1,0:T(8,128)(2,1)S(1)}, u32[]{:S(2)}, u32[]{:S(2)}) collective-permute-start(bf16[192,1536]{1,0:T(8,128)(2,1)S(1)} %project_out.2), channel_id=1, source_target_pairs={{0,32},{32,64},{64,96},{96,128},{128,160},{160,192},{192,224},{224... | collective-permute-start | bytes 1769480 | tf_op jit(solution)/shard_map/ppermute | solution.py:44
  204.6 16.8 %collective-permute-start.18 = (bf16[192,1536]{1,0:T(8,128)(2,1)S(1)}, bf16[192,1536]{1,0:T(8,128)(2,1)S(1)}, u32[]{:S(2)}, u32[]{:S(2)}) collective-permute-start(bf16[192,1536]{1,0:T(8,128)(2,1)S(1)} %project_out.3), channel_id=1, source_target_pairs={{0,32},{32,64},{64,96},{96,128},{128,160},{160,192},{192,224},{224... | collective-permute-start | bytes 1769480 | tf_op jit(solution)/shard_map/ppermute | solution.py:44

commit v3 on v2

v3 whole, which is shorter than its diff:
```python
import math

import jax
import jax.numpy as jnp
from jax import lax
from jax.experimental import pallas as pl
from jax.experimental.pallas import tpu as pltpu
from jax.sharding import PartitionSpec as P

HEADS = 12
HEAD_DIM = 128
SPAN = 2
NB = 4
Y, Z = 4, 8
COLS = 512
SMALL = 12 * 1024 * 1024
LARGE = 20 * 1024 * 1024
VMEM = pl.BlockSpec(memory_space=pltpu.VMEM)
SMEM = pl.BlockSpec(memory_space=pltpu.SMEM)
HBM = pl.BlockSpec(memory_space=pltpu.HBM)
OFFSETS = [-1, 1, -2, 2]


def along_z(value, steps, wrap=True):
    pairs = [
        (y * Z + z, y * Z + (z + steps) % Z)
        for y in range(Y)
        for z in range(Z)
        if wrap or 0 <= z + steps < Z
    ]
    return lax.ppermute(value, "patch", pairs)


def around_rows(value):
    ends = [(y * Z + Z - 1, (y + 1) * Z) for y in range(Y - 1)]
    return lax.ppermute(value, "patch", ends + [(b, a) for a, b in ends])


def along_y(value, steps):
    return lax.ppermute(
        value, "patch", [(y * Z + z, ((y + steps) % Y) * Z + z) for y in range(Y) for z in range(Z)]
    )


def along_y_by_half(value, steps):
    pairs = [
        (y * Z + z, ((y + (steps if z < Z // 2 else -steps)) % Y) * Z + z)
        for y in range(Y)
        for z in range(Z)
    ]
    return lax.ppermute(value, "patch", pairs)


def across_rows(value):
    pairs = [(y * Z + Z - 1, (y + 1) * Z + Z - 1) for y in range(Y - 1)]
    pairs += [((y + 1) * Z, y * Z) for y in range(Y - 1)]
    return lax.ppermute(value, "patch", pairs)


def to_next_section(block):
    count = lax.axis_size("section")
    return lax.ppermute(block, "section", [(i, (i + 1) % count) for i in range(count)])


def norm_rows(x, modulation):
    values = x.astype(jnp.float32)
    width = values.shape[1]
    average = jnp.sum(values, axis=-1, keepdims=True) * (1.0 / width)
    centered = values - average
    variance = jnp.sum(centered * centered, axis=-1, keepdims=True) * (1.0 / width)
    scaled = centered * lax.rsqrt(variance + 1e-06)
    return (scaled * (1.0 + modulation[1:2]) + modulation[0:1]).astype(jnp.bfloat16)


def head_norm(raw, gains):
    parts = []
    for h in range(raw.shape[1] // HEAD_DIM):
        piece = raw[:, h * HEAD_DIM : (h + 1) * HEAD_DIM]
        square = jnp.sum(piece * piece, axis=-1, keepdims=True) * (1.0 / HEAD_DIM)
        gain = gains[:, h * HEAD_DIM : (h + 1) * HEAD_DIM]
        parts.append((piece * lax.rsqrt(square + 1e-06) * gain).astype(jnp.bfloat16))
    return jnp.concatenate(parts, axis=1) if len(parts) > 1 else parts[0]


def kernel(body, name, specs, shapes, scratch, aliases, flops, limit, operands):
    moved = sum(o.size * o.dtype.itemsize for o in operands)
    return pl.pallas_call(
        body,
        in_specs=specs,
        out_specs=[VMEM for _ in shapes],
        out_shape=shapes,
        scratch_shapes=scratch,
        input_output_aliases=aliases,
        compiler_params=pltpu.CompilerParams(vmem_limit_bytes=limit),
        cost_estimate=pl.CostEstimate(flops=flops, transcendentals=0, bytes_accessed=moved),
        name=name,
    )(*operands)


def after(value, *others):
    return lax.optimization_barrier((value, *others))[0]


def own_tile(x, modulation, w_kv, gains):
    rows, width = x.shape
    wide = w_kv.shape[1]
    steps = wide // COLS

    def body(x_hbm, modulation_ref, w_hbm, gain_ref, window_ref, normed_ref, w_ref, x_ref, sems):
        def fetch(j):
            cols = pl.ds(pl.multiple_of(j * COLS, COLS), COLS)
            return pltpu.make_async_copy(w_hbm.at[:, cols], w_ref.at[:, cols], sems.at[j])

        rows_in = pltpu.make_async_copy(x_hbm, x_ref, sems.at[steps])
        rows_in.start()
        for j in range(steps):
            fetch(j).start()
        rows_in.wait()
        normed_ref[...] = norm_rows(x_ref[...], modulation_ref)

        @pl.loop(0, steps // 2)
        def _(j):
            fetch(j).wait()
            cols = pl.ds(pl.multiple_of(j * COLS, COLS), COLS)
            raw = jnp.dot(normed_ref[...], w_ref[:, cols], preferred_element_type=jnp.float32)
            window_ref[2 * SPAN, :, cols] = head_norm(raw, gain_ref[:, cols])

        @pl.loop(steps // 2, steps)
        def _(j):
            fetch(j).wait()
            cols = pl.ds(pl.multiple_of(j * COLS, COLS), COLS)
            raw = jnp.dot(normed_ref[...], w_ref[:, cols], preferred_element_type=jnp.float32)
            window_ref[2 * SPAN, :, cols] = raw.astype(jnp.bfloat16)

    shapes = [
        jax.ShapeDtypeStruct((2 * SPAN + 1, rows, wide), jnp.bfloat16),
        jax.ShapeDtypeStruct((rows, width), jnp.bfloat16),
        jax.ShapeDtypeStruct(w_kv.shape, w_kv.dtype),
    ]
    scratch = [pltpu.VMEM((rows, width), x.dtype), pltpu.SemaphoreType.DMA((steps + 1,))]
    flops = 2 * rows * width * wide
    x, w_kv = (pltpu.with_memory_space_constraint(o, pltpu.HBM) for o in (x, w_kv))
    operands = [x, modulation, w_kv, gains]
    specs = [HBM, VMEM, HBM, VMEM]
    return kernel(body, "own_tile", specs, shapes, scratch, {}, flops, SMALL, operands)


def near_tile(place, scalars, tile, modulation, w_kv, gains, window):
    rows, width = tile.shape
    wide = w_kv.shape[1]

    def body(
        at_ref, list_ref, live_ref, x_ref, modulation_ref, w_ref, gain_ref, _, window_ref, normed
    ):
        named = False
        for j in range(1, NB):
            hit = (list_ref[j] - at_ref[0] == OFFSETS[place]) & (live_ref[0] > j)
            named = named | hit

        @pl.when(named)
        def _():
            normed[...] = norm_rows(x_ref[...], modulation_ref)

            @pl.loop(0, wide // (2 * COLS))
            def _(j):
                cols = pl.ds(pl.multiple_of(j * COLS, COLS), COLS)
                raw = jnp.dot(normed[...], w_ref[:, cols], preferred_element_type=jnp.float32)
                window_ref[place, :, cols] = head_norm(raw, gain_ref[:, cols])
                cols = pl.ds(pl.multiple_of(wide // 2 + j * COLS, COLS), COLS)
                raw = jnp.dot(normed[...], w_ref[:, cols], preferred_element_type=jnp.float32)
                window_ref[place, :, cols] = raw.astype(jnp.bfloat16)

    shapes = [jax.ShapeDtypeStruct(window.shape, window.dtype)]
    specs = [SMEM] * 3 + [VMEM] * 5
    scratch = [pltpu.VMEM((rows, width), jnp.bfloat16)]
    operands = [*scalars, tile, modulation, w_kv, gains, window]
    flops = 2 * rows * width * wide
    aliases = {len(operands) - 1: 0}
    return kernel(body, "near_tile", specs, shapes, scratch, aliases, flops, SMALL, operands)[0]


def join(parts):
    rows, width = parts[0].shape
    count = rows // 2

    def body(*refs):
        whole = refs[-1]
        second = count * len(parts)
        for k, ref in enumerate(refs[:-1]):
            whole[k * count : (k + 1) * count, :] = ref[:count, :]
            whole[second + k * count : second + (k + 1) * count, :] = ref[count:, :]

    shapes = [jax.ShapeDtypeStruct((len(parts) * rows, width), parts[0].dtype)]
    return kernel(body, "join", [VMEM] * len(parts), shapes, [], {}, 1, SMALL, parts)[0]


def onward(at, lows, highs):
    rows, width = lows[0].shape
    half = rows // 2
    count = len(lows)

    def body(at_ref, *refs):
        low_refs, high_refs, (query_ref, out_ref) = (
            refs[:count],
            refs[count : 2 * count],
            refs[2 * count :],
        )
        for left, query_from, out_from in (
            (True, high_refs, low_refs),
            (False, low_refs, high_refs),
        ):

            @pl.when((at_ref[0] % Z < Z // 2) == left)
            def _(query_from=query_from, out_from=out_from):
                for k in range(count):
                    query_ref[k * half : (k + 1) * half, :] = query_from[k][:half, :]
                    out_ref[k * half : (k + 1) * half, :] = out_from[k][half:, :]

    shapes = [jax.ShapeDtypeStruct((count * half, width), lows[0].dtype)] * 2
    specs = [SMEM] + [VMEM] * (2 * count)
    return kernel(body, "onward", specs, shapes, [], {}, 1, SMALL, [at, *lows, *highs])


def place_rows(at_ref, sources, plan, size, target):
    own_y, own_z = at_ref[0] // Z, at_ref[0] % Z
    for ref, (dy, zs, begin) in zip(sources, plan, strict=True):
        at_y = (own_y + dy) % Y
        for k, dz in enumerate(zs):
            shard = at_y * Z + (own_z + dz) % Z
            row = pl.multiple_of(shard * size, 16)
            target[pl.ds(row, size), :] = ref[begin + k * size : begin + (k + 1) * size, :]


def project_query(at, normed, gains, pieces, plan):
    rows, width = normed.shape
    inner = gains.shape[1]
    size = width // (Y * Z)

    def body(at_ref, normed_ref, gain_ref, *refs):
        sources, (out_ref, whole) = refs[: len(pieces)], refs[len(pieces) :]
        place_rows(at_ref, sources, plan, size, whole)
        for j in range(inner // COLS):
            cols = slice(j * COLS, (j + 1) * COLS)
            raw = jnp.dot(normed_ref[...], whole[:, cols], preferred_element_type=jnp.float32)
            out_ref[:, cols] = head_norm(raw, gain_ref[:, cols])

    shapes = [jax.ShapeDtypeStruct((rows, inner), jnp.bfloat16)]
    scratch = [pltpu.VMEM((width, inner), jnp.bfloat16)]
    specs = [SMEM] + [VMEM] * (2 + len(pieces))
    operands = [at, normed, gains, *pieces]
    flops = 2 * rows * width * inner
    return kernel(body, "project_query", specs, shapes, scratch, {}, flops, SMALL, operands)[0]


def whole_out(at, pieces, plan, inner):
    width = pieces[0].shape[1]
    size = inner // (Y * Z)

    def body(at_ref, *refs):
        place_rows(at_ref, refs[: len(pieces)], plan, size, refs[-1])

    shapes = [jax.ShapeDtypeStruct((inner, width), jnp.bfloat16)]
    specs = [SMEM] + [VMEM] * len(pieces)
    return kernel(body, "whole_out", specs, shapes, [], {}, 1, SMALL, [at, *pieces])[0]


def attend(scalars, query, window):
    rows, inner = query.shape
    factor = math.log2(math.e) / math.sqrt(HEAD_DIM)

    def body(at_ref, list_ref, live_ref, q_ref, window_ref, out_ref):
        def place(j):
            away = list_ref[j] - at_ref[0]
            found = jnp.where(away < 0, -2 * away - 2, 2 * away - 1)
            return jnp.where(away == 0, 2 * SPAN, jnp.clip(found, 0, 2 * SPAN - 1))

        def head(h, places):
            begin = pl.multiple_of(h * HEAD_DIM, HEAD_DIM)
            cols = pl.ds(begin, HEAD_DIM)
            value_cols = pl.ds(begin + inner, HEAD_DIM)
            q = q_ref[:, cols]
            scores = []
            for p in places:
                keys = window_ref[p, :, cols]
                scores.append(
                    lax.dot_general(
                        q, keys, (((1,), (1,)), ((), ())), preferred_element_type=jnp.float32
                    )
                )
            highest = jnp.max(scores[0], axis=-1, keepdims=True)
            for s in scores[1:]:
                highest = jnp.maximum(highest, jnp.max(s, axis=-1, keepdims=True))
            total = mixed = None
            for s, p in zip(scores, places, strict=True):
                weight = jnp.exp2((s - highest) * factor)
                line = jnp.sum(weight, axis=-1, keepdims=True)
                term = jnp.dot(
                    weight.astype(jnp.bfloat16),
                    window_ref[p, :, value_cols],
                    preferred_element_type=jnp.float32,
                )
                total = line if total is None else total + line
                mixed = term if mixed is None else mixed + term
            out_ref[:, cols] = (mixed * (1.0 / total)).astype(jnp.bfloat16)

        for live in range(2, NB + 1):

            @pl.when(live_ref[0] == live)
            def _(live=live):
                places = [2 * SPAN] + [place(j) for j in range(1, live)]

                @pl.loop(0, HEADS // 2)
                def _(pair):
                    head(2 * pair, places)
                    head(2 * pair + 1, places)

    shapes = [jax.ShapeDtypeStruct((rows, inner), jnp.bfloat16)]
    flops = 4 * NB * rows * rows * inner
    operands = [*scalars, query, window]
    specs = [SMEM] * 3 + [VMEM] * 2
    return kernel(body, "attend", specs, shapes, [], {}, flops, LARGE, operands)[0]


def project_out(attended, w_out, gate, x, at, count):
    width = w_out.shape[1]

    def body(a_ref, w_ref, gate_ref, x_ref, out_ref):
        for j in range(width // COLS):
            cols = slice(j * COLS, (j + 1) * COLS)
            branch = jnp.dot(
                a_ref[at : at + count, :], w_ref[:, cols], preferred_element_type=jnp.float32
            )
            residual = x_ref[at : at + count, cols].astype(jnp.float32)
            out_ref[:, cols] = (residual + gate_ref[:, cols] * branch).astype(jnp.bfloat16)

    shapes = [jax.ShapeDtypeStruct((count, width), jnp.bfloat16)]
    flops = 2 * count * width * w_out.shape[0]
    operands = [attended, w_out, gate, x]
    return kernel(body, "project_out", [VMEM] * 4, shapes, [], {}, flops, SMALL, operands)[0]


def on_device(arriving, modulation, gate, w_query, w_kv, w_out, qk_gain, neighbors, live):
    x = arriving[0, 0]
    rows = x.shape[0]
    at = lax.axis_index("patch").astype(jnp.int32).reshape(1)
    size = w_query.shape[1]
    scalars = [at, neighbors[0], live]
    gains = qk_gain[0]

    shard = jnp.concatenate([w_query[0], w_out[0]], axis=0)
    zs_a, zs_b = [-2, -1, 0, 1], [-4, -3, 3, 2]
    up, down = [shard], [shard]
    for k in range(1, 3):
        up.append(along_z(up[-1], 1))
        down.append(along_z(down[-1], -1))
    crossed = across_rows(x)
    own_z = at[0] % Z
    block_a = join([up[2], up[1], shard, down[1]])
    low_a, high_a = along_y(block_a, 1), along_y(block_a, -1)
    up.append(along_z(up[2], 1))
    down.append(along_z(down[2], -1))
    up.append(along_z(after(up[3], block_a), 1))
    block_b = join([up[4], up[3], down[3], down[2]])
    x_up = after(jnp.where(own_z == Z - 1, crossed, x), up[4], down[3])
    x_down = after(jnp.where(own_z == 0, crossed, x), up[4], down[3])
    low1, high1 = along_z(x_up, 1), along_z(x_down, -1)
    low_b = along_y(block_b, 1)
    window, normed, w_kv_near = own_tile(after(x, block_b), modulation[0], w_kv[0], gains[1:2])
    high_b = along_y(after(block_b, normed, low_a, high_a), -1)
    low2, high2 = along_z(low1, 1, wrap=False), along_z(high1, -1, wrap=False)

    def add_tile(window, place, tile):
        return near_tile(place, scalars, tile, modulation[0], w_kv_near, gains[1:2], window)

    window = add_tile(add_tile(window, 0, low1), 1, high1)
    low_b, high_b, window = lax.optimization_barrier((low_b, high_b, window))
    edge = after(jnp.where(own_z == 0, high1, low1), low_b)
    edge_far = around_rows(edge)
    query_on, out_on = onward(at, [low_a, after(low_b, edge)], [high_a, high_b])
    query_far = along_y_by_half(query_on, -1)
    out_far = along_y_by_half(out_on, 1)
    near_blocks = [block_a, low_a, high_a, block_b, low_b, high_b]
    sides = [(dy, zs) for zs in (zs_a, zs_b) for dy in (0, Y - 1, 1)]
    half = len(zs_a) * size
    query_plan = [(dy, zs, 0) for dy, zs in sides] + [(2, zs_a + zs_b, 0)]
    out_plan = [(dy, zs, half) for dy, zs in sides] + [(2, zs_a + zs_b, 0)]
    query_pieces = near_blocks + [query_far]
    out_pieces = near_blocks + [out_far]

    window = add_tile(window, 2, jnp.where(own_z == 0, edge_far, low2))
    window = add_tile(window, 3, jnp.where(own_z == Z - 1, edge_far, high2))
    query = project_query(at, normed, gains[0:1], query_pieces, query_plan)
    out_whole = whole_out(at, out_pieces, out_plan, gains.shape[1])
    attended = attend(scalars, query, window)
    count = rows // 2
    parts = [
        to_next_section(project_out(attended, out_whole, gate, x, at_row, count))
        for at_row in (0, count)
    ]
    return jnp.concatenate(parts, axis=0)[None, None]


def solution(mesh):
    placed = (
        P("section", "patch", None, None),
        P("section", None, None),
        P("section", None),
        P("section", "patch", None),
        P("section", None, None),
        P("section", "patch", None),
        P("section", None, None),
        P("patch", None),
        P("patch"),
    )
    return jax.shard_map(
        on_device,
        mesh=mesh,
        in_specs=placed,
        out_specs=P("section", "patch", None, None),
        check_vma=False,
    )
```

time: 222 us -> 164 us (0.74)
  the two profiles are of different devices: /device:TPU:224 before, /device:TPU:24 now
where the time goes in v3:
time: 164 us; the launch traced here: 165 us
  waiting for transfers between devices  78.4 us (48%)
  Pallas kernels  43.7 us (27%)
  starting transfers between devices  38.5 us (23%)
  other arithmetic  2.57 us (2%)
    pallas_call x13, Pallas kernels, kernel(): pl.pallas_call(body, in_specs=specs, out_specs=[VMEM for _ in shapes], ou...  43.7 us
    ppermute x11, waiting for transfers between devices, along_z(): return lax.ppermute(value, 'patch', pairs)  34.8 us
    ppermute x1, waiting for transfers between devices, around_rows(): return lax.ppermute(value, 'patch', ends + [(b, a) for a, b in ends])  20 us
    ppermute x11, starting transfers between devices, along_z(): return lax.ppermute(value, 'patch', pairs)  16.9 us
    ppermute x2, waiting for transfers between devices, to_next_section(): lax.ppermute(block, 'section', [(i, (i + 1) % count) for i in range(count)])  15.2 us
    ppermute x1, starting transfers between devices, around_rows(): return lax.ppermute(value, 'patch', ends + [(b, a) for a, b in ends])  8.46 us
    ppermute x4, waiting for transfers between devices, along_y(): lax.ppermute(value, 'patch', [(y * Z + z, (y + steps) % Y * Z + z) for y...  5.7 us
    ppermute x4, starting transfers between devices, along_y(): lax.ppermute(value, 'patch', [(y * Z + z, (y + steps) % Y * Z + z) for y...  5.51 us
  transfers between devices with their start and end apart: 21, of which 13 were waited for; matrix products, arithmetic and copies ran while one was open for 1% of the time, Pallas kernels for 25%

profile of v3, /device:TPU:24, one launch (start us, length us, event | category | flops | bytes accessed | tf_op | source)
XLA Modules:
  0.0 165.0 jit_solution(18257676358925163689)
XLA Ops:
  0.0 2.7 %collective-permute-start.11 = (bf16[384,1536]{1,0:T(8,128)(2,1)}, bf16[384,1536]{1,0:T(8,128)(2,1)S(1)}, u32[]{:S(2)}, u32[]{:S(2)}) collective-permute-start(bf16[384,1536]{1,0:T(8,128)(2,1)} %bitcast.15), channel_id=1, source_target_pairs={{7,15},{15,23},{23,31},{8,0},{16,8},{24,16},{39,47},{47,55},{55,63... | collective-permute-start | bytes 3538952 | tf_op jit(solution)/shard_map/ppermute | solution.py:57
  2.7 1.0 pad_maximum_fusion.refs_2_
  3.7 0.1 collective-permute-start
  3.8 4.5 %collective-permute-start.3 = (bf16[96,1536]{1,0:T(8,128)(2,1)S(1)}, bf16[96,1536]{1,0:T(8,128)(2,1)S(1)}, u32[]{:S(2)}, u32[]{:S(2)}) collective-permute-start(bf16[96,1536]{1,0:T(8,128)(2,1)S(1)} %pad_maximum_fusion.refs_2_), channel_id=1, source_target_pairs={{0,7},{1,0},{2,1},{3,2},{4,3},{5,4},{6,5},{7,6},{8,15},{9,8},{10,9... | collective-permute-start | bytes 884744 | tf_op jit(solution)/shard_map/ppermute | solution.py:31
  8.3 6.9 %collective-permute-done.refs_1_ = bf16[96,1536]{1,0:T(8,128)(2,1)S(1)} collective-permute-done((bf16[96,1536]{1,0:T(8,128)(2,1)S(1)}, bf16[96,1536]{1,0:T(8,128)(2,1)S(1)}, u32[]{:S(2)}, u32[]{:S(2)}) %collective-permute-start) | collective-permute-done | bytes 294944 | tf_op jit(solution)/shard_map/ppermute | solution.py:31
  15.2 3.2 %collective-permute-start.5 = (bf16[96,1536]{1,0:T(8,128)(2,1)S(1)}, bf16[96,1536]{1,0:T(8,128)(2,1)S(1)}, u32[]{:S(2)}, u32[]{:S(2)}) collective-permute-start(bf16[96,1536]{1,0:T(8,128)(2,1)S(1)} %collective-permute-done.3.refs_3_), channel_id=1, source_target_pairs={{0,7},{1,0},{2,1},{3,2},{4,3},{5,4},{6,5},{7,6},{8,15},{9,8},{10,9... | collective-permute-start | bytes 884744 | tf_op jit(solution)/shard_map/ppermute | solution.py:31
  18.5 6.2 %collective-permute-done.1.refs_0_ = bf16[96,1536]{1,0:T(8,128)(2,1)S(1)} collective-permute-done((bf16[96,1536]{1,0:T(8,128)(2,1)S(1)}, bf16[96,1536]{1,0:T(8,128)(2,1)S(1)}, u32[]{:S(2)}, u32[]{:S(2)}) %collective-permute-start.1) | collective-permute-done | bytes 294944 | tf_op jit(solution)/shard_map/ppermute | solution.py:31
  24.6 0.1 join.2.refs_0_
  24.7 2.0 %collective-permute-start.7 = (bf16[384,1536]{1,0:T(8,128)(2,1)S(1)}, bf16[384,1536]{1,0:T(8,128)(2,1)S(1)}, u32[]{:S(2)}, u32[]{:S(2)}) collective-permute-start(bf16[384,1536]{1,0:T(8,128)(2,1)S(1)} %join.2.refs_0_), channel_id=1, source_target_pairs={{0,8},{1,9},{2,10},{3,11},{4,12},{5,13},{6,14},{7,15},{8,16},{9,17... | collective-permute-start | bytes 3538952 | tf_op jit(solution)/shard_map/ppermute | solution.py:40
  26.7 0.2 collective-permute-start.8
  27.0 3.2 %collective-permute-start.6 = (bf16[96,1536]{1,0:T(8,128)(2,1)S(1)}, bf16[96,1536]{1,0:T(8,128)(2,1)S(1)}, u32[]{:S(2)}, u32[]{:S(2)}) collective-permute-start(bf16[96,1536]{1,0:T(8,128)(2,1)S(1)} %collective-permute-done.5.refs_3_), channel_id=1, source_target_pairs={{0,7},{1,0},{2,1},{3,2},{4,3},{5,4},{6,5},{7,6},{8,15},{9,8},{10,9... | collective-permute-start | bytes 884744 | tf_op jit(solution)/shard_map/ppermute | solution.py:31
  30.2 2.9 %collective-permute-done.2.refs_1_ = bf16[96,1536]{1,0:T(8,128)(2,1)S(1)} collective-permute-done((bf16[96,1536]{1,0:T(8,128)(2,1)S(1)}, bf16[96,1536]{1,0:T(8,128)(2,1)S(1)}, u32[]{:S(2)}, u32[]{:S(2)}) %collective-permute-start.2) | collective-permute-done | bytes 294944 | tf_op jit(solution)/shard_map/ppermute | solution.py:31
  33.1 0.2 broadcast_select_fusion.1
  33.3 1.1 collective-permute-done.6.refs_2_
  34.4 6.6 %collective-permute-done.4.refs_0_ = bf16[96,1536]{1,0:T(8,128)(2,1)S(1)} collective-permute-done((bf16[96,1536]{1,0:T(8,128)(2,1)S(1)}, bf16[96,1536]{1,0:T(8,128)(2,1)S(1)}, u32[]{:S(2)}, u32[]{:S(2)}) %collective-permute-start.4) | collective-permute-done | bytes 294944 | tf_op jit(solution)/shard_map/ppermute | solution.py:31
  41.1 3.2 %collective-permute-start.12 = (bf16[384,1536]{1,0:T(8,128)(2,1)S(1)}, bf16[384,1536]{1,0:T(8,128)(2,1)S(1)}, u32[]{:S(2)}, u32[]{:S(2)}) collective-permute-start(bf16[384,1536]{1,0:T(8,128)(2,1)S(1)} %get-tuple-element.24), channel_id=1, source_target_pairs={{0,7},{1,0},{2,1},{3,2},{4,3},{5,4},{6,5},{7,6},{8,15},{9,8},{10,9... | collective-permute-start | bytes 3538952 | tf_op jit(solution)/shard_map/ppermute | solution.py:31
  45.0 0.1 join.3.refs_3_
  45.1 1.6 collective-permute-start.9
  46.7 7.4 %own_tile.1 = (bf16[5,384,3072]{2,1,0:T(8,128)(2,1)S(1)}, bf16[384,1536]{1,0:T(8,128)(2,1)S(1)}, bf16[1536,3072]{1,0:T(8,128)(2,1)S(1)}) custom-call(bf16[384,1536]{1,0:T(8,128)(2,1)} %bitcast.16, f32[2,1536]{1,0:T(2,128)S(1)} %bitcast.19, bf16[1536,3072]{1,0:T(8,128)(2,1)} %bitcast.31, f32[1,1536]{1,0:T(1,128)S(1)} %get-tuple-element.40.gain_ref), custom_call_target="tpu_custom_call" | custom-call | flops 3623878656 | bytes 10635264 | tf_op jit(solution)/shard_map/own_tile/pallas_call | solution.py:87
  54.2 1.6 collective-permute-start.10
  55.8 10.9 %collective-permute-done.13.x_ref = bf16[384,1536]{1,0:T(8,128)(2,1)S(1)} collective-permute-done((bf16[384,1536]{1,0:T(8,128)(2,1)S(1)}, bf16[384,1536]{1,0:T(8,128)(2,1)S(1)}, u32[]{:S(2)}, u32[]{:S(2)}) %collective-permute-start.13) | collective-permute-done | bytes 1179680 | tf_op jit(solution)/shard_map/ppermute | solution.py:31
  66.7 1.4 collective-permute-start.17
  68.1 1.3 collective-permute-start.16
  69.4 0.6 near_tile.4._
  70.0 5.6 %near_tile.5._ = bf16[5,384,3072]{2,1,0:T(8,128)(2,1)S(1)} custom-call(s32[1]{0:T(128)} %bitcast.at_ref, s32[4]{0:T(128)S(1)} %bitcast.25, s32[1]{0:T(128)S(6)} %copy.18.live_ref, bf16[384,1536]{1,0:T(8,128)(2,1)S(1)} %collective-permute-done.12.x_ref, f32[2,1536]{1,0:T(2,128)S(1)} %bitcast.21, ...), custom_call_target="tpu_custom_call", output_to_operand_aliasing={{}: (7, {})} | custom-call | flops 3623878656 | bytes 22431768 | tf_op jit(solution)/shard_map/near_tile/pallas_call | solution.py:87
  75.6 0.1 broadcast_select_fusion.3
  75.7 0.6 collective-permute-done.9.refs_1_.refs_4_
  76.3 5.1 %collective-permute-done.10.refs_3_.refs_5_ = bf16[384,1536]{1,0:T(8,128)(2,1)S(1)} collective-permute-done((bf16[384,1536]{1,0:T(8,128)(2,1)S(1)}, bf16[384,1536]{1,0:T(8,128)(2,1)S(1)}, u32[]{:S(2)}, u32[]{:S(2)}) %collective-permute-start.10) | collective-permute-done | bytes 1179680 | tf_op jit(solution)/shard_map/ppermute | solution.py:40
  81.4 8.5 %collective-permute-start.15 = (bf16[384,1536]{1,0:T(8,128)(2,1)S(1)}, bf16[384,1536]{1,0:T(8,128)(2,1)S(1)}, u32[]{:S(2)}, u32[]{:S(2)}) collective-permute-start(bf16[384,1536]{1,0:T(8,128)(2,1)S(1)} %broadcast_select_fusion.3), channel_id=1, source_target_pairs={{7,8},{15,16},{23,24},{8,7},{16,15},{24,23},{39,40},{47,48},{55,56... | collective-permute-start | bytes 3538952 | tf_op jit(solution)/shard_map/ppermute | solution.py:36
  89.9 0.2 onward.1
  90.0 0.5 collective-permute-start.14
  90.6 2.8 %collective-permute-start.18 = (bf16[384,1536]{1,0:T(8,128)(2,1)S(1)}, bf16[384,1536]{1,0:T(8,128)(2,1)S(1)}, u32[]{:S(2)}, u32[]{:S(2)}) collective-permute-start(bf16[384,1536]{1,0:T(8,128)(2,1)S(1)} %get-tuple-element.34), channel_id=1, source_target_pairs={{0,8},{1,9},{2,10},{3,11},{4,28},{5,29},{6,30},{7,31},{8,16},{9,17... | collective-permute-start | bytes 3538952 | tf_op jit(solution)/shard_map/ppermute | solution.py:51
  93.4 0.2 collective-permute-done.16
  93.5 20.0 %collective-permute-done.15 = bf16[384,1536]{1,0:T(8,128)(2,1)S(1)} collective-permute-done((bf16[384,1536]{1,0:T(8,128)(2,1)S(1)}, bf16[384,1536]{1,0:T(8,128)(2,1)S(1)}, u32[]{:S(2)}, u32[]{:S(2)}) %collective-permute-start.15) | collective-permute-done | bytes 1179680 | tf_op jit(solution)/shard_map/ppermute | solution.py:36
  113.5 0.2 broadcast_select_fusion.2
  113.7 2.6 %collective-permute-done.14.refs_6_ = bf16[384,1536]{1,0:T(8,128)(2,1)S(1)} collective-permute-done((bf16[384,1536]{1,0:T(8,128)(2,1)S(1)}, bf16[384,1536]{1,0:T(8,128)(2,1)S(1)}, u32[]{:S(2)}, u32[]{:S(2)}) %collective-permute-start.14) | collective-permute-done | bytes 1179680 | tf_op jit(solution)/shard_map/ppermute | solution.py:51
  116.3 2.5 %project_query.1.q_ref = bf16[384,1536]{1,0:T(8,128)(2,1)S(1)} custom-call(s32[1]{0:T(128)} %bitcast.at_ref, bf16[384,1536]{1,0:T(8,128)(2,1)S(1)} %get-tuple-element.22.normed_ref, f32[1,1536]{1,0:T(1,128)S(1)} %get-tuple-element.39.gain_ref, bf16[384,1536]{1,0:T(8,128)(2,1)S(1)} %join.2.refs_0_, ...), custom_call_target="tpu_custom_call" | custom-call | flops 1811939328 | bytes 9443332 | tf_op jit(solution)/shard_map/project_query/pallas_call | solution.py:87
  118.9 5.6 %near_tile.6._ = bf16[5,384,3072]{2,1,0:T(8,128)(2,1)S(1)} custom-call(s32[1]{0:T(128)} %bitcast.at_ref, s32[4]{0:T(128)S(1)} %bitcast.26, s32[1]{0:T(128)S(6)} %copy.18.live_ref, bf16[384,1536]{1,0:T(8,128)(2,1)S(1)} %get-tuple-element.37.x_ref, f32[2,1536]{1,0:T(2,128)S(1)} %bitcast.22, ...), custom_call_target="tpu_custom_call", output_to_operand_aliasing={{}: (7, {})} | custom-call | flops 3623878656 | bytes 22431768 | tf_op jit(solution)/shard_map/near_tile/pallas_call | solution.py:87
  124.5 5.8 %near_tile.7.window_ref = bf16[5,384,3072]{2,1,0:T(8,128)(2,1)S(1)} custom-call(s32[1]{0:T(128)} %bitcast.at_ref, s32[4]{0:T(128)S(1)} %bitcast.27, s32[1]{0:T(128)S(6)} %copy.18.live_ref, bf16[384,1536]{1,0:T(8,128)(2,1)S(1)} %get-tuple-element.38.x_ref, f32[2,1536]{1,0:T(2,128)S(1)} %bitcast.23, ...), custom_call_target="tpu_custom_call", output_to_operand_aliasing={{}: (7, {})} | custom-call | flops 3623878656 | bytes 22431768 | tf_op jit(solution)/shard_map/near_tile/pallas_call | solution.py:87
  130.3 13.3 %attend.1.a_ref = bf16[384,1536]{1,0:T(8,128)(2,1)S(1)} custom-call(s32[1]{0:T(128)} %bitcast.at_ref, s32[4]{0:T(128)S(1)} %bitcast.28, s32[1]{0:T(128)S(6)} %copy.18.live_ref, bf16[384,1536]{1,0:T(8,128)(2,1)S(1)} %project_query.1.q_ref, bf16[5,384,3072]{2,1,0:T(8,128)(2,1)S(1)} %near_tile.7.window_ref), custom_call_target="tpu_custom_call" | custom-call | flops 3623878656 | bytes 12976152 | tf_op jit(solution)/shard_map/attend/pallas_call | solution.py:87
  143.6 0.4 whole_out.1.w_ref
  144.0 0.8 copy-done.1
  144.8 1.1 project_out.3
  145.9 1.1 project_out.2
  147.1 1.6 collective-permute-start.19
  148.7 8.9 %collective-permute-done.20 = bf16[192,1536]{1,0:T(8,128)(2,1)S(1)} collective-permute-done((bf16[192,1536]{1,0:T(8,128)(2,1)S(1)}, bf16[192,1536]{1,0:T(8,128)(2,1)S(1)}, u32[]{:S(2)}, u32[]{:S(2)}) %collective-permute-start.20) | collective-permute-done | bytes 589856 | tf_op jit(solution)/shard_map/ppermute | solution.py:62
  157.6 6.3 %collective-permute-done.19 = bf16[192,1536]{1,0:T(8,128)(2,1)S(1)} collective-permute-done((bf16[192,1536]{1,0:T(8,128)(2,1)S(1)}, bf16[192,1536]{1,0:T(8,128)(2,1)S(1)}, u32[]{:S(2)}, u32[]{:S(2)}) %collective-permute-start.19) | collective-permute-done | bytes 589856 | tf_op jit(solution)/shard_map/ppermute | solution.py:62
  163.9 1.1 maximum_bitcast_fusion
  (25 shorter events, 0.1 us)
Async XLA Ops:
  0.0 33.1 %collective-permute-start.11 = (bf16[384,1536]{1,0:T(8,128)(2,1)}, bf16[384,1536]{1,0:T(8,128)(2,1)S(1)}, u32[]{:S(2)}, u32[]{:S(2)}) collective-permute-start(bf16[384,1536]{1,0:T(8,128)(2,1)} %bitcast.15), channel_id=1, source_target_pairs={{7,15},{15,23},{23,31},{8,0},{16,8},{24,16},{39,47},{47,55},{55,63... | collective-permute-start | bytes 3538952 | tf_op jit(solution)/shard_map/ppermute | solution.py:57
  3.7 11.5 %collective-permute-start = (bf16[96,1536]{1,0:T(8,128)(2,1)S(1)}, bf16[96,1536]{1,0:T(8,128)(2,1)S(1)}, u32[]{:S(2)}, u32[]{:S(2)}) collective-permute-start(bf16[96,1536]{1,0:T(8,128)(2,1)S(1)} %pad_maximum_fusion.refs_2_), channel_id=1, source_target_pairs={{0,1},{1,2},{2,3},{3,4},{4,5},{5,6},{6,7},{7,0},{8,9},{9,10},{10,1... | collective-permute-start | bytes 884744 | tf_op jit(solution)/shard_map/ppermute | solution.py:31
  3.8 11.4 %collective-permute-start.3 = (bf16[96,1536]{1,0:T(8,128)(2,1)S(1)}, bf16[96,1536]{1,0:T(8,128)(2,1)S(1)}, u32[]{:S(2)}, u32[]{:S(2)}) collective-permute-start(bf16[96,1536]{1,0:T(8,128)(2,1)S(1)} %pad_maximum_fusion.refs_2_), channel_id=1, source_target_pairs={{0,7},{1,0},{2,1},{3,2},{4,3},{5,4},{6,5},{7,6},{8,15},{9,8},{10,9... | collective-permute-start | bytes 884744 | tf_op jit(solution)/shard_map/ppermute | solution.py:31
  15.2 9.4 %collective-permute-start.1 = (bf16[96,1536]{1,0:T(8,128)(2,1)S(1)}, bf16[96,1536]{1,0:T(8,128)(2,1)S(1)}, u32[]{:S(2)}, u32[]{:S(2)}) collective-permute-start(bf16[96,1536]{1,0:T(8,128)(2,1)S(1)} %collective-permute-done.refs_1_), channel_id=1, source_target_pairs={{0,1},{1,2},{2,3},{3,4},{4,5},{5,6},{6,7},{7,0},{8,9},{9,10},{10,1... | collective-permute-start | bytes 884744 | tf_op jit(solution)/shard_map/ppermute | solution.py:31
  15.2 11.7 %collective-permute-start.5 = (bf16[96,1536]{1,0:T(8,128)(2,1)S(1)}, bf16[96,1536]{1,0:T(8,128)(2,1)S(1)}, u32[]{:S(2)}, u32[]{:S(2)}) collective-permute-start(bf16[96,1536]{1,0:T(8,128)(2,1)S(1)} %collective-permute-done.3.refs_3_), channel_id=1, source_target_pairs={{0,7},{1,0},{2,1},{3,2},{4,3},{5,4},{6,5},{7,6},{8,15},{9,8},{10,9... | collective-permute-start | bytes 884744 | tf_op jit(solution)/shard_map/ppermute | solution.py:31
  24.6 8.5 %collective-permute-start.2 = (bf16[96,1536]{1,0:T(8,128)(2,1)S(1)}, bf16[96,1536]{1,0:T(8,128)(2,1)S(1)}, u32[]{:S(2)}, u32[]{:S(2)}) collective-permute-start(bf16[96,1536]{1,0:T(8,128)(2,1)S(1)} %collective-permute-done.1.refs_0_), channel_id=1, source_target_pairs={{0,1},{1,2},{2,3},{3,4},{4,5},{5,6},{6,7},{7,0},{8,9},{9,10},{10,1... | collective-permute-start | bytes 884744 | tf_op jit(solution)/shard_map/ppermute | solution.py:31
  24.6 8.5 %copy-start = (bf16[1,1,384,1536]{3,2,1,0:T(8,128)(2,1)S(1)}, bf16[1,1,384,1536]{3,2,1,0:T(8,128)(2,1)}, u32[]{:S(2)}) copy-start(bf16[1,1,384,1536]{3,2,1,0:T(8,128)(2,1)} %param.9) | copy-start | bytes 3538948
  24.7 20.2 %copy-start.5 = (f32[1,2,1536]{2,1,0:T(2,128)S(1)}, f32[1,2,1536]{2,1,0:T(2,128)}, u32[]{:S(2)}) copy-start(f32[1,2,1536]{2,1,0:T(2,128)} %param.15) | copy-start | bytes 36868
  24.7 29.4 %collective-permute-start.7 = (bf16[384,1536]{1,0:T(8,128)(2,1)S(1)}, bf16[384,1536]{1,0:T(8,128)(2,1)S(1)}, u32[]{:S(2)}, u32[]{:S(2)}) collective-permute-start(bf16[384,1536]{1,0:T(8,128)(2,1)S(1)} %join.2.refs_0_), channel_id=1, source_target_pairs={{0,8},{1,9},{2,10},{3,11},{4,12},{5,13},{6,14},{7,15},{8,16},{9,17... | collective-permute-start | bytes 3538952 | tf_op jit(solution)/shard_map/ppermute | solution.py:40
  26.7 27.5 %collective-permute-start.8 = (bf16[384,1536]{1,0:T(8,128)(2,1)S(1)}, bf16[384,1536]{1,0:T(8,128)(2,1)S(1)}, u32[]{:S(2)}, u32[]{:S(2)}) collective-permute-start(bf16[384,1536]{1,0:T(8,128)(2,1)S(1)} %join.2.refs_0_), channel_id=1, source_target_pairs={{0,24},{1,25},{2,26},{3,27},{4,28},{5,29},{6,30},{7,31},{8,0},{9,1... | collective-permute-start | bytes 3538952 | tf_op jit(solution)/shard_map/ppermute | solution.py:40
  27.0 7.5 %collective-permute-start.6 = (bf16[96,1536]{1,0:T(8,128)(2,1)S(1)}, bf16[96,1536]{1,0:T(8,128)(2,1)S(1)}, u32[]{:S(2)}, u32[]{:S(2)}) collective-permute-start(bf16[96,1536]{1,0:T(8,128)(2,1)S(1)} %collective-permute-done.5.refs_3_), channel_id=1, source_target_pairs={{0,7},{1,0},{2,1},{3,2},{4,3},{5,4},{6,5},{7,6},{8,15},{9,8},{10,9... | collective-permute-start | bytes 884744 | tf_op jit(solution)/shard_map/ppermute | solution.py:31
  33.1 7.9 %collective-permute-start.4 = (bf16[96,1536]{1,0:T(8,128)(2,1)S(1)}, bf16[96,1536]{1,0:T(8,128)(2,1)S(1)}, u32[]{:S(2)}, u32[]{:S(2)}) collective-permute-start(bf16[96,1536]{1,0:T(8,128)(2,1)S(1)} %collective-permute-done.2.refs_1_), channel_id=1, source_target_pairs={{0,1},{1,2},{2,3},{3,4},{4,5},{5,6},{6,7},{7,0},{8,9},{9,10},{10,1... | collective-permute-start | bytes 884744 | tf_op jit(solution)/shard_map/ppermute | solution.py:31
  41.1 25.7 %collective-permute-start.13 = (bf16[384,1536]{1,0:T(8,128)(2,1)S(1)}, bf16[384,1536]{1,0:T(8,128)(2,1)S(1)}, u32[]{:S(2)}, u32[]{:S(2)}) collective-permute-start(bf16[384,1536]{1,0:T(8,128)(2,1)S(1)} %get-tuple-element.26), channel_id=1, source_target_pairs={{0,1},{1,2},{2,3},{3,4},{4,5},{5,6},{6,7},{7,0},{8,9},{9,10},{10,1... | collective-permute-start | bytes 3538952 | tf_op jit(solution)/shard_map/ppermute | solution.py:31
  41.1 27.0 %collective-permute-start.12 = (bf16[384,1536]{1,0:T(8,128)(2,1)S(1)}, bf16[384,1536]{1,0:T(8,128)(2,1)S(1)}, u32[]{:S(2)}, u32[]{:S(2)}) collective-permute-start(bf16[384,1536]{1,0:T(8,128)(2,1)S(1)} %get-tuple-element.24), channel_id=1, source_target_pairs={{0,7},{1,0},{2,1},{3,2},{4,3},{5,4},{6,5},{7,6},{8,15},{9,8},{10,9... | collective-permute-start | bytes 3538952 | tf_op jit(solution)/shard_map/ppermute | solution.py:31
  45.0 1.7 %copy-start.2 = (f32[1,2,1536]{2,1,0:T(2,128)S(1)}, f32[1,2,1536]{2,1,0:T(2,128)}, u32[]{:S(2)}) copy-start(f32[1,2,1536]{2,1,0:T(2,128)} %param.10) | copy-start | bytes 36868
  45.1 31.3 %collective-permute-start.9 = (bf16[384,1536]{1,0:T(8,128)(2,1)S(1)}, bf16[384,1536]{1,0:T(8,128)(2,1)S(1)}, u32[]{:S(2)}, u32[]{:S(2)}) collective-permute-start(bf16[384,1536]{1,0:T(8,128)(2,1)S(1)} %join.3.refs_3_), channel_id=1, source_target_pairs={{0,8},{1,9},{2,10},{3,11},{4,12},{5,13},{6,14},{7,15},{8,16},{9,17... | collective-permute-start | bytes 3538952 | tf_op jit(solution)/shard_map/ppermute | solution.py:40
  46.7 22.7 %copy-start.4 = (s32[1,4]{1,0:T(1,128)S(1)}, s32[1,4]{1,0:T(1,128)}, u32[]{:S(2)}) copy-start(s32[1,4]{1,0:T(1,128)} %param.16) | copy-start | bytes 52
  54.2 27.2 %collective-permute-start.10 = (bf16[384,1536]{1,0:T(8,128)(2,1)S(1)}, bf16[384,1536]{1,0:T(8,128)(2,1)S(1)}, u32[]{:S(2)}, u32[]{:S(2)}) collective-permute-start(bf16[384,1536]{1,0:T(8,128)(2,1)S(1)} %join.3.refs_3_), channel_id=1, source_target_pairs={{0,24},{1,25},{2,26},{3,27},{4,28},{5,29},{6,30},{7,31},{8,0},{9,1... | collective-permute-start | bytes 3538952 | tf_op jit(solution)/shard_map/ppermute | solution.py:40
  66.7 26.6 %collective-permute-start.17 = (bf16[384,1536]{1,0:T(8,128)(2,1)S(1)}, bf16[384,1536]{1,0:T(8,128)(2,1)S(1)}, u32[]{:S(2)}, u32[]{:S(2)}) collective-permute-start(bf16[384,1536]{1,0:T(8,128)(2,1)S(1)} %collective-permute-done.13.x_ref), channel_id=1, source_target_pairs={{0,1},{1,2},{2,3},{3,4},{4,5},{5,6},{6,7},{8,9},{9,10},{10,11},{11... | collective-permute-start | bytes 3538952 | tf_op jit(solution)/shard_map/ppermute | solution.py:31
  68.1 25.4 %collective-permute-start.16 = (bf16[384,1536]{1,0:T(8,128)(2,1)S(1)}, bf16[384,1536]{1,0:T(8,128)(2,1)S(1)}, u32[]{:S(2)}, u32[]{:S(2)}) collective-permute-start(bf16[384,1536]{1,0:T(8,128)(2,1)S(1)} %collective-permute-done.12.x_ref), channel_id=1, source_target_pairs={{1,0},{2,1},{3,2},{4,3},{5,4},{6,5},{7,6},{9,8},{10,9},{11,10},{12... | collective-permute-start | bytes 3538952 | tf_op jit(solution)/shard_map/ppermute | solution.py:31
  81.4 32.1 %collective-permute-start.15 = (bf16[384,1536]{1,0:T(8,128)(2,1)S(1)}, bf16[384,1536]{1,0:T(8,128)(2,1)S(1)}, u32[]{:S(2)}, u32[]{:S(2)}) collective-permute-start(bf16[384,1536]{1,0:T(8,128)(2,1)S(1)} %broadcast_select_fusion.3), channel_id=1, source_target_pairs={{7,8},{15,16},{23,24},{8,7},{16,15},{24,23},{39,40},{47,48},{55,56... | collective-permute-start | bytes 3538952 | tf_op jit(solution)/shard_map/ppermute | solution.py:36
  90.0 26.3 %collective-permute-start.14 = (bf16[384,1536]{1,0:T(8,128)(2,1)S(1)}, bf16[384,1536]{1,0:T(8,128)(2,1)S(1)}, u32[]{:S(2)}, u32[]{:S(2)}) collective-permute-start(bf16[384,1536]{1,0:T(8,128)(2,1)S(1)} %get-tuple-element.32), channel_id=1, source_target_pairs={{0,24},{1,25},{2,26},{3,27},{4,12},{5,13},{6,14},{7,15},{8,0},{9,1... | collective-permute-start | bytes 3538952 | tf_op jit(solution)/shard_map/ppermute | solution.py:51
  90.6 53.0 %collective-permute-start.18 = (bf16[384,1536]{1,0:T(8,128)(2,1)S(1)}, bf16[384,1536]{1,0:T(8,128)(2,1)S(1)}, u32[]{:S(2)}, u32[]{:S(2)}) collective-permute-start(bf16[384,1536]{1,0:T(8,128)(2,1)S(1)} %get-tuple-element.34), channel_id=1, source_target_pairs={{0,8},{1,9},{2,10},{3,11},{4,28},{5,29},{6,30},{7,31},{8,16},{9,17... | collective-permute-start | bytes 3538952 | tf_op jit(solution)/shard_map/ppermute | solution.py:51
  143.5 1.3 copy-start.1
  143.5 1.3 copy-start.3
  147.1 10.5 %collective-permute-start.20 = (bf16[192,1536]{1,0:T(8,128)(2,1)S(1)}, bf16[192,1536]{1,0:T(8,128)(2,1)S(1)}, u32[]{:S(2)}, u32[]{:S(2)}) collective-permute-start(bf16[192,1536]{1,0:T(8,128)(2,1)S(1)} %project_out.3), channel_id=1, source_target_pairs={{0,32},{32,64},{64,96},{96,128},{128,160},{160,192},{192,224},{224... | collective-permute-start | bytes 1769480 | tf_op jit(solution)/shard_map/ppermute | solution.py:62
  147.1 16.8 %collective-permute-start.19 = (bf16[192,1536]{1,0:T(8,128)(2,1)S(1)}, bf16[192,1536]{1,0:T(8,128)(2,1)S(1)}, u32[]{:S(2)}, u32[]{:S(2)}) collective-permute-start(bf16[192,1536]{1,0:T(8,128)(2,1)S(1)} %project_out.2), channel_id=1, source_target_pairs={{0,32},{32,64},{64,96},{96,128},{128,160},{160,192},{192,224},{224... | collective-permute-start | bytes 1769480 | tf_op jit(solution)/shard_map/ppermute | solution.py:62

commit v4 on v3

--- a/solution.py
+++ b/solution.py
@@ -42,12 +42,8 @@
     )
 
 
-def along_y_by_half(value, steps):
-    pairs = [
-        (y * Z + z, ((y + (steps if z < Z // 2 else -steps)) % Y) * Z + z)
-        for y in range(Y)
-        for z in range(Z)
-    ]
+def along_y_by_place(value, steps):
+    pairs = [(y * Z + z, ((y + steps[z]) % Y) * Z + z) for y in range(Y) for z in range(Z)]
     return lax.ppermute(value, "patch", pairs)
 
 
@@ -152,12 +148,19 @@
     def body(
         at_ref, list_ref, live_ref, x_ref, modulation_ref, w_ref, gain_ref, _, window_ref, normed
     ):
+        own_z = at_ref[0] % Z
+        if place is None:
+            spot = jnp.where(own_z == 0, 2, 3)
+            offset = jnp.where(own_z == 0, OFFSETS[2], OFFSETS[3])
+            here = (own_z == 0) | (own_z == Z - 1)
+        else:
+            spot, offset = place, OFFSETS[place]
+            here = {0: True, 1: True, 2: own_z != 0, 3: own_z != Z - 1}[place]
         named = False
         for j in range(1, NB):
-            hit = (list_ref[j] - at_ref[0] == OFFSETS[place]) & (live_ref[0] > j)
-            named = named | hit
-
-        @pl.when(named)
+            named = named | ((list_ref[j] - at_ref[0] == offset) & (live_ref[0] > j))
+
+        @pl.when(named & here)
         def _():
             normed[...] = norm_rows(x_ref[...], modulation_ref)
 
@@ -165,10 +168,10 @@
             def _(j):
                 cols = pl.ds(pl.multiple_of(j * COLS, COLS), COLS)
                 raw = jnp.dot(normed[...], w_ref[:, cols], preferred_element_type=jnp.float32)
-                window_ref[place, :, cols] = head_norm(raw, gain_ref[:, cols])
+                window_ref[spot, :, cols] = head_norm(raw, gain_ref[:, cols])
                 cols = pl.ds(pl.multiple_of(wide // 2 + j * COLS, COLS), COLS)
                 raw = jnp.dot(normed[...], w_ref[:, cols], preferred_element_type=jnp.float32)
-                window_ref[place, :, cols] = raw.astype(jnp.bfloat16)
+                window_ref[spot, :, cols] = raw.astype(jnp.bfloat16)
 
     shapes = [jax.ShapeDtypeStruct(window.shape, window.dtype)]
     specs = [SMEM] * 3 + [VMEM] * 5
@@ -195,28 +198,35 @@
 
 
 def onward(at, lows, highs):
-    rows, width = lows[0].shape
-    half = rows // 2
+    width = lows[0].shape[1]
+    halves = [low.shape[0] // 2 for low in lows]
+    begins = [sum(halves[:k]) for k in range(len(halves))]
     count = len(lows)
 
     def body(at_ref, *refs):
-        low_refs, high_refs, (query_ref, out_ref) = (
-            refs[:count],
-            refs[count : 2 * count],
-            refs[2 * count :],
-        )
-        for left, query_from, out_from in (
-            (True, high_refs, low_refs),
-            (False, low_refs, high_refs),
-        ):
-
-            @pl.when((at_ref[0] % Z < Z // 2) == left)
-            def _(query_from=query_from, out_from=out_from):
-                for k in range(count):
-                    query_ref[k * half : (k + 1) * half, :] = query_from[k][:half, :]
-                    out_ref[k * half : (k + 1) * half, :] = out_from[k][half:, :]
-
-    shapes = [jax.ShapeDtypeStruct((count * half, width), lows[0].dtype)] * 2
+        low_refs, high_refs = refs[:count], refs[count : 2 * count]
+        query_ref, out_refs = refs[2 * count], refs[2 * count + 1 :]
+        own_z = at_ref[0] % Z
+        left = own_z < Z // 2
+        right = jnp.logical_not(left)
+        end = (own_z == 0) | (own_z == Z - 1)
+        for pick, source in ((left, high_refs), (right, low_refs)):
+
+            @pl.when(pick)
+            def _(source=source):
+                for k, (begin, half) in enumerate(zip(begins, halves, strict=True)):
+                    query_ref[begin : begin + half, :] = source[k][:half, :]
+
+        for k, half in enumerate(halves):
+            from_low = left if k < count - 1 else left != end
+            for pick, source in ((from_low, low_refs), (jnp.logical_not(from_low), high_refs)):
+
+                @pl.when(pick)
+                def _(k=k, half=half, source=source):
+                    out_refs[k][...] = source[k][half:, :]
+
+    sizes = [sum(halves), *halves]
+    shapes = [jax.ShapeDtypeStruct((n, width), lows[0].dtype) for n in sizes]
     specs = [SMEM] + [VMEM] * (2 * count)
     return kernel(body, "onward", specs, shapes, [], {}, 1, SMALL, [at, *lows, *highs])
 
@@ -315,7 +325,7 @@
                     head(2 * pair + 1, places)
 
     shapes = [jax.ShapeDtypeStruct((rows, inner), jnp.bfloat16)]
-    flops = 4 * NB * rows * rows * inner
+    flops = 4 * rows * NB * window.shape[1] * inner
     operands = [*scalars, query, window]
     specs = [SMEM] * 3 + [VMEM] * 2
     return kernel(body, "attend", specs, shapes, [], {}, flops, LARGE, operands)[0]
@@ -348,19 +358,19 @@
     gains = qk_gain[0]
 
     shard = jnp.concatenate([w_query[0], w_out[0]], axis=0)
-    zs_a, zs_b = [-2, -1, 0, 1], [-4, -3, 3, 2]
+    zs_a, zs_b = [-2, -1, 0, 1, 2], [-4, -3, 3]
     up, down = [shard], [shard]
     for k in range(1, 3):
         up.append(along_z(up[-1], 1))
         down.append(along_z(down[-1], -1))
     crossed = across_rows(x)
     own_z = at[0] % Z
-    block_a = join([up[2], up[1], shard, down[1]])
+    block_a = join([up[2], up[1], shard, down[1], down[2]])
     low_a, high_a = along_y(block_a, 1), along_y(block_a, -1)
     up.append(along_z(up[2], 1))
     down.append(along_z(down[2], -1))
     up.append(along_z(after(up[3], block_a), 1))
-    block_b = join([up[4], up[3], down[3], down[2]])
+    block_b = join([up[4], up[3], down[3]])
     x_up = after(jnp.where(own_z == Z - 1, crossed, x), up[4], down[3])
     x_down = after(jnp.where(own_z == 0, crossed, x), up[4], down[3])
     low1, high1 = along_z(x_up, 1), along_z(x_down, -1)
@@ -376,26 +386,30 @@
     low_b, high_b, window = lax.optimization_barrier((low_b, high_b, window))
     edge = after(jnp.where(own_z == 0, high1, low1), low_b)
     edge_far = around_rows(edge)
-    query_on, out_on = onward(at, [low_a, after(low_b, edge)], [high_a, high_b])
-    query_far = along_y_by_half(query_on, -1)
-    out_far = along_y_by_half(out_on, 1)
+    query_on, out_on_a, out_on_b = onward(at, [low_a, after(low_b, edge)], [high_a, high_b])
+    query_far = along_y_by_place(query_on, [-1] * (Z // 2) + [1] * (Z // 2))
+    out_far_a = along_y_by_place(out_on_a, [1] * (Z // 2) + [-1] * (Z // 2))
+    out_far_b = along_y_by_place(
+        out_on_b, [-1] + [1] * (Z // 2 - 1) + [-1] * (Z // 2 - 1) + [1]
+    )
+    window = add_tile(add_tile(window, 2, low2), 3, high2)
     near_blocks = [block_a, low_a, high_a, block_b, low_b, high_b]
     sides = [(dy, zs) for zs in (zs_a, zs_b) for dy in (0, Y - 1, 1)]
-    half = len(zs_a) * size
     query_plan = [(dy, zs, 0) for dy, zs in sides] + [(2, zs_a + zs_b, 0)]
-    out_plan = [(dy, zs, half) for dy, zs in sides] + [(2, zs_a + zs_b, 0)]
+    out_plan = [(dy, zs, len(zs) * size) for dy, zs in sides] + [(2, zs_a, 0), (2, zs_b, 0)]
     query_pieces = near_blocks + [query_far]
-    out_pieces = near_blocks + [out_far]
-
-    window = add_tile(window, 2, jnp.where(own_z == 0, edge_far, low2))
-    window = add_tile(window, 3, jnp.where(own_z == Z - 1, edge_far, high2))
+    out_pieces = near_blocks + [out_far_a, out_far_b]
+
     query = project_query(at, normed, gains[0:1], query_pieces, query_plan)
+    query, window, edge_far = lax.optimization_barrier((query, window, edge_far))
+    window = add_tile(window, None, edge_far)
+    attended = attend(scalars, query, window)
+    attended, *out_pieces[-2:] = lax.optimization_barrier((attended, *out_pieces[-2:]))
     out_whole = whole_out(at, out_pieces, out_plan, gains.shape[1])
-    attended = attend(scalars, query, window)
     count = rows // 2
     parts = [
-        to_next_section(project_out(attended, out_whole, gate, x, at_row, count))
-        for at_row in (0, count)
+        to_next_section(project_out(attended, out_whole, gate, x, begin, count))
+        for begin in (0, count)
     ]
     return jnp.concatenate(parts, axis=0)[None, None]
 

time: 164 us -> 156 us (0.951)
  waiting for transfers between devices: 78.4 us -> 67.1 us
  starting transfers between devices: 38.5 us -> 40.3 us
    ppermute x1, waiting for transfers between devices: 20 us -> 1.14 us  [around_rows(): return lax.ppermute(value, 'patch', ends + [(b, a) for a, b in ends])]
    ppermute x2 -> x3, waiting for transfers between devices: 2.65 us -> 10.7 us  [along_y_by_place(): return lax.ppermute(value, 'patch', pairs)]
    ppermute x11, waiting for transfers between devices: 34.8 us -> 28.3 us  [along_z(): return lax.ppermute(value, 'patch', pairs)]
    ppermute x4, waiting for transfers between devices: 5.7 us -> 11.7 us  [along_y(): lax.ppermute(value, 'patch', [(y * Z + z, (y + steps) % Y * Z + z) for y...]
    pallas_call x13 -> x14, Pallas kernels: 43.7 us -> 44.2 us  [kernel(): pl.pallas_call(body, in_specs=specs, out_specs=[VMEM for _ in shapes], ou...]
    ppermute x2 -> x3, starting transfers between devices: 3.31 us -> 3.44 us  [along_y_by_place(): return lax.ppermute(value, 'patch', pairs)]
  transfers between devices with their start and end apart: 21 -> 22, of which waited for: 13 -> 13; matrix products, arithmetic and copies ran while one was open for 1% -> 1% of each run, Pallas kernels for 25% -> 27%
where the time goes in v4:
time: 156 us
  waiting for transfers between devices  67.1 us (43%)
  Pallas kernels  44.2 us (28%)
  starting transfers between devices  40.3 us (26%)
  other arithmetic  2.38 us (2%)
    pallas_call x14, Pallas kernels, kernel(): pl.pallas_call(body, in_specs=specs, out_specs=[VMEM for _ in shapes], ou...  44.2 us
    ppermute x11, waiting for transfers between devices, along_z(): return lax.ppermute(value, 'patch', pairs)  28.3 us
    ppermute x11, starting transfers between devices, along_z(): return lax.ppermute(value, 'patch', pairs)  16.9 us
    ppermute x2, waiting for transfers between devices, to_next_section(): lax.ppermute(block, 'section', [(i, (i + 1) % count) for i in range(count)])  15.2 us
    ppermute x4, waiting for transfers between devices, along_y(): lax.ppermute(value, 'patch', [(y * Z + z, (y + steps) % Y * Z + z) for y...  11.7 us
    ppermute x3, waiting for transfers between devices, along_y_by_place(): return lax.ppermute(value, 'patch', pairs)  10.7 us
    ppermute x1, starting transfers between devices, around_rows(): return lax.ppermute(value, 'patch', ends + [(b, a) for a, b in ends])  9.68 us
    ppermute x4, starting transfers between devices, along_y(): lax.ppermute(value, 'patch', [(y * Z + z, (y + steps) % Y * Z + z) for y...  5.9 us
  transfers between devices with their start and end apart: 22, of which 13 were waited for; matrix products, arithmetic and copies ran while one was open for 1% of the time, Pallas kernels for 27%

profile of v4, /device:TPU:24, one launch (start us, length us, event | category | flops | bytes accessed | tf_op | source)
XLA Modules:
  0.0 155.7 jit_solution(7837230117470133227)
XLA Ops:
  0.0 2.7 %collective-permute-start.11 = (bf16[384,1536]{1,0:T(8,128)(2,1)}, bf16[384,1536]{1,0:T(8,128)(2,1)S(1)}, u32[]{:S(2)}, u32[]{:S(2)}) collective-permute-start(bf16[384,1536]{1,0:T(8,128)(2,1)} %bitcast.15), channel_id=1, source_target_pairs={{7,15},{15,23},{23,31},{8,0},{16,8},{24,16},{39,47},{47,55},{55,63... | collective-permute-start | bytes 3538952 | tf_op jit(solution)/shard_map/ppermute | solution.py:53
  2.7 1.0 pad_maximum_fusion.refs_2_
  3.7 0.1 collective-permute-start
  3.8 4.5 %collective-permute-start.3 = (bf16[96,1536]{1,0:T(8,128)(2,1)S(1)}, bf16[96,1536]{1,0:T(8,128)(2,1)S(1)}, u32[]{:S(2)}, u32[]{:S(2)}) collective-permute-start(bf16[96,1536]{1,0:T(8,128)(2,1)S(1)} %pad_maximum_fusion.refs_2_), channel_id=1, source_target_pairs={{0,7},{1,0},{2,1},{3,2},{4,3},{5,4},{6,5},{7,6},{8,15},{9,8},{10,9... | collective-permute-start | bytes 884744 | tf_op jit(solution)/shard_map/ppermute | solution.py:31
  8.3 6.9 %collective-permute-done.refs_1_ = bf16[96,1536]{1,0:T(8,128)(2,1)S(1)} collective-permute-done((bf16[96,1536]{1,0:T(8,128)(2,1)S(1)}, bf16[96,1536]{1,0:T(8,128)(2,1)S(1)}, u32[]{:S(2)}, u32[]{:S(2)}) %collective-permute-start) | collective-permute-done | bytes 294944 | tf_op jit(solution)/shard_map/ppermute | solution.py:31
  15.2 3.2 %collective-permute-start.4 = (bf16[96,1536]{1,0:T(8,128)(2,1)S(1)}, bf16[96,1536]{1,0:T(8,128)(2,1)S(1)}, u32[]{:S(2)}, u32[]{:S(2)}) collective-permute-start(bf16[96,1536]{1,0:T(8,128)(2,1)S(1)} %collective-permute-done.3.refs_3_), channel_id=1, source_target_pairs={{0,7},{1,0},{2,1},{3,2},{4,3},{5,4},{6,5},{7,6},{8,15},{9,8},{10,9... | collective-permute-start | bytes 884744 | tf_op jit(solution)/shard_map/ppermute | solution.py:31
  18.5 6.2 %collective-permute-done.1.refs_0_ = bf16[96,1536]{1,0:T(8,128)(2,1)S(1)} collective-permute-done((bf16[96,1536]{1,0:T(8,128)(2,1)S(1)}, bf16[96,1536]{1,0:T(8,128)(2,1)S(1)}, u32[]{:S(2)}, u32[]{:S(2)}) %collective-permute-start.1) | collective-permute-done | bytes 294944 | tf_op jit(solution)/shard_map/ppermute | solution.py:31
  24.7 0.1 join.2.refs_0_
  24.8 2.0 %collective-permute-start.7 = (bf16[480,1536]{1,0:T(8,128)(2,1)S(1)}, bf16[480,1536]{1,0:T(8,128)(2,1)S(1)}, u32[]{:S(2)}, u32[]{:S(2)}) collective-permute-start(bf16[480,1536]{1,0:T(8,128)(2,1)S(1)} %join.2.refs_0_), channel_id=1, source_target_pairs={{0,8},{1,9},{2,10},{3,11},{4,12},{5,13},{6,14},{7,15},{8,16},{9,17... | collective-permute-start | bytes 4423688 | tf_op jit(solution)/shard_map/ppermute | solution.py:40
  26.7 0.2 collective-permute-start.8
  27.0 3.2 %collective-permute-start.6 = (bf16[96,1536]{1,0:T(8,128)(2,1)S(1)}, bf16[96,1536]{1,0:T(8,128)(2,1)S(1)}, u32[]{:S(2)}, u32[]{:S(2)}) collective-permute-start(bf16[96,1536]{1,0:T(8,128)(2,1)S(1)} %collective-permute-done.4.refs_4_), channel_id=1, source_target_pairs={{0,7},{1,0},{2,1},{3,2},{4,3},{5,4},{6,5},{7,6},{8,15},{9,8},{10,9... | collective-permute-start | bytes 884744 | tf_op jit(solution)/shard_map/ppermute | solution.py:31
  30.2 2.9 %collective-permute-done.2.refs_1_ = bf16[96,1536]{1,0:T(8,128)(2,1)S(1)} collective-permute-done((bf16[96,1536]{1,0:T(8,128)(2,1)S(1)}, bf16[96,1536]{1,0:T(8,128)(2,1)S(1)}, u32[]{:S(2)}, u32[]{:S(2)}) %collective-permute-start.2) | collective-permute-done | bytes 294944 | tf_op jit(solution)/shard_map/ppermute | solution.py:31
  33.1 0.2 broadcast_select_fusion
  33.3 1.1 collective-permute-done.6.refs_2_
  34.5 6.6 %collective-permute-done.5.refs_0_ = bf16[96,1536]{1,0:T(8,128)(2,1)S(1)} collective-permute-done((bf16[96,1536]{1,0:T(8,128)(2,1)S(1)}, bf16[96,1536]{1,0:T(8,128)(2,1)S(1)}, u32[]{:S(2)}, u32[]{:S(2)}) %collective-permute-start.5) | collective-permute-done | bytes 294944 | tf_op jit(solution)/shard_map/ppermute | solution.py:31
  41.1 3.2 %collective-permute-start.12 = (bf16[384,1536]{1,0:T(8,128)(2,1)S(1)}, bf16[384,1536]{1,0:T(8,128)(2,1)S(1)}, u32[]{:S(2)}, u32[]{:S(2)}) collective-permute-start(bf16[384,1536]{1,0:T(8,128)(2,1)S(1)} %get-tuple-element.31), channel_id=1, source_target_pairs={{0,7},{1,0},{2,1},{3,2},{4,3},{5,4},{6,5},{7,6},{8,15},{9,8},{10,9... | collective-permute-start | bytes 3538952 | tf_op jit(solution)/shard_map/ppermute | solution.py:31
  45.0 1.6 %collective-permute-start.9 = (bf16[288,1536]{1,0:T(8,128)(2,1)S(1)}, bf16[288,1536]{1,0:T(8,128)(2,1)S(1)}, u32[]{:S(2)}, u32[]{:S(2)}) collective-permute-start(bf16[288,1536]{1,0:T(8,128)(2,1)S(1)} %join.3.refs_3_), channel_id=1, source_target_pairs={{0,8},{1,9},{2,10},{3,11},{4,12},{5,13},{6,14},{7,15},{8,16},{9,17... | collective-permute-start | bytes 2654216 | tf_op jit(solution)/shard_map/ppermute | solution.py:40
  46.7 7.4 %own_tile.1 = (bf16[5,384,3072]{2,1,0:T(8,128)(2,1)S(1)}, bf16[384,1536]{1,0:T(8,128)(2,1)S(1)}, bf16[1536,3072]{1,0:T(8,128)(2,1)S(1)}) custom-call(bf16[384,1536]{1,0:T(8,128)(2,1)} %bitcast.16, f32[2,1536]{1,0:T(2,128)S(1)} %bitcast.19, bf16[1536,3072]{1,0:T(8,128)(2,1)} %bitcast.33, f32[1,1536]{1,0:T(1,128)S(1)} %get-tuple-element.52.gain_ref), custom_call_target="tpu_custom_call" | custom-call | flops 3623878656 | bytes 10635264 | tf_op jit(solution)/shard_map/own_tile/pallas_call | solution.py:83
  54.1 6.0 %collective-permute-done.7.refs_0_.refs_1_ = bf16[480,1536]{1,0:T(8,128)(2,1)S(1)} collective-permute-done((bf16[480,1536]{1,0:T(8,128)(2,1)S(1)}, bf16[480,1536]{1,0:T(8,128)(2,1)S(1)}, u32[]{:S(2)}, u32[]{:S(2)}) %collective-permute-start.7) | collective-permute-done | bytes 1474592 | tf_op jit(solution)/shard_map/ppermute | solution.py:40
  60.1 2.0 %collective-permute-start.10 = (bf16[288,1536]{1,0:T(8,128)(2,1)S(1)}, bf16[288,1536]{1,0:T(8,128)(2,1)S(1)}, u32[]{:S(2)}, u32[]{:S(2)}) collective-permute-start(bf16[288,1536]{1,0:T(8,128)(2,1)S(1)} %join.3.refs_3_), channel_id=1, source_target_pairs={{0,24},{1,25},{2,26},{3,27},{4,28},{5,29},{6,30},{7,31},{8,0},{9,1... | collective-permute-start | bytes 2654216 | tf_op jit(solution)/shard_map/ppermute | solution.py:40
  62.1 4.6 %collective-permute-done.13.x_ref = bf16[384,1536]{1,0:T(8,128)(2,1)S(1)} collective-permute-done((bf16[384,1536]{1,0:T(8,128)(2,1)S(1)}, bf16[384,1536]{1,0:T(8,128)(2,1)S(1)}, u32[]{:S(2)}, u32[]{:S(2)}) %collective-permute-start.13) | collective-permute-done | bytes 1179680 | tf_op jit(solution)/shard_map/ppermute | solution.py:31
  66.7 1.4 collective-permute-start.16
  68.1 1.3 collective-permute-start.15
  69.4 0.1 broadcast_select_fusion.1
  69.5 0.6 near_tile.5._
  70.1 5.6 %near_tile.6._ = bf16[5,384,3072]{2,1,0:T(8,128)(2,1)S(1)} custom-call(s32[1]{0:T(128)} %bitcast.at_ref, s32[4]{0:T(128)S(1)} %bitcast.26, s32[1]{0:T(128)S(6)} %copy.20.live_ref, bf16[384,1536]{1,0:T(8,128)(2,1)S(1)} %collective-permute-done.12.x_ref, f32[2,1536]{1,0:T(2,128)S(1)} %bitcast.21, ...), custom_call_target="tpu_custom_call", output_to_operand_aliasing={{}: (7, {})} | custom-call | flops 3623878656 | bytes 22431768 | tf_op jit(solution)/shard_map/near_tile/pallas_call | solution.py:83
  75.7 0.7 collective-permute-done.9.refs_1_.refs_4_
  76.4 5.0 %collective-permute-done.10.refs_3_.refs_5_ = bf16[288,1536]{1,0:T(8,128)(2,1)S(1)} collective-permute-done((bf16[288,1536]{1,0:T(8,128)(2,1)S(1)}, bf16[288,1536]{1,0:T(8,128)(2,1)S(1)}, u32[]{:S(2)}, u32[]{:S(2)}) %collective-permute-start.10) | collective-permute-done | bytes 884768 | tf_op jit(solution)/shard_map/ppermute | solution.py:40
  81.4 0.2 onward.1
  81.6 1.3 collective-permute-start.14
  82.9 9.7 %collective-permute-start.17 = (bf16[384,1536]{1,0:T(8,128)(2,1)S(1)}, bf16[384,1536]{1,0:T(8,128)(2,1)S(1)}, u32[]{:S(2)}, u32[]{:S(2)}) collective-permute-start(bf16[384,1536]{1,0:T(8,128)(2,1)S(1)} %broadcast_select_fusion.1), channel_id=1, source_target_pairs={{7,8},{15,16},{23,24},{8,7},{16,15},{24,23},{39,40},{47,48},{55,56... | collective-permute-start | bytes 3538952 | tf_op jit(solution)/shard_map/ppermute | solution.py:36
  92.6 0.1 collective-permute-start.18
  92.7 2.0 %collective-permute-start.19 = (bf16[144,1536]{1,0:T(8,128)(2,1)S(1)}, bf16[144,1536]{1,0:T(8,128)(2,1)S(1)}, u32[]{:S(2)}, u32[]{:S(2)}) collective-permute-start(bf16[144,1536]{1,0:T(8,128)(2,1)S(1)} %get-tuple-element.45), channel_id=1, source_target_pairs={{0,24},{1,9},{2,10},{3,11},{4,28},{5,29},{6,30},{7,15},{8,0},{9,17... | collective-permute-start | bytes 1327112 | tf_op jit(solution)/shard_map/ppermute | solution.py:47
  94.7 0.6 near_tile.7._
  95.3 5.8 %near_tile.8._ = bf16[5,384,3072]{2,1,0:T(8,128)(2,1)S(1)} custom-call(s32[1]{0:T(128)} %bitcast.at_ref, s32[4]{0:T(128)S(1)} %bitcast.28, s32[1]{0:T(128)S(6)} %copy.20.live_ref, bf16[384,1536]{1,0:T(8,128)(2,1)S(1)} %collective-permute-done.15.x_ref, f32[2,1536]{1,0:T(2,128)S(1)} %bitcast.23, ...), custom_call_target="tpu_custom_call", output_to_operand_aliasing={{}: (7, {})} | custom-call | flops 3623878656 | bytes 22431768 | tf_op jit(solution)/shard_map/near_tile/pallas_call | solution.py:83
  101.1 10.7 %collective-permute-done.14.refs_6_ = bf16[384,1536]{1,0:T(8,128)(2,1)S(1)} collective-permute-done((bf16[384,1536]{1,0:T(8,128)(2,1)S(1)}, bf16[384,1536]{1,0:T(8,128)(2,1)S(1)}, u32[]{:S(2)}, u32[]{:S(2)}) %collective-permute-start.14) | collective-permute-done | bytes 1179680 | tf_op jit(solution)/shard_map/ppermute | solution.py:47
  111.8 2.5 %project_query.1.q_ref = bf16[384,1536]{1,0:T(8,128)(2,1)S(1)} custom-call(s32[1]{0:T(128)} %bitcast.at_ref, bf16[384,1536]{1,0:T(8,128)(2,1)S(1)} %get-tuple-element.29.normed_ref, f32[1,1536]{1,0:T(1,128)S(1)} %get-tuple-element.51.gain_ref, bf16[480,1536]{1,0:T(8,128)(2,1)S(1)} %join.2.refs_0_, ...), custom_call_target="tpu_custom_call" | custom-call | flops 1811939328 | bytes 9443332 | tf_op jit(solution)/shard_map/project_query/pallas_call | solution.py:83
  114.3 1.1 collective-permute-done.17.x_ref
  115.4 5.6 %near_tile.9.window_ref = bf16[5,384,3072]{2,1,0:T(8,128)(2,1)S(1)} custom-call(s32[1]{0:T(128)} %bitcast.at_ref, s32[4]{0:T(128)S(1)} %bitcast.29, s32[1]{0:T(128)S(6)} %copy.20.live_ref, bf16[384,1536]{1,0:T(8,128)(2,1)S(1)} %collective-permute-done.17.x_ref, f32[2,1536]{1,0:T(2,128)S(1)} %bitcast.24, ...), custom_call_target="tpu_custom_call", output_to_operand_aliasing={{}: (7, {})} | custom-call | flops 3623878656 | bytes 22431768 | tf_op jit(solution)/shard_map/near_tile/pallas_call | solution.py:83
  121.0 13.2 %attend.1.a_ref = bf16[384,1536]{1,0:T(8,128)(2,1)S(1)} custom-call(s32[1]{0:T(128)} %bitcast.at_ref, s32[4]{0:T(128)S(1)} %bitcast.30, s32[1]{0:T(128)S(6)} %copy.20.live_ref, bf16[384,1536]{1,0:T(8,128)(2,1)S(1)} %project_query.1.q_ref, bf16[5,384,3072]{2,1,0:T(8,128)(2,1)S(1)} %near_tile.9.window_ref), custom_call_target="tpu_custom_call" | custom-call | flops 3623878656 | bytes 12976152 | tf_op jit(solution)/shard_map/attend/pallas_call | solution.py:83
  134.3 0.4 whole_out.1.w_ref
  134.7 0.8 copy-done.1
  135.6 1.1 project_out.2
  136.7 1.1 project_out.3
  137.8 1.6 %collective-permute-start.21 = (bf16[192,1536]{1,0:T(8,128)(2,1)S(1)}, bf16[192,1536]{1,0:T(8,128)(2,1)S(1)}, u32[]{:S(2)}, u32[]{:S(2)}) collective-permute-start(bf16[192,1536]{1,0:T(8,128)(2,1)S(1)} %project_out.3), channel_id=1, source_target_pairs={{0,32},{32,64},{64,96},{96,128},{128,160},{160,192},{192,224},{224... | collective-permute-start | bytes 1769480 | tf_op jit(solution)/shard_map/ppermute | solution.py:58
  139.4 8.9 %collective-permute-done.20 = bf16[192,1536]{1,0:T(8,128)(2,1)S(1)} collective-permute-done((bf16[192,1536]{1,0:T(8,128)(2,1)S(1)}, bf16[192,1536]{1,0:T(8,128)(2,1)S(1)}, u32[]{:S(2)}, u32[]{:S(2)}) %collective-permute-start.20) | collective-permute-done | bytes 589856 | tf_op jit(solution)/shard_map/ppermute | solution.py:58
  148.3 6.3 %collective-permute-done.21 = bf16[192,1536]{1,0:T(8,128)(2,1)S(1)} collective-permute-done((bf16[192,1536]{1,0:T(8,128)(2,1)S(1)}, bf16[192,1536]{1,0:T(8,128)(2,1)S(1)}, u32[]{:S(2)}, u32[]{:S(2)}) %collective-permute-start.21) | collective-permute-done | bytes 589856 | tf_op jit(solution)/shard_map/ppermute | solution.py:58
  154.6 1.1 maximum_bitcast_fusion
  (27 shorter events, 0.2 us)
Async XLA Ops:
  0.0 33.1 %collective-permute-start.11 = (bf16[384,1536]{1,0:T(8,128)(2,1)}, bf16[384,1536]{1,0:T(8,128)(2,1)S(1)}, u32[]{:S(2)}, u32[]{:S(2)}) collective-permute-start(bf16[384,1536]{1,0:T(8,128)(2,1)} %bitcast.15), channel_id=1, source_target_pairs={{7,15},{15,23},{23,31},{8,0},{16,8},{24,16},{39,47},{47,55},{55,63... | collective-permute-start | bytes 3538952 | tf_op jit(solution)/shard_map/ppermute | solution.py:53
  3.7 11.5 %collective-permute-start = (bf16[96,1536]{1,0:T(8,128)(2,1)S(1)}, bf16[96,1536]{1,0:T(8,128)(2,1)S(1)}, u32[]{:S(2)}, u32[]{:S(2)}) collective-permute-start(bf16[96,1536]{1,0:T(8,128)(2,1)S(1)} %pad_maximum_fusion.refs_2_), channel_id=1, source_target_pairs={{0,1},{1,2},{2,3},{3,4},{4,5},{5,6},{6,7},{7,0},{8,9},{9,10},{10,1... | collective-permute-start | bytes 884744 | tf_op jit(solution)/shard_map/ppermute | solution.py:31
  3.8 11.4 %collective-permute-start.3 = (bf16[96,1536]{1,0:T(8,128)(2,1)S(1)}, bf16[96,1536]{1,0:T(8,128)(2,1)S(1)}, u32[]{:S(2)}, u32[]{:S(2)}) collective-permute-start(bf16[96,1536]{1,0:T(8,128)(2,1)S(1)} %pad_maximum_fusion.refs_2_), channel_id=1, source_target_pairs={{0,7},{1,0},{2,1},{3,2},{4,3},{5,4},{6,5},{7,6},{8,15},{9,8},{10,9... | collective-permute-start | bytes 884744 | tf_op jit(solution)/shard_map/ppermute | solution.py:31
  15.2 9.4 %collective-permute-start.1 = (bf16[96,1536]{1,0:T(8,128)(2,1)S(1)}, bf16[96,1536]{1,0:T(8,128)(2,1)S(1)}, u32[]{:S(2)}, u32[]{:S(2)}) collective-permute-start(bf16[96,1536]{1,0:T(8,128)(2,1)S(1)} %collective-permute-done.refs_1_), channel_id=1, source_target_pairs={{0,1},{1,2},{2,3},{3,4},{4,5},{5,6},{6,7},{7,0},{8,9},{9,10},{10,1... | collective-permute-start | bytes 884744 | tf_op jit(solution)/shard_map/ppermute | solution.py:31
  15.2 9.4 %collective-permute-start.4 = (bf16[96,1536]{1,0:T(8,128)(2,1)S(1)}, bf16[96,1536]{1,0:T(8,128)(2,1)S(1)}, u32[]{:S(2)}, u32[]{:S(2)}) collective-permute-start(bf16[96,1536]{1,0:T(8,128)(2,1)S(1)} %collective-permute-done.3.refs_3_), channel_id=1, source_target_pairs={{0,7},{1,0},{2,1},{3,2},{4,3},{5,4},{6,5},{7,6},{8,15},{9,8},{10,9... | collective-permute-start | bytes 884744 | tf_op jit(solution)/shard_map/ppermute | solution.py:31
  24.6 8.5 %collective-permute-start.2 = (bf16[96,1536]{1,0:T(8,128)(2,1)S(1)}, bf16[96,1536]{1,0:T(8,128)(2,1)S(1)}, u32[]{:S(2)}, u32[]{:S(2)}) collective-permute-start(bf16[96,1536]{1,0:T(8,128)(2,1)S(1)} %collective-permute-done.1.refs_0_), channel_id=1, source_target_pairs={{0,1},{1,2},{2,3},{3,4},{4,5},{5,6},{6,7},{7,0},{8,9},{9,10},{10,1... | collective-permute-start | bytes 884744 | tf_op jit(solution)/shard_map/ppermute | solution.py:31
  24.6 8.5 %copy-start = (bf16[1,1,384,1536]{3,2,1,0:T(8,128)(2,1)S(1)}, bf16[1,1,384,1536]{3,2,1,0:T(8,128)(2,1)}, u32[]{:S(2)}) copy-start(bf16[1,1,384,1536]{3,2,1,0:T(8,128)(2,1)} %param.9) | copy-start | bytes 3538948
  24.8 20.2 %copy-start.5 = (f32[1,2,1536]{2,1,0:T(2,128)S(1)}, f32[1,2,1536]{2,1,0:T(2,128)}, u32[]{:S(2)}) copy-start(f32[1,2,1536]{2,1,0:T(2,128)} %param.15) | copy-start | bytes 36868
  24.8 35.3 %collective-permute-start.7 = (bf16[480,1536]{1,0:T(8,128)(2,1)S(1)}, bf16[480,1536]{1,0:T(8,128)(2,1)S(1)}, u32[]{:S(2)}, u32[]{:S(2)}) collective-permute-start(bf16[480,1536]{1,0:T(8,128)(2,1)S(1)} %join.2.refs_0_), channel_id=1, source_target_pairs={{0,8},{1,9},{2,10},{3,11},{4,12},{5,13},{6,14},{7,15},{8,16},{9,17... | collective-permute-start | bytes 4423688 | tf_op jit(solution)/shard_map/ppermute | solution.py:40
  26.7 33.4 %collective-permute-start.8 = (bf16[480,1536]{1,0:T(8,128)(2,1)S(1)}, bf16[480,1536]{1,0:T(8,128)(2,1)S(1)}, u32[]{:S(2)}, u32[]{:S(2)}) collective-permute-start(bf16[480,1536]{1,0:T(8,128)(2,1)S(1)} %join.2.refs_0_), channel_id=1, source_target_pairs={{0,24},{1,25},{2,26},{3,27},{4,28},{5,29},{6,30},{7,31},{8,0},{9,1... | collective-permute-start | bytes 4423688 | tf_op jit(solution)/shard_map/ppermute | solution.py:40
  27.0 7.5 %collective-permute-start.6 = (bf16[96,1536]{1,0:T(8,128)(2,1)S(1)}, bf16[96,1536]{1,0:T(8,128)(2,1)S(1)}, u32[]{:S(2)}, u32[]{:S(2)}) collective-permute-start(bf16[96,1536]{1,0:T(8,128)(2,1)S(1)} %collective-permute-done.4.refs_4_), channel_id=1, source_target_pairs={{0,7},{1,0},{2,1},{3,2},{4,3},{5,4},{6,5},{7,6},{8,15},{9,8},{10,9... | collective-permute-start | bytes 884744 | tf_op jit(solution)/shard_map/ppermute | solution.py:31
  33.1 7.9 %collective-permute-start.5 = (bf16[96,1536]{1,0:T(8,128)(2,1)S(1)}, bf16[96,1536]{1,0:T(8,128)(2,1)S(1)}, u32[]{:S(2)}, u32[]{:S(2)}) collective-permute-start(bf16[96,1536]{1,0:T(8,128)(2,1)S(1)} %collective-permute-done.2.refs_1_), channel_id=1, source_target_pairs={{0,1},{1,2},{2,3},{3,4},{4,5},{5,6},{6,7},{7,0},{8,9},{9,10},{10,1... | collective-permute-start | bytes 884744 | tf_op jit(solution)/shard_map/ppermute | solution.py:31
  33.3 13.4 %copy-start.2 = (f32[1,2,1536]{2,1,0:T(2,128)S(1)}, f32[1,2,1536]{2,1,0:T(2,128)}, u32[]{:S(2)}) copy-start(f32[1,2,1536]{2,1,0:T(2,128)} %param.10) | copy-start | bytes 36868
  41.1 25.7 %collective-permute-start.13 = (bf16[384,1536]{1,0:T(8,128)(2,1)S(1)}, bf16[384,1536]{1,0:T(8,128)(2,1)S(1)}, u32[]{:S(2)}, u32[]{:S(2)}) collective-permute-start(bf16[384,1536]{1,0:T(8,128)(2,1)S(1)} %get-tuple-element.33), channel_id=1, source_target_pairs={{0,1},{1,2},{2,3},{3,4},{4,5},{5,6},{6,7},{7,0},{8,9},{9,10},{10,1... | collective-permute-start | bytes 3538952 | tf_op jit(solution)/shard_map/ppermute | solution.py:31
  41.1 27.0 %collective-permute-start.12 = (bf16[384,1536]{1,0:T(8,128)(2,1)S(1)}, bf16[384,1536]{1,0:T(8,128)(2,1)S(1)}, u32[]{:S(2)}, u32[]{:S(2)}) collective-permute-start(bf16[384,1536]{1,0:T(8,128)(2,1)S(1)} %get-tuple-element.31), channel_id=1, source_target_pairs={{0,7},{1,0},{2,1},{3,2},{4,3},{5,4},{6,5},{7,6},{8,15},{9,8},{10,9... | collective-permute-start | bytes 3538952 | tf_op jit(solution)/shard_map/ppermute | solution.py:31
  45.0 31.3 %collective-permute-start.9 = (bf16[288,1536]{1,0:T(8,128)(2,1)S(1)}, bf16[288,1536]{1,0:T(8,128)(2,1)S(1)}, u32[]{:S(2)}, u32[]{:S(2)}) collective-permute-start(bf16[288,1536]{1,0:T(8,128)(2,1)S(1)} %join.3.refs_3_), channel_id=1, source_target_pairs={{0,8},{1,9},{2,10},{3,11},{4,12},{5,13},{6,14},{7,15},{8,16},{9,17... | collective-permute-start | bytes 2654216 | tf_op jit(solution)/shard_map/ppermute | solution.py:40
  60.1 9.4 %copy-start.4 = (s32[1,4]{1,0:T(1,128)S(1)}, s32[1,4]{1,0:T(1,128)}, u32[]{:S(2)}) copy-start(s32[1,4]{1,0:T(1,128)} %param.16) | copy-start | bytes 52
  60.1 21.3 %collective-permute-start.10 = (bf16[288,1536]{1,0:T(8,128)(2,1)S(1)}, bf16[288,1536]{1,0:T(8,128)(2,1)S(1)}, u32[]{:S(2)}, u32[]{:S(2)}) collective-permute-start(bf16[288,1536]{1,0:T(8,128)(2,1)S(1)} %join.3.refs_3_), channel_id=1, source_target_pairs={{0,24},{1,25},{2,26},{3,27},{4,28},{5,29},{6,30},{7,31},{8,0},{9,1... | collective-permute-start | bytes 2654216 | tf_op jit(solution)/shard_map/ppermute | solution.py:40
  66.7 26.0 %collective-permute-start.16 = (bf16[384,1536]{1,0:T(8,128)(2,1)S(1)}, bf16[384,1536]{1,0:T(8,128)(2,1)S(1)}, u32[]{:S(2)}, u32[]{:S(2)}) collective-permute-start(bf16[384,1536]{1,0:T(8,128)(2,1)S(1)} %collective-permute-done.13.x_ref), channel_id=1, source_target_pairs={{0,1},{1,2},{2,3},{3,4},{4,5},{5,6},{6,7},{8,9},{9,10},{10,11},{11... | collective-permute-start | bytes 3538952 | tf_op jit(solution)/shard_map/ppermute | solution.py:31
  68.1 27.2 %collective-permute-start.15 = (bf16[384,1536]{1,0:T(8,128)(2,1)S(1)}, bf16[384,1536]{1,0:T(8,128)(2,1)S(1)}, u32[]{:S(2)}, u32[]{:S(2)}) collective-permute-start(bf16[384,1536]{1,0:T(8,128)(2,1)S(1)} %collective-permute-done.12.x_ref), channel_id=1, source_target_pairs={{1,0},{2,1},{3,2},{4,3},{5,4},{6,5},{7,6},{9,8},{10,9},{11,10},{12... | collective-permute-start | bytes 3538952 | tf_op jit(solution)/shard_map/ppermute | solution.py:31
  81.6 30.2 %collective-permute-start.14 = (bf16[384,1536]{1,0:T(8,128)(2,1)S(1)}, bf16[384,1536]{1,0:T(8,128)(2,1)S(1)}, u32[]{:S(2)}, u32[]{:S(2)}) collective-permute-start(bf16[384,1536]{1,0:T(8,128)(2,1)S(1)} %get-tuple-element.39), channel_id=1, source_target_pairs={{0,24},{1,25},{2,26},{3,27},{4,12},{5,13},{6,14},{7,15},{8,0},{9,1... | collective-permute-start | bytes 3538952 | tf_op jit(solution)/shard_map/ppermute | solution.py:47
  82.9 32.5 %collective-permute-start.17 = (bf16[384,1536]{1,0:T(8,128)(2,1)S(1)}, bf16[384,1536]{1,0:T(8,128)(2,1)S(1)}, u32[]{:S(2)}, u32[]{:S(2)}) collective-permute-start(bf16[384,1536]{1,0:T(8,128)(2,1)S(1)} %broadcast_select_fusion.1), channel_id=1, source_target_pairs={{7,8},{15,16},{23,24},{8,7},{16,15},{24,23},{39,40},{47,48},{55,56... | collective-permute-start | bytes 3538952 | tf_op jit(solution)/shard_map/ppermute | solution.py:36
  92.6 41.7 %collective-permute-start.18 = (bf16[240,1536]{1,0:T(8,128)(2,1)S(1)}, bf16[240,1536]{1,0:T(8,128)(2,1)S(1)}, u32[]{:S(2)}, u32[]{:S(2)}) collective-permute-start(bf16[240,1536]{1,0:T(8,128)(2,1)S(1)} %get-tuple-element.44), channel_id=1, source_target_pairs={{0,8},{1,9},{2,10},{3,11},{4,28},{5,29},{6,30},{7,31},{8,16},{9,17... | collective-permute-start | bytes 2211848 | tf_op jit(solution)/shard_map/ppermute | solution.py:47
  92.7 41.6 %collective-permute-start.19 = (bf16[144,1536]{1,0:T(8,128)(2,1)S(1)}, bf16[144,1536]{1,0:T(8,128)(2,1)S(1)}, u32[]{:S(2)}, u32[]{:S(2)}) collective-permute-start(bf16[144,1536]{1,0:T(8,128)(2,1)S(1)} %get-tuple-element.45), channel_id=1, source_target_pairs={{0,24},{1,9},{2,10},{3,11},{4,28},{5,29},{6,30},{7,15},{8,0},{9,17... | collective-permute-start | bytes 1327112 | tf_op jit(solution)/shard_map/ppermute | solution.py:47
  134.3 1.3 copy-start.1
  134.3 1.3 copy-start.3
  137.8 10.5 %collective-permute-start.20 = (bf16[192,1536]{1,0:T(8,128)(2,1)S(1)}, bf16[192,1536]{1,0:T(8,128)(2,1)S(1)}, u32[]{:S(2)}, u32[]{:S(2)}) collective-permute-start(bf16[192,1536]{1,0:T(8,128)(2,1)S(1)} %project_out.2), channel_id=1, source_target_pairs={{0,32},{32,64},{64,96},{96,128},{128,160},{160,192},{192,224},{224... | collective-permute-start | bytes 1769480 | tf_op jit(solution)/shard_map/ppermute | solution.py:58
  137.8 16.8 %collective-permute-start.21 = (bf16[192,1536]{1,0:T(8,128)(2,1)S(1)}, bf16[192,1536]{1,0:T(8,128)(2,1)S(1)}, u32[]{:S(2)}, u32[]{:S(2)}) collective-permute-start(bf16[192,1536]{1,0:T(8,128)(2,1)S(1)} %project_out.3), channel_id=1, source_target_pairs={{0,32},{32,64},{64,96},{96,128},{128,160},{160,192},{192,224},{224... | collective-permute-start | bytes 1769480 | tf_op jit(solution)/shard_map/ppermute | solution.py:58

commit v5 on v4

--- a/solution.py
+++ b/solution.py
@@ -274,8 +274,8 @@
     return kernel(body, "whole_out", specs, shapes, [], {}, 1, SMALL, [at, *pieces])[0]
 
 
-def attend(scalars, query, window):
-    rows, inner = query.shape
+def attend(scalars, query, window, at, rows):
+    inner = query.shape[1]
     factor = math.log2(math.e) / math.sqrt(HEAD_DIM)
 
     def body(at_ref, list_ref, live_ref, q_ref, window_ref, out_ref):
@@ -288,7 +288,7 @@
             begin = pl.multiple_of(h * HEAD_DIM, HEAD_DIM)
             cols = pl.ds(begin, HEAD_DIM)
             value_cols = pl.ds(begin + inner, HEAD_DIM)
-            q = q_ref[:, cols]
+            q = q_ref[at : at + rows, cols]
             scores = []
             for p in places:
                 keys = window_ref[p, :, cols]
@@ -331,15 +331,14 @@
     return kernel(body, "attend", specs, shapes, [], {}, flops, LARGE, operands)[0]
 
 
-def project_out(attended, w_out, gate, x, at, count):
+def project_out(attended, w_out, gate, x, at):
+    count = attended.shape[0]
     width = w_out.shape[1]
 
     def body(a_ref, w_ref, gate_ref, x_ref, out_ref):
         for j in range(width // COLS):
             cols = slice(j * COLS, (j + 1) * COLS)
-            branch = jnp.dot(
-                a_ref[at : at + count, :], w_ref[:, cols], preferred_element_type=jnp.float32
-            )
+            branch = jnp.dot(a_ref[...], w_ref[:, cols], preferred_element_type=jnp.float32)
             residual = x_ref[at : at + count, cols].astype(jnp.float32)
             out_ref[:, cols] = (residual + gate_ref[:, cols] * branch).astype(jnp.bfloat16)
 
@@ -403,14 +402,15 @@
     query = project_query(at, normed, gains[0:1], query_pieces, query_plan)
     query, window, edge_far = lax.optimization_barrier((query, window, edge_far))
     window = add_tile(window, None, edge_far)
-    attended = attend(scalars, query, window)
+    count = rows // 2
+    attended = attend(scalars, query, window, 0, count)
     attended, *out_pieces[-2:] = lax.optimization_barrier((attended, *out_pieces[-2:]))
     out_whole = whole_out(at, out_pieces, out_plan, gains.shape[1])
-    count = rows // 2
-    parts = [
-        to_next_section(project_out(attended, out_whole, gate, x, begin, count))
-        for begin in (0, count)
-    ]
+    first = project_out(attended, out_whole, gate, x, 0)
+    first_handed = to_next_section(first)
+    attended = attend(scalars, after(query, first), window, count, count)
+    second = project_out(attended, out_whole, gate, x, count)
+    parts = [first_handed, to_next_section(after(second, first_handed))]
     return jnp.concatenate(parts, axis=0)[None, None]
 
 

time: 156 us -> 155 us (level)
  waiting for transfers between devices: 67.1 us -> 79.9 us
  Pallas kernels: 44.2 us -> 32.8 us
  starting transfers between devices: 40.3 us -> 38.7 us
    ppermute x3, waiting for transfers between devices: 10.7 us -> 24.8 us  [along_y_by_place(): return lax.ppermute(value, 'patch', pairs)]
    pallas_call x14 -> x15, Pallas kernels: 44.2 us -> 32.8 us  [kernel(): pl.pallas_call(body, in_specs=specs, out_specs=[VMEM for _ in shapes], ou...]
    ppermute x2, starting transfers between devices: 1.61 us -> 0.03 us  [to_next_section(): lax.ppermute(block, 'section', [(i, (i + 1) % count) for i in range(count)])]
  transfers between devices with their start and end apart: 22 -> 22, of which waited for: 13 -> 14; matrix products, arithmetic and copies ran while one was open for 1% -> 1% of each run, Pallas kernels for 27% -> 20%
where the time goes in v5:
time: 155 us
  waiting for transfers between devices  79.9 us (52%)
  starting transfers between devices  38.7 us (25%)
  Pallas kernels  32.8 us (21%)
  other arithmetic  2.38 us (2%)
    pallas_call x15, Pallas kernels, kernel(): pl.pallas_call(body, in_specs=specs, out_specs=[VMEM for _ in shapes], ou...  32.8 us
    ppermute x11, waiting for transfers between devices, along_z(): return lax.ppermute(value, 'patch', pairs)  28.3 us
    ppermute x3, waiting for transfers between devices, along_y_by_place(): return lax.ppermute(value, 'patch', pairs)  24.8 us
    ppermute x11, starting transfers between devices, along_z(): return lax.ppermute(value, 'patch', pairs)  16.9 us
    ppermute x2, waiting for transfers between devices, to_next_section(): lax.ppermute(block, 'section', [(i, (i + 1) % count) for i in range(count)])  13.9 us
    ppermute x4, waiting for transfers between devices, along_y(): lax.ppermute(value, 'patch', [(y * Z + z, (y + steps) % Y * Z + z) for y...  11.7 us
    ppermute x1, starting transfers between devices, around_rows(): return lax.ppermute(value, 'patch', ends + [(b, a) for a, b in ends])  9.68 us
    ppermute x4, starting transfers between devices, along_y(): lax.ppermute(value, 'patch', [(y * Z + z, (y + steps) % Y * Z + z) for y...  5.9 us
  transfers between devices with their start and end apart: 22, of which 14 were waited for; matrix products, arithmetic and copies ran while one was open for 1% of the time, Pallas kernels for 20%

profile of v5, /device:TPU:24, one launch (start us, length us, event | category | flops | bytes accessed | tf_op | source)
XLA Modules:
  0.0 154.8 jit_solution(17202223835737906993)
XLA Ops:
  0.0 2.7 %collective-permute-start.11 = (bf16[384,1536]{1,0:T(8,128)(2,1)}, bf16[384,1536]{1,0:T(8,128)(2,1)S(1)}, u32[]{:S(2)}, u32[]{:S(2)}) collective-permute-start(bf16[384,1536]{1,0:T(8,128)(2,1)} %bitcast.15), channel_id=1, source_target_pairs={{7,15},{15,23},{23,31},{8,0},{16,8},{24,16},{39,47},{47,55},{55,63... | collective-permute-start | bytes 3538952 | tf_op jit(solution)/shard_map/ppermute | solution.py:53
  2.7 1.0 pad_maximum_fusion.refs_2_
  3.7 0.1 collective-permute-start
  3.8 4.5 %collective-permute-start.3 = (bf16[96,1536]{1,0:T(8,128)(2,1)S(1)}, bf16[96,1536]{1,0:T(8,128)(2,1)S(1)}, u32[]{:S(2)}, u32[]{:S(2)}) collective-permute-start(bf16[96,1536]{1,0:T(8,128)(2,1)S(1)} %pad_maximum_fusion.refs_2_), channel_id=1, source_target_pairs={{0,7},{1,0},{2,1},{3,2},{4,3},{5,4},{6,5},{7,6},{8,15},{9,8},{10,9... | collective-permute-start | bytes 884744 | tf_op jit(solution)/shard_map/ppermute | solution.py:31
  8.3 6.9 %collective-permute-done.refs_1_ = bf16[96,1536]{1,0:T(8,128)(2,1)S(1)} collective-permute-done((bf16[96,1536]{1,0:T(8,128)(2,1)S(1)}, bf16[96,1536]{1,0:T(8,128)(2,1)S(1)}, u32[]{:S(2)}, u32[]{:S(2)}) %collective-permute-start) | collective-permute-done | bytes 294944 | tf_op jit(solution)/shard_map/ppermute | solution.py:31
  15.2 3.2 %collective-permute-start.4 = (bf16[96,1536]{1,0:T(8,128)(2,1)S(1)}, bf16[96,1536]{1,0:T(8,128)(2,1)S(1)}, u32[]{:S(2)}, u32[]{:S(2)}) collective-permute-start(bf16[96,1536]{1,0:T(8,128)(2,1)S(1)} %collective-permute-done.3.refs_3_), channel_id=1, source_target_pairs={{0,7},{1,0},{2,1},{3,2},{4,3},{5,4},{6,5},{7,6},{8,15},{9,8},{10,9... | collective-permute-start | bytes 884744 | tf_op jit(solution)/shard_map/ppermute | solution.py:31
  18.5 6.2 %collective-permute-done.1.refs_0_ = bf16[96,1536]{1,0:T(8,128)(2,1)S(1)} collective-permute-done((bf16[96,1536]{1,0:T(8,128)(2,1)S(1)}, bf16[96,1536]{1,0:T(8,128)(2,1)S(1)}, u32[]{:S(2)}, u32[]{:S(2)}) %collective-permute-start.1) | collective-permute-done | bytes 294944 | tf_op jit(solution)/shard_map/ppermute | solution.py:31
  24.7 0.1 join.2.refs_0_
  24.8 2.0 %collective-permute-start.7 = (bf16[480,1536]{1,0:T(8,128)(2,1)S(1)}, bf16[480,1536]{1,0:T(8,128)(2,1)S(1)}, u32[]{:S(2)}, u32[]{:S(2)}) collective-permute-start(bf16[480,1536]{1,0:T(8,128)(2,1)S(1)} %join.2.refs_0_), channel_id=1, source_target_pairs={{0,8},{1,9},{2,10},{3,11},{4,12},{5,13},{6,14},{7,15},{8,16},{9,17... | collective-permute-start | bytes 4423688 | tf_op jit(solution)/shard_map/ppermute | solution.py:40
  26.7 0.2 collective-permute-start.8
  27.0 3.2 %collective-permute-start.6 = (bf16[96,1536]{1,0:T(8,128)(2,1)S(1)}, bf16[96,1536]{1,0:T(8,128)(2,1)S(1)}, u32[]{:S(2)}, u32[]{:S(2)}) collective-permute-start(bf16[96,1536]{1,0:T(8,128)(2,1)S(1)} %collective-permute-done.4.refs_4_), channel_id=1, source_target_pairs={{0,7},{1,0},{2,1},{3,2},{4,3},{5,4},{6,5},{7,6},{8,15},{9,8},{10,9... | collective-permute-start | bytes 884744 | tf_op jit(solution)/shard_map/ppermute | solution.py:31
  30.2 2.9 %collective-permute-done.2.refs_1_ = bf16[96,1536]{1,0:T(8,128)(2,1)S(1)} collective-permute-done((bf16[96,1536]{1,0:T(8,128)(2,1)S(1)}, bf16[96,1536]{1,0:T(8,128)(2,1)S(1)}, u32[]{:S(2)}, u32[]{:S(2)}) %collective-permute-start.2) | collective-permute-done | bytes 294944 | tf_op jit(solution)/shard_map/ppermute | solution.py:31
  33.1 0.2 broadcast_select_fusion
  33.3 1.1 collective-permute-done.6.refs_2_
  34.5 6.6 %collective-permute-done.5.refs_0_ = bf16[96,1536]{1,0:T(8,128)(2,1)S(1)} collective-permute-done((bf16[96,1536]{1,0:T(8,128)(2,1)S(1)}, bf16[96,1536]{1,0:T(8,128)(2,1)S(1)}, u32[]{:S(2)}, u32[]{:S(2)}) %collective-permute-start.5) | collective-permute-done | bytes 294944 | tf_op jit(solution)/shard_map/ppermute | solution.py:31
  41.1 3.2 %collective-permute-start.12 = (bf16[384,1536]{1,0:T(8,128)(2,1)S(1)}, bf16[384,1536]{1,0:T(8,128)(2,1)S(1)}, u32[]{:S(2)}, u32[]{:S(2)}) collective-permute-start(bf16[384,1536]{1,0:T(8,128)(2,1)S(1)} %get-tuple-element.33), channel_id=1, source_target_pairs={{0,7},{1,0},{2,1},{3,2},{4,3},{5,4},{6,5},{7,6},{8,15},{9,8},{10,9... | collective-permute-start | bytes 3538952 | tf_op jit(solution)/shard_map/ppermute | solution.py:31
  45.0 1.6 %collective-permute-start.9 = (bf16[288,1536]{1,0:T(8,128)(2,1)S(1)}, bf16[288,1536]{1,0:T(8,128)(2,1)S(1)}, u32[]{:S(2)}, u32[]{:S(2)}) collective-permute-start(bf16[288,1536]{1,0:T(8,128)(2,1)S(1)} %join.3.refs_3_), channel_id=1, source_target_pairs={{0,8},{1,9},{2,10},{3,11},{4,12},{5,13},{6,14},{7,15},{8,16},{9,17... | collective-permute-start | bytes 2654216 | tf_op jit(solution)/shard_map/ppermute | solution.py:40
  46.7 7.3 %own_tile.1 = (bf16[5,384,3072]{2,1,0:T(8,128)(2,1)S(1)}, bf16[384,1536]{1,0:T(8,128)(2,1)S(1)}, bf16[1536,3072]{1,0:T(8,128)(2,1)S(1)}) custom-call(bf16[384,1536]{1,0:T(8,128)(2,1)} %bitcast.16, f32[2,1536]{1,0:T(2,128)S(1)} %bitcast.19, bf16[1536,3072]{1,0:T(8,128)(2,1)} %bitcast.34, f32[1,1536]{1,0:T(1,128)S(1)} %get-tuple-element.56.gain_ref), custom_call_target="tpu_custom_call" | custom-call | flops 3623878656 | bytes 10635264 | tf_op jit(solution)/shard_map/own_tile/pallas_call | solution.py:83
  54.0 6.1 %collective-permute-done.7.refs_0_.refs_1_ = bf16[480,1536]{1,0:T(8,128)(2,1)S(1)} collective-permute-done((bf16[480,1536]{1,0:T(8,128)(2,1)S(1)}, bf16[480,1536]{1,0:T(8,128)(2,1)S(1)}, u32[]{:S(2)}, u32[]{:S(2)}) %collective-permute-start.7) | collective-permute-done | bytes 1474592 | tf_op jit(solution)/shard_map/ppermute | solution.py:40
  60.1 2.0 %collective-permute-start.10 = (bf16[288,1536]{1,0:T(8,128)(2,1)S(1)}, bf16[288,1536]{1,0:T(8,128)(2,1)S(1)}, u32[]{:S(2)}, u32[]{:S(2)}) collective-permute-start(bf16[288,1536]{1,0:T(8,128)(2,1)S(1)} %join.3.refs_3_), channel_id=1, source_target_pairs={{0,24},{1,25},{2,26},{3,27},{4,28},{5,29},{6,30},{7,31},{8,0},{9,1... | collective-permute-start | bytes 2654216 | tf_op jit(solution)/shard_map/ppermute | solution.py:40
  62.1 4.6 %collective-permute-done.13.x_ref = bf16[384,1536]{1,0:T(8,128)(2,1)S(1)} collective-permute-done((bf16[384,1536]{1,0:T(8,128)(2,1)S(1)}, bf16[384,1536]{1,0:T(8,128)(2,1)S(1)}, u32[]{:S(2)}, u32[]{:S(2)}) %collective-permute-start.13) | collective-permute-done | bytes 1179680 | tf_op jit(solution)/shard_map/ppermute | solution.py:31
  66.7 1.4 collective-permute-start.16
  68.1 1.3 collective-permute-start.15
  69.4 0.1 broadcast_select_fusion.1
  69.5 0.6 near_tile.5._
  70.1 5.7 %near_tile.6._ = bf16[5,384,3072]{2,1,0:T(8,128)(2,1)S(1)} custom-call(s32[1]{0:T(128)} %bitcast.at_ref, s32[4]{0:T(128)S(1)} %bitcast.26, s32[1]{0:T(128)S(6)} %copy.20.live_ref, bf16[384,1536]{1,0:T(8,128)(2,1)S(1)} %collective-permute-done.12.x_ref, f32[2,1536]{1,0:T(2,128)S(1)} %bitcast.21, ...), custom_call_target="tpu_custom_call", output_to_operand_aliasing={{}: (7, {})} | custom-call | flops 3623878656 | bytes 22431768 | tf_op jit(solution)/shard_map/near_tile/pallas_call | solution.py:83
  75.8 0.6 collective-permute-done.9.refs_1_.refs_4_
  76.4 5.0 %collective-permute-done.10.refs_3_.refs_5_ = bf16[288,1536]{1,0:T(8,128)(2,1)S(1)} collective-permute-done((bf16[288,1536]{1,0:T(8,128)(2,1)S(1)}, bf16[288,1536]{1,0:T(8,128)(2,1)S(1)}, u32[]{:S(2)}, u32[]{:S(2)}) %collective-permute-start.10) | collective-permute-done | bytes 884768 | tf_op jit(solution)/shard_map/ppermute | solution.py:40
  81.4 0.2 onward.1
  81.6 1.3 collective-permute-start.14
  82.9 9.7 %collective-permute-start.17 = (bf16[384,1536]{1,0:T(8,128)(2,1)S(1)}, bf16[384,1536]{1,0:T(8,128)(2,1)S(1)}, u32[]{:S(2)}, u32[]{:S(2)}) collective-permute-start(bf16[384,1536]{1,0:T(8,128)(2,1)S(1)} %broadcast_select_fusion.1), channel_id=1, source_target_pairs={{7,8},{15,16},{23,24},{8,7},{16,15},{24,23},{39,40},{47,48},{55,56... | collective-permute-start | bytes 3538952 | tf_op jit(solution)/shard_map/ppermute | solution.py:36
  92.6 0.1 collective-permute-start.18
  92.7 2.0 %collective-permute-start.19 = (bf16[144,1536]{1,0:T(8,128)(2,1)S(1)}, bf16[144,1536]{1,0:T(8,128)(2,1)S(1)}, u32[]{:S(2)}, u32[]{:S(2)}) collective-permute-start(bf16[144,1536]{1,0:T(8,128)(2,1)S(1)} %get-tuple-element.47), channel_id=1, source_target_pairs={{0,24},{1,9},{2,10},{3,11},{4,28},{5,29},{6,30},{7,15},{8,0},{9,17... | collective-permute-start | bytes 1327112 | tf_op jit(solution)/shard_map/ppermute | solution.py:47
  94.7 0.6 near_tile.7._
  95.3 0.8 near_tile.8._
  96.1 15.7 %collective-permute-done.14.refs_6_ = bf16[384,1536]{1,0:T(8,128)(2,1)S(1)} collective-permute-done((bf16[384,1536]{1,0:T(8,128)(2,1)S(1)}, bf16[384,1536]{1,0:T(8,128)(2,1)S(1)}, u32[]{:S(2)}, u32[]{:S(2)}) %collective-permute-start.14) | collective-permute-done | bytes 1179680 | tf_op jit(solution)/shard_map/ppermute | solution.py:47
  111.8 2.5 %project_query.1.q_ref = bf16[384,1536]{1,0:T(8,128)(2,1)S(1)} custom-call(s32[1]{0:T(128)} %bitcast.at_ref, bf16[384,1536]{1,0:T(8,128)(2,1)S(1)} %get-tuple-element.31.normed_ref, f32[1,1536]{1,0:T(1,128)S(1)} %get-tuple-element.55.gain_ref, bf16[480,1536]{1,0:T(8,128)(2,1)S(1)} %join.2.refs_0_, ...), custom_call_target="tpu_custom_call" | custom-call | flops 1811939328 | bytes 9443332 | tf_op jit(solution)/shard_map/project_query/pallas_call | solution.py:83
  114.3 1.1 collective-permute-done.17.x_ref
  115.4 0.6 near_tile.9.window_ref
  116.0 6.0 %attend.2.a_ref = bf16[192,1536]{1,0:T(8,128)(2,1)S(1)} custom-call(s32[1]{0:T(128)} %bitcast.at_ref, s32[4]{0:T(128)S(1)} %bitcast.30, s32[1]{0:T(128)S(6)} %copy.20.live_ref, bf16[384,1536]{1,0:T(8,128)(2,1)S(1)} %project_query.1.q_ref, bf16[5,384,3072]{2,1,0:T(8,128)(2,1)S(1)} %near_tile.9.window_ref), custom_call_target="tpu_custom_call" | custom-call | flops 1811939328 | bytes 12976152 | tf_op jit(solution)/shard_map/attend/pallas_call | solution.py:83
  122.0 9.1 %collective-permute-done.18.refs_6_ = bf16[240,1536]{1,0:T(8,128)(2,1)S(1)} collective-permute-done((bf16[240,1536]{1,0:T(8,128)(2,1)S(1)}, bf16[240,1536]{1,0:T(8,128)(2,1)S(1)}, u32[]{:S(2)}, u32[]{:S(2)}) %collective-permute-start.18) | collective-permute-done | bytes 737312 | tf_op jit(solution)/shard_map/ppermute | solution.py:47
  131.1 0.4 whole_out.1.w_ref
  131.5 1.1 project_out.2
  132.7 6.0 %attend.3.a_ref = bf16[192,1536]{1,0:T(8,128)(2,1)S(1)} custom-call(s32[1]{0:T(128)} %bitcast.at_ref, s32[4]{0:T(128)S(1)} %bitcast.31, s32[1]{0:T(128)S(6)} %copy.20.live_ref, bf16[384,1536]{1,0:T(8,128)(2,1)S(1)} %project_query.1.q_ref, bf16[5,384,3072]{2,1,0:T(8,128)(2,1)S(1)} %near_tile.9.window_ref), custom_call_target="tpu_custom_call" | custom-call | flops 1811939328 | bytes 12976152 | tf_op jit(solution)/shard_map/attend/pallas_call | solution.py:83
  138.6 1.1 project_out.3
  139.7 3.4 %collective-permute-done.20 = bf16[192,1536]{1,0:T(8,128)(2,1)S(1)} collective-permute-done((bf16[192,1536]{1,0:T(8,128)(2,1)S(1)}, bf16[192,1536]{1,0:T(8,128)(2,1)S(1)}, u32[]{:S(2)}, u32[]{:S(2)}) %collective-permute-start.20) | collective-permute-done | bytes 589856 | tf_op jit(solution)/shard_map/ppermute | solution.py:58
  143.2 10.5 %collective-permute-done.21 = bf16[192,1536]{1,0:T(8,128)(2,1)S(1)} collective-permute-done((bf16[192,1536]{1,0:T(8,128)(2,1)S(1)}, bf16[192,1536]{1,0:T(8,128)(2,1)S(1)}, u32[]{:S(2)}, u32[]{:S(2)}) %collective-permute-start.21) | collective-permute-done | bytes 589856 | tf_op jit(solution)/shard_map/ppermute | solution.py:58
  153.7 1.1 maximum_bitcast_fusion
  (28 shorter events, 0.2 us)
Async XLA Ops:
  0.0 33.1 %collective-permute-start.11 = (bf16[384,1536]{1,0:T(8,128)(2,1)}, bf16[384,1536]{1,0:T(8,128)(2,1)S(1)}, u32[]{:S(2)}, u32[]{:S(2)}) collective-permute-start(bf16[384,1536]{1,0:T(8,128)(2,1)} %bitcast.15), channel_id=1, source_target_pairs={{7,15},{15,23},{23,31},{8,0},{16,8},{24,16},{39,47},{47,55},{55,63... | collective-permute-start | bytes 3538952 | tf_op jit(solution)/shard_map/ppermute | solution.py:53
  3.7 11.5 %collective-permute-start = (bf16[96,1536]{1,0:T(8,128)(2,1)S(1)}, bf16[96,1536]{1,0:T(8,128)(2,1)S(1)}, u32[]{:S(2)}, u32[]{:S(2)}) collective-permute-start(bf16[96,1536]{1,0:T(8,128)(2,1)S(1)} %pad_maximum_fusion.refs_2_), channel_id=1, source_target_pairs={{0,1},{1,2},{2,3},{3,4},{4,5},{5,6},{6,7},{7,0},{8,9},{9,10},{10,1... | collective-permute-start | bytes 884744 | tf_op jit(solution)/shard_map/ppermute | solution.py:31
  3.8 11.4 %collective-permute-start.3 = (bf16[96,1536]{1,0:T(8,128)(2,1)S(1)}, bf16[96,1536]{1,0:T(8,128)(2,1)S(1)}, u32[]{:S(2)}, u32[]{:S(2)}) collective-permute-start(bf16[96,1536]{1,0:T(8,128)(2,1)S(1)} %pad_maximum_fusion.refs_2_), channel_id=1, source_target_pairs={{0,7},{1,0},{2,1},{3,2},{4,3},{5,4},{6,5},{7,6},{8,15},{9,8},{10,9... | collective-permute-start | bytes 884744 | tf_op jit(solution)/shard_map/ppermute | solution.py:31
  15.2 9.4 %collective-permute-start.1 = (bf16[96,1536]{1,0:T(8,128)(2,1)S(1)}, bf16[96,1536]{1,0:T(8,128)(2,1)S(1)}, u32[]{:S(2)}, u32[]{:S(2)}) collective-permute-start(bf16[96,1536]{1,0:T(8,128)(2,1)S(1)} %collective-permute-done.refs_1_), channel_id=1, source_target_pairs={{0,1},{1,2},{2,3},{3,4},{4,5},{5,6},{6,7},{7,0},{8,9},{9,10},{10,1... | collective-permute-start | bytes 884744 | tf_op jit(solution)/shard_map/ppermute | solution.py:31
  15.2 9.4 %collective-permute-start.4 = (bf16[96,1536]{1,0:T(8,128)(2,1)S(1)}, bf16[96,1536]{1,0:T(8,128)(2,1)S(1)}, u32[]{:S(2)}, u32[]{:S(2)}) collective-permute-start(bf16[96,1536]{1,0:T(8,128)(2,1)S(1)} %collective-permute-done.3.refs_3_), channel_id=1, source_target_pairs={{0,7},{1,0},{2,1},{3,2},{4,3},{5,4},{6,5},{7,6},{8,15},{9,8},{10,9... | collective-permute-start | bytes 884744 | tf_op jit(solution)/shard_map/ppermute | solution.py:31
  24.6 8.5 %collective-permute-start.2 = (bf16[96,1536]{1,0:T(8,128)(2,1)S(1)}, bf16[96,1536]{1,0:T(8,128)(2,1)S(1)}, u32[]{:S(2)}, u32[]{:S(2)}) collective-permute-start(bf16[96,1536]{1,0:T(8,128)(2,1)S(1)} %collective-permute-done.1.refs_0_), channel_id=1, source_target_pairs={{0,1},{1,2},{2,3},{3,4},{4,5},{5,6},{6,7},{7,0},{8,9},{9,10},{10,1... | collective-permute-start | bytes 884744 | tf_op jit(solution)/shard_map/ppermute | solution.py:31
  24.6 8.5 %copy-start = (bf16[1,1,384,1536]{3,2,1,0:T(8,128)(2,1)S(1)}, bf16[1,1,384,1536]{3,2,1,0:T(8,128)(2,1)}, u32[]{:S(2)}) copy-start(bf16[1,1,384,1536]{3,2,1,0:T(8,128)(2,1)} %param.9) | copy-start | bytes 3538948
  24.8 20.2 %copy-start.5 = (f32[1,2,1536]{2,1,0:T(2,128)S(1)}, f32[1,2,1536]{2,1,0:T(2,128)}, u32[]{:S(2)}) copy-start(f32[1,2,1536]{2,1,0:T(2,128)} %param.15) | copy-start | bytes 36868
  24.8 35.3 %collective-permute-start.7 = (bf16[480,1536]{1,0:T(8,128)(2,1)S(1)}, bf16[480,1536]{1,0:T(8,128)(2,1)S(1)}, u32[]{:S(2)}, u32[]{:S(2)}) collective-permute-start(bf16[480,1536]{1,0:T(8,128)(2,1)S(1)} %join.2.refs_0_), channel_id=1, source_target_pairs={{0,8},{1,9},{2,10},{3,11},{4,12},{5,13},{6,14},{7,15},{8,16},{9,17... | collective-permute-start | bytes 4423688 | tf_op jit(solution)/shard_map/ppermute | solution.py:40
  26.7 33.4 %collective-permute-start.8 = (bf16[480,1536]{1,0:T(8,128)(2,1)S(1)}, bf16[480,1536]{1,0:T(8,128)(2,1)S(1)}, u32[]{:S(2)}, u32[]{:S(2)}) collective-permute-start(bf16[480,1536]{1,0:T(8,128)(2,1)S(1)} %join.2.refs_0_), channel_id=1, source_target_pairs={{0,24},{1,25},{2,26},{3,27},{4,28},{5,29},{6,30},{7,31},{8,0},{9,1... | collective-permute-start | bytes 4423688 | tf_op jit(solution)/shard_map/ppermute | solution.py:40
  27.0 7.5 %collective-permute-start.6 = (bf16[96,1536]{1,0:T(8,128)(2,1)S(1)}, bf16[96,1536]{1,0:T(8,128)(2,1)S(1)}, u32[]{:S(2)}, u32[]{:S(2)}) collective-permute-start(bf16[96,1536]{1,0:T(8,128)(2,1)S(1)} %collective-permute-done.4.refs_4_), channel_id=1, source_target_pairs={{0,7},{1,0},{2,1},{3,2},{4,3},{5,4},{6,5},{7,6},{8,15},{9,8},{10,9... | collective-permute-start | bytes 884744 | tf_op jit(solution)/shard_map/ppermute | solution.py:31
  33.1 7.9 %collective-permute-start.5 = (bf16[96,1536]{1,0:T(8,128)(2,1)S(1)}, bf16[96,1536]{1,0:T(8,128)(2,1)S(1)}, u32[]{:S(2)}, u32[]{:S(2)}) collective-permute-start(bf16[96,1536]{1,0:T(8,128)(2,1)S(1)} %collective-permute-done.2.refs_1_), channel_id=1, source_target_pairs={{0,1},{1,2},{2,3},{3,4},{4,5},{5,6},{6,7},{7,0},{8,9},{9,10},{10,1... | collective-permute-start | bytes 884744 | tf_op jit(solution)/shard_map/ppermute | solution.py:31
  33.3 13.4 %copy-start.2 = (f32[1,2,1536]{2,1,0:T(2,128)S(1)}, f32[1,2,1536]{2,1,0:T(2,128)}, u32[]{:S(2)}) copy-start(f32[1,2,1536]{2,1,0:T(2,128)} %param.10) | copy-start | bytes 36868
  41.1 25.7 %collective-permute-start.13 = (bf16[384,1536]{1,0:T(8,128)(2,1)S(1)}, bf16[384,1536]{1,0:T(8,128)(2,1)S(1)}, u32[]{:S(2)}, u32[]{:S(2)}) collective-permute-start(bf16[384,1536]{1,0:T(8,128)(2,1)S(1)} %get-tuple-element.35), channel_id=1, source_target_pairs={{0,1},{1,2},{2,3},{3,4},{4,5},{5,6},{6,7},{7,0},{8,9},{9,10},{10,1... | collective-permute-start | bytes 3538952 | tf_op jit(solution)/shard_map/ppermute | solution.py:31
  41.1 27.0 %collective-permute-start.12 = (bf16[384,1536]{1,0:T(8,128)(2,1)S(1)}, bf16[384,1536]{1,0:T(8,128)(2,1)S(1)}, u32[]{:S(2)}, u32[]{:S(2)}) collective-permute-start(bf16[384,1536]{1,0:T(8,128)(2,1)S(1)} %get-tuple-element.33), channel_id=1, source_target_pairs={{0,7},{1,0},{2,1},{3,2},{4,3},{5,4},{6,5},{7,6},{8,15},{9,8},{10,9... | collective-permute-start | bytes 3538952 | tf_op jit(solution)/shard_map/ppermute | solution.py:31
  45.0 31.3 %collective-permute-start.9 = (bf16[288,1536]{1,0:T(8,128)(2,1)S(1)}, bf16[288,1536]{1,0:T(8,128)(2,1)S(1)}, u32[]{:S(2)}, u32[]{:S(2)}) collective-permute-start(bf16[288,1536]{1,0:T(8,128)(2,1)S(1)} %join.3.refs_3_), channel_id=1, source_target_pairs={{0,8},{1,9},{2,10},{3,11},{4,12},{5,13},{6,14},{7,15},{8,16},{9,17... | collective-permute-start | bytes 2654216 | tf_op jit(solution)/shard_map/ppermute | solution.py:40
  60.1 9.4 %copy-start.3 = (s32[1,4]{1,0:T(1,128)S(1)}, s32[1,4]{1,0:T(1,128)}, u32[]{:S(2)}) copy-start(s32[1,4]{1,0:T(1,128)} %param.16) | copy-start | bytes 52
  60.1 21.3 %collective-permute-start.10 = (bf16[288,1536]{1,0:T(8,128)(2,1)S(1)}, bf16[288,1536]{1,0:T(8,128)(2,1)S(1)}, u32[]{:S(2)}, u32[]{:S(2)}) collective-permute-start(bf16[288,1536]{1,0:T(8,128)(2,1)S(1)} %join.3.refs_3_), channel_id=1, source_target_pairs={{0,24},{1,25},{2,26},{3,27},{4,28},{5,29},{6,30},{7,31},{8,0},{9,1... | collective-permute-start | bytes 2654216 | tf_op jit(solution)/shard_map/ppermute | solution.py:40
  66.7 26.0 %collective-permute-start.16 = (bf16[384,1536]{1,0:T(8,128)(2,1)S(1)}, bf16[384,1536]{1,0:T(8,128)(2,1)S(1)}, u32[]{:S(2)}, u32[]{:S(2)}) collective-permute-start(bf16[384,1536]{1,0:T(8,128)(2,1)S(1)} %collective-permute-done.13.x_ref), channel_id=1, source_target_pairs={{0,1},{1,2},{2,3},{3,4},{4,5},{5,6},{6,7},{8,9},{9,10},{10,11},{11... | collective-permute-start | bytes 3538952 | tf_op jit(solution)/shard_map/ppermute | solution.py:31
  68.1 27.2 %collective-permute-start.15 = (bf16[384,1536]{1,0:T(8,128)(2,1)S(1)}, bf16[384,1536]{1,0:T(8,128)(2,1)S(1)}, u32[]{:S(2)}, u32[]{:S(2)}) collective-permute-start(bf16[384,1536]{1,0:T(8,128)(2,1)S(1)} %collective-permute-done.12.x_ref), channel_id=1, source_target_pairs={{1,0},{2,1},{3,2},{4,3},{5,4},{6,5},{7,6},{9,8},{10,9},{11,10},{12... | collective-permute-start | bytes 3538952 | tf_op jit(solution)/shard_map/ppermute | solution.py:31
  81.6 30.2 %collective-permute-start.14 = (bf16[384,1536]{1,0:T(8,128)(2,1)S(1)}, bf16[384,1536]{1,0:T(8,128)(2,1)S(1)}, u32[]{:S(2)}, u32[]{:S(2)}) collective-permute-start(bf16[384,1536]{1,0:T(8,128)(2,1)S(1)} %get-tuple-element.41), channel_id=1, source_target_pairs={{0,24},{1,25},{2,26},{3,27},{4,12},{5,13},{6,14},{7,15},{8,0},{9,1... | collective-permute-start | bytes 3538952 | tf_op jit(solution)/shard_map/ppermute | solution.py:47
  82.9 32.5 %collective-permute-start.17 = (bf16[384,1536]{1,0:T(8,128)(2,1)S(1)}, bf16[384,1536]{1,0:T(8,128)(2,1)S(1)}, u32[]{:S(2)}, u32[]{:S(2)}) collective-permute-start(bf16[384,1536]{1,0:T(8,128)(2,1)S(1)} %broadcast_select_fusion.1), channel_id=1, source_target_pairs={{7,8},{15,16},{23,24},{8,7},{16,15},{24,23},{39,40},{47,48},{55,56... | collective-permute-start | bytes 3538952 | tf_op jit(solution)/shard_map/ppermute | solution.py:36
  92.6 38.5 %collective-permute-start.18 = (bf16[240,1536]{1,0:T(8,128)(2,1)S(1)}, bf16[240,1536]{1,0:T(8,128)(2,1)S(1)}, u32[]{:S(2)}, u32[]{:S(2)}) collective-permute-start(bf16[240,1536]{1,0:T(8,128)(2,1)S(1)} %get-tuple-element.46), channel_id=1, source_target_pairs={{0,8},{1,9},{2,10},{3,11},{4,28},{5,29},{6,30},{7,31},{8,16},{9,17... | collective-permute-start | bytes 2211848 | tf_op jit(solution)/shard_map/ppermute | solution.py:47
  92.7 29.3 %collective-permute-start.19 = (bf16[144,1536]{1,0:T(8,128)(2,1)S(1)}, bf16[144,1536]{1,0:T(8,128)(2,1)S(1)}, u32[]{:S(2)}, u32[]{:S(2)}) collective-permute-start(bf16[144,1536]{1,0:T(8,128)(2,1)S(1)} %get-tuple-element.47), channel_id=1, source_target_pairs={{0,24},{1,9},{2,10},{3,11},{4,28},{5,29},{6,30},{7,15},{8,0},{9,17... | collective-permute-start | bytes 1327112 | tf_op jit(solution)/shard_map/ppermute | solution.py:47
  122.0 9.5 %copy-start.1 = (bf16[1,1,384,1536]{3,2,1,0:T(8,128)(2,1)S(1)}, bf16[1,1,384,1536]{3,2,1,0:T(8,128)(2,1)}, u32[]{:S(2)}) copy-start(bf16[1,1,384,1536]{3,2,1,0:T(8,128)(2,1)} %param.9) | copy-start | bytes 3538948
  122.0 9.5 %copy-start.4 = (f32[1,1536]{1,0:T(1,128)S(1)}, f32[1,1536]{1,0:T(1,128)}, u32[]{:S(2)}) copy-start(f32[1,1536]{1,0:T(1,128)} %gate_ref.3) | copy-start | bytes 18436
  132.6 10.5 %collective-permute-start.20 = (bf16[192,1536]{1,0:T(8,128)(2,1)S(1)}, bf16[192,1536]{1,0:T(8,128)(2,1)S(1)}, u32[]{:S(2)}, u32[]{:S(2)}) collective-permute-start(bf16[192,1536]{1,0:T(8,128)(2,1)S(1)} %project_out.2), channel_id=1, source_target_pairs={{0,32},{32,64},{64,96},{96,128},{128,160},{160,192},{192,224},{224... | collective-permute-start | bytes 1769480 | tf_op jit(solution)/shard_map/ppermute | solution.py:58
  143.2 10.5 %collective-permute-start.21 = (bf16[192,1536]{1,0:T(8,128)(2,1)S(1)}, bf16[192,1536]{1,0:T(8,128)(2,1)S(1)}, u32[]{:S(2)}, u32[]{:S(2)}) collective-permute-start(bf16[192,1536]{1,0:T(8,128)(2,1)S(1)} %project_out.3), channel_id=1, source_target_pairs={{0,32},{32,64},{64,96},{96,128},{128,160},{160,192},{192,224},{224... | collective-permute-start | bytes 1769480 | tf_op jit(solution)/shard_map/ppermute | solution.py:58

commit v6 on v5

--- a/solution.py
+++ b/solution.py
@@ -335,17 +335,24 @@
     count = attended.shape[0]
     width = w_out.shape[1]
 
-    def body(a_ref, w_ref, gate_ref, x_ref, out_ref):
+    def body(a_ref, w_ref, gate_ref, x_hbm, out_ref, x_ref, sem):
+        rows_in = pltpu.make_async_copy(x_hbm.at[at : at + count, :], x_ref, sem)
+        rows_in.start()
         for j in range(width // COLS):
             cols = slice(j * COLS, (j + 1) * COLS)
             branch = jnp.dot(a_ref[...], w_ref[:, cols], preferred_element_type=jnp.float32)
-            residual = x_ref[at : at + count, cols].astype(jnp.float32)
+            if j == 0:
+                rows_in.wait()
+            residual = x_ref[:, cols].astype(jnp.float32)
             out_ref[:, cols] = (residual + gate_ref[:, cols] * branch).astype(jnp.bfloat16)
 
+    x = pltpu.with_memory_space_constraint(x, pltpu.HBM)
     shapes = [jax.ShapeDtypeStruct((count, width), jnp.bfloat16)]
+    scratch = [pltpu.VMEM((count, width), x.dtype), pltpu.SemaphoreType.DMA(())]
     flops = 2 * count * width * w_out.shape[0]
     operands = [attended, w_out, gate, x]
-    return kernel(body, "project_out", [VMEM] * 4, shapes, [], {}, flops, SMALL, operands)[0]
+    specs = [VMEM] * 3 + [HBM]
+    return kernel(body, "project_out", specs, shapes, scratch, {}, flops, SMALL, operands)[0]
 
 
 def on_device(arriving, modulation, gate, w_query, w_kv, w_out, qk_gain, neighbors, live):
@@ -410,8 +417,9 @@
     first_handed = to_next_section(first)
     attended = attend(scalars, after(query, first), window, count, count)
     second = project_out(attended, out_whole, gate, x, count)
-    parts = [first_handed, to_next_section(after(second, first_handed))]
-    return jnp.concatenate(parts, axis=0)[None, None]
+    second_handed = to_next_section(after(second, first_handed))
+    whole = lax.optimization_barrier(jnp.pad(first_handed, ((0, count), (0, 0))))
+    return lax.dynamic_update_slice(whole, second_handed, (count, 0))[None, None]
 
 
 def solution(mesh):

time: 155 us -> 156 us (level)
  waiting for transfers between devices: 79.9 us -> 60.9 us
  Pallas kernels: 32.8 us -> 50.1 us
  local copies, waits for them, and re-layouts: 0.04 us -> 1.98 us
  starting transfers between devices: 38.7 us -> 40.3 us
    pallas_call x15, Pallas kernels: 32.8 us -> 50.1 us  [kernel(): pl.pallas_call(body, in_specs=specs, out_specs=[VMEM for _ in shapes], ou...]
    ppermute x3, waiting for transfers between devices: 24.8 us -> 17 us  [along_y_by_place(): return lax.ppermute(value, 'patch', pairs)]
    ppermute x2, waiting for transfers between devices: 13.9 us -> 7.86 us  [to_next_section(): lax.ppermute(block, 'section', [(i, (i + 1) % count) for i in range(count)])]
    ppermute x4, waiting for transfers between devices: 11.7 us -> 6.51 us  [along_y(): lax.ppermute(value, 'patch', [(y * Z + z, (y + steps) % Y * Z + z) for y...]
    ppermute x2, starting transfers between devices: 0.03 us -> 1.61 us  [to_next_section(): lax.ppermute(block, 'section', [(i, (i + 1) % count) for i in range(count)])]
  transfers between devices with their start and end apart: 22 -> 22, of which waited for: 14 -> 12; matrix products, arithmetic and copies ran while one was open for 1% -> 2% of each run, Pallas kernels for 20% -> 31%
where the time goes in v6:
time: 156 us; the launch traced here: 155 us
  waiting for transfers between devices  60.9 us (39%)
  Pallas kernels  50.1 us (32%)
  starting transfers between devices  40.3 us (26%)
  local copies, waits for them, and re-layouts  1.98 us (1%)
    pallas_call x15, Pallas kernels, kernel(): pl.pallas_call(body, in_specs=specs, out_specs=[VMEM for _ in shapes], ou...  50.1 us
    ppermute x11, waiting for transfers between devices, along_z(): return lax.ppermute(value, 'patch', pairs)  28.3 us
    ppermute x3, waiting for transfers between devices, along_y_by_place(): return lax.ppermute(value, 'patch', pairs)  17 us
    ppermute x11, starting transfers between devices, along_z(): return lax.ppermute(value, 'patch', pairs)  16.9 us
    ppermute x1, starting transfers between devices, around_rows(): return lax.ppermute(value, 'patch', ends + [(b, a) for a, b in ends])  9.68 us
    ppermute x2, waiting for transfers between devices, to_next_section(): lax.ppermute(block, 'section', [(i, (i + 1) % count) for i in range(count)])  7.86 us
    ppermute x4, waiting for transfers between devices, along_y(): lax.ppermute(value, 'patch', [(y * Z + z, (y + steps) % Y * Z + z) for y...  6.51 us
    ppermute x4, starting transfers between devices, along_y(): lax.ppermute(value, 'patch', [(y * Z + z, (y + steps) % Y * Z + z) for y...  5.9 us
  transfers between devices with their start and end apart: 22, of which 12 were waited for; matrix products, arithmetic and copies ran while one was open for 2% of the time, Pallas kernels for 31%

profile of v6, /device:TPU:24, one launch (start us, length us, event | category | flops | bytes accessed | tf_op | source)
XLA Modules:
  0.0 155.5 jit_solution(10816741660273703398)
XLA Ops:
  0.0 2.7 %collective-permute-start.11 = (bf16[384,1536]{1,0:T(8,128)(2,1)}, bf16[384,1536]{1,0:T(8,128)(2,1)S(1)}, u32[]{:S(2)}, u32[]{:S(2)}) collective-permute-start(bf16[384,1536]{1,0:T(8,128)(2,1)} %bitcast.29), channel_id=1, source_target_pairs={{7,15},{15,23},{23,31},{8,0},{16,8},{24,16},{39,47},{47,55},{55,63... | collective-permute-start | bytes 3538952 | tf_op jit(solution)/shard_map/ppermute | solution.py:53
  2.7 1.0 pad_maximum_fusion.refs_2_
  3.7 0.1 collective-permute-start
  3.8 4.5 %collective-permute-start.3 = (bf16[96,1536]{1,0:T(8,128)(2,1)S(1)}, bf16[96,1536]{1,0:T(8,128)(2,1)S(1)}, u32[]{:S(2)}, u32[]{:S(2)}) collective-permute-start(bf16[96,1536]{1,0:T(8,128)(2,1)S(1)} %pad_maximum_fusion.refs_2_), channel_id=1, source_target_pairs={{0,7},{1,0},{2,1},{3,2},{4,3},{5,4},{6,5},{7,6},{8,15},{9,8},{10,9... | collective-permute-start | bytes 884744 | tf_op jit(solution)/shard_map/ppermute | solution.py:31
  8.3 6.9 %collective-permute-done.refs_1_ = bf16[96,1536]{1,0:T(8,128)(2,1)S(1)} collective-permute-done((bf16[96,1536]{1,0:T(8,128)(2,1)S(1)}, bf16[96,1536]{1,0:T(8,128)(2,1)S(1)}, u32[]{:S(2)}, u32[]{:S(2)}) %collective-permute-start) | collective-permute-done | bytes 294944 | tf_op jit(solution)/shard_map/ppermute | solution.py:31
  15.2 3.2 %collective-permute-start.4 = (bf16[96,1536]{1,0:T(8,128)(2,1)S(1)}, bf16[96,1536]{1,0:T(8,128)(2,1)S(1)}, u32[]{:S(2)}, u32[]{:S(2)}) collective-permute-start(bf16[96,1536]{1,0:T(8,128)(2,1)S(1)} %collective-permute-done.3.refs_3_), channel_id=1, source_target_pairs={{0,7},{1,0},{2,1},{3,2},{4,3},{5,4},{6,5},{7,6},{8,15},{9,8},{10,9... | collective-permute-start | bytes 884744 | tf_op jit(solution)/shard_map/ppermute | solution.py:31
  18.5 6.2 %collective-permute-done.1.refs_0_ = bf16[96,1536]{1,0:T(8,128)(2,1)S(1)} collective-permute-done((bf16[96,1536]{1,0:T(8,128)(2,1)S(1)}, bf16[96,1536]{1,0:T(8,128)(2,1)S(1)}, u32[]{:S(2)}, u32[]{:S(2)}) %collective-permute-start.1) | collective-permute-done | bytes 294944 | tf_op jit(solution)/shard_map/ppermute | solution.py:31
  24.7 0.1 join.2.refs_0_
  24.8 2.0 %collective-permute-start.7 = (bf16[480,1536]{1,0:T(8,128)(2,1)S(1)}, bf16[480,1536]{1,0:T(8,128)(2,1)S(1)}, u32[]{:S(2)}, u32[]{:S(2)}) collective-permute-start(bf16[480,1536]{1,0:T(8,128)(2,1)S(1)} %join.2.refs_0_), channel_id=1, source_target_pairs={{0,8},{1,9},{2,10},{3,11},{4,12},{5,13},{6,14},{7,15},{8,16},{9,17... | collective-permute-start | bytes 4423688 | tf_op jit(solution)/shard_map/ppermute | solution.py:40
  26.7 0.2 collective-permute-start.8
  27.0 3.2 %collective-permute-start.6 = (bf16[96,1536]{1,0:T(8,128)(2,1)S(1)}, bf16[96,1536]{1,0:T(8,128)(2,1)S(1)}, u32[]{:S(2)}, u32[]{:S(2)}) collective-permute-start(bf16[96,1536]{1,0:T(8,128)(2,1)S(1)} %collective-permute-done.4.refs_4_), channel_id=1, source_target_pairs={{0,7},{1,0},{2,1},{3,2},{4,3},{5,4},{6,5},{7,6},{8,15},{9,8},{10,9... | collective-permute-start | bytes 884744 | tf_op jit(solution)/shard_map/ppermute | solution.py:31
  30.2 2.9 %collective-permute-done.2.refs_1_ = bf16[96,1536]{1,0:T(8,128)(2,1)S(1)} collective-permute-done((bf16[96,1536]{1,0:T(8,128)(2,1)S(1)}, bf16[96,1536]{1,0:T(8,128)(2,1)S(1)}, u32[]{:S(2)}, u32[]{:S(2)}) %collective-permute-start.2) | collective-permute-done | bytes 294944 | tf_op jit(solution)/shard_map/ppermute | solution.py:31
  33.1 0.2 broadcast_select_fusion
  33.3 1.1 collective-permute-done.6.refs_2_
  34.5 6.6 %collective-permute-done.5.refs_0_ = bf16[96,1536]{1,0:T(8,128)(2,1)S(1)} collective-permute-done((bf16[96,1536]{1,0:T(8,128)(2,1)S(1)}, bf16[96,1536]{1,0:T(8,128)(2,1)S(1)}, u32[]{:S(2)}, u32[]{:S(2)}) %collective-permute-start.5) | collective-permute-done | bytes 294944 | tf_op jit(solution)/shard_map/ppermute | solution.py:31
  41.1 3.2 %collective-permute-start.12 = (bf16[384,1536]{1,0:T(8,128)(2,1)S(1)}, bf16[384,1536]{1,0:T(8,128)(2,1)S(1)}, u32[]{:S(2)}, u32[]{:S(2)}) collective-permute-start(bf16[384,1536]{1,0:T(8,128)(2,1)S(1)} %get-tuple-element.33), channel_id=1, source_target_pairs={{0,7},{1,0},{2,1},{3,2},{4,3},{5,4},{6,5},{7,6},{8,15},{9,8},{10,9... | collective-permute-start | bytes 3538952 | tf_op jit(solution)/shard_map/ppermute | solution.py:31
  45.0 1.6 %collective-permute-start.9 = (bf16[288,1536]{1,0:T(8,128)(2,1)S(1)}, bf16[288,1536]{1,0:T(8,128)(2,1)S(1)}, u32[]{:S(2)}, u32[]{:S(2)}) collective-permute-start(bf16[288,1536]{1,0:T(8,128)(2,1)S(1)} %join.3.refs_3_), channel_id=1, source_target_pairs={{0,8},{1,9},{2,10},{3,11},{4,12},{5,13},{6,14},{7,15},{8,16},{9,17... | collective-permute-start | bytes 2654216 | tf_op jit(solution)/shard_map/ppermute | solution.py:40
  46.7 7.3 %own_tile.1 = (bf16[5,384,3072]{2,1,0:T(8,128)(2,1)S(1)}, bf16[384,1536]{1,0:T(8,128)(2,1)S(1)}, bf16[1536,3072]{1,0:T(8,128)(2,1)S(1)}) custom-call(bf16[384,1536]{1,0:T(8,128)(2,1)} %bitcast.30, f32[2,1536]{1,0:T(2,128)S(1)} %bitcast.16, bf16[1536,3072]{1,0:T(8,128)(2,1)} %bitcast.36, f32[1,1536]{1,0:T(1,128)S(1)} %get-tuple-element.56.gain_ref), custom_call_target="tpu_custom_call" | custom-call | flops 3623878656 | bytes 10635264 | tf_op jit(solution)/shard_map/own_tile/pallas_call | solution.py:83
  54.0 6.1 %collective-permute-done.7.refs_0_.refs_1_ = bf16[480,1536]{1,0:T(8,128)(2,1)S(1)} collective-permute-done((bf16[480,1536]{1,0:T(8,128)(2,1)S(1)}, bf16[480,1536]{1,0:T(8,128)(2,1)S(1)}, u32[]{:S(2)}, u32[]{:S(2)}) %collective-permute-start.7) | collective-permute-done | bytes 1474592 | tf_op jit(solution)/shard_map/ppermute | solution.py:40
  60.1 2.0 %collective-permute-start.10 = (bf16[288,1536]{1,0:T(8,128)(2,1)S(1)}, bf16[288,1536]{1,0:T(8,128)(2,1)S(1)}, u32[]{:S(2)}, u32[]{:S(2)}) collective-permute-start(bf16[288,1536]{1,0:T(8,128)(2,1)S(1)} %join.3.refs_3_), channel_id=1, source_target_pairs={{0,24},{1,25},{2,26},{3,27},{4,28},{5,29},{6,30},{7,31},{8,0},{9,1... | collective-permute-start | bytes 2654216 | tf_op jit(solution)/shard_map/ppermute | solution.py:40
  62.1 4.6 %collective-permute-done.13.x_ref = bf16[384,1536]{1,0:T(8,128)(2,1)S(1)} collective-permute-done((bf16[384,1536]{1,0:T(8,128)(2,1)S(1)}, bf16[384,1536]{1,0:T(8,128)(2,1)S(1)}, u32[]{:S(2)}, u32[]{:S(2)}) %collective-permute-start.13) | collective-permute-done | bytes 1179680 | tf_op jit(solution)/shard_map/ppermute | solution.py:31
  66.7 1.4 collective-permute-start.16
  68.1 1.3 collective-permute-start.15
  69.4 0.2 broadcast_select_fusion.1
  69.6 5.7 %near_tile.5._ = bf16[5,384,3072]{2,1,0:T(8,128)(2,1)S(1)} custom-call(s32[1]{0:T(128)} %bitcast.at_ref, s32[4]{0:T(128)S(1)} %bitcast.22, s32[1]{0:T(128)S(6)} %copy.21.live_ref, bf16[384,1536]{1,0:T(8,128)(2,1)S(1)} %collective-permute-done.13.x_ref, f32[2,1536]{1,0:T(2,128)S(1)} %bitcast.17, ...), custom_call_target="tpu_custom_call", output_to_operand_aliasing={{}: (7, {})} | custom-call | flops 3623878656 | bytes 22431768 | tf_op jit(solution)/shard_map/near_tile/pallas_call | solution.py:83
  75.3 5.7 %near_tile.6._ = bf16[5,384,3072]{2,1,0:T(8,128)(2,1)S(1)} custom-call(s32[1]{0:T(128)} %bitcast.at_ref, s32[4]{0:T(128)S(1)} %bitcast.23, s32[1]{0:T(128)S(6)} %copy.21.live_ref, bf16[384,1536]{1,0:T(8,128)(2,1)S(1)} %collective-permute-done.12.x_ref, f32[2,1536]{1,0:T(2,128)S(1)} %bitcast.18, ...), custom_call_target="tpu_custom_call", output_to_operand_aliasing={{}: (7, {})} | custom-call | flops 3623878656 | bytes 22431768 | tf_op jit(solution)/shard_map/near_tile/pallas_call | solution.py:83
  81.0 0.4 collective-permute-done.10.refs_3_.refs_5_
  81.4 0.2 onward.1
  81.6 1.3 collective-permute-start.14
  82.9 9.7 %collective-permute-start.17 = (bf16[384,1536]{1,0:T(8,128)(2,1)S(1)}, bf16[384,1536]{1,0:T(8,128)(2,1)S(1)}, u32[]{:S(2)}, u32[]{:S(2)}) collective-permute-start(bf16[384,1536]{1,0:T(8,128)(2,1)S(1)} %broadcast_select_fusion.1), channel_id=1, source_target_pairs={{7,8},{15,16},{23,24},{8,7},{16,15},{24,23},{39,40},{47,48},{55,56... | collective-permute-start | bytes 3538952 | tf_op jit(solution)/shard_map/ppermute | solution.py:36
  92.6 0.1 collective-permute-start.18
  92.7 2.0 %collective-permute-start.19 = (bf16[144,1536]{1,0:T(8,128)(2,1)S(1)}, bf16[144,1536]{1,0:T(8,128)(2,1)S(1)}, u32[]{:S(2)}, u32[]{:S(2)}) collective-permute-start(bf16[144,1536]{1,0:T(8,128)(2,1)S(1)} %get-tuple-element.47), channel_id=1, source_target_pairs={{0,24},{1,9},{2,10},{3,11},{4,28},{5,29},{6,30},{7,15},{8,0},{9,17... | collective-permute-start | bytes 1327112 | tf_op jit(solution)/shard_map/ppermute | solution.py:47
  94.7 0.6 near_tile.7._
  95.3 0.8 near_tile.8._
  96.1 15.7 %collective-permute-done.14.refs_6_ = bf16[384,1536]{1,0:T(8,128)(2,1)S(1)} collective-permute-done((bf16[384,1536]{1,0:T(8,128)(2,1)S(1)}, bf16[384,1536]{1,0:T(8,128)(2,1)S(1)}, u32[]{:S(2)}, u32[]{:S(2)}) %collective-permute-start.14) | collective-permute-done | bytes 1179680 | tf_op jit(solution)/shard_map/ppermute | solution.py:47
  111.8 2.5 %project_query.1.q_ref = bf16[384,1536]{1,0:T(8,128)(2,1)S(1)} custom-call(s32[1]{0:T(128)} %bitcast.at_ref, bf16[384,1536]{1,0:T(8,128)(2,1)S(1)} %get-tuple-element.31.normed_ref, f32[1,1536]{1,0:T(1,128)S(1)} %get-tuple-element.55.gain_ref, bf16[480,1536]{1,0:T(8,128)(2,1)S(1)} %join.2.refs_0_, ...), custom_call_target="tpu_custom_call" | custom-call | flops 1811939328 | bytes 9443332 | tf_op jit(solution)/shard_map/project_query/pallas_call | solution.py:83
  114.3 1.1 collective-permute-done.17.x_ref
  115.4 5.7 %near_tile.9.window_ref = bf16[5,384,3072]{2,1,0:T(8,128)(2,1)S(1)} custom-call(s32[1]{0:T(128)} %bitcast.at_ref, s32[4]{0:T(128)S(1)} %bitcast.26, s32[1]{0:T(128)S(6)} %copy.21.live_ref, bf16[384,1536]{1,0:T(8,128)(2,1)S(1)} %collective-permute-done.17.x_ref, f32[2,1536]{1,0:T(2,128)S(1)} %bitcast.21, ...), custom_call_target="tpu_custom_call", output_to_operand_aliasing={{}: (7, {})} | custom-call | flops 3623878656 | bytes 22431768 | tf_op jit(solution)/shard_map/near_tile/pallas_call | solution.py:83
  121.1 8.6 %attend.2.a_ref = bf16[192,1536]{1,0:T(8,128)(2,1)S(1)} custom-call(s32[1]{0:T(128)} %bitcast.at_ref, s32[4]{0:T(128)S(1)} %bitcast.27, s32[1]{0:T(128)S(6)} %copy.21.live_ref, bf16[384,1536]{1,0:T(8,128)(2,1)S(1)} %project_query.1.q_ref, bf16[5,384,3072]{2,1,0:T(8,128)(2,1)S(1)} %near_tile.9.window_ref), custom_call_target="tpu_custom_call" | custom-call | flops 1811939328 | bytes 12976152 | tf_op jit(solution)/shard_map/attend/pallas_call | solution.py:83
  129.8 1.3 collective-permute-done.18.refs_6_
  131.1 0.4 whole_out.1.w_ref
  131.5 1.9 %project_out.2 = bf16[192,1536]{1,0:T(8,128)(2,1)S(1)} custom-call(bf16[192,1536]{1,0:T(8,128)(2,1)S(1)} %attend.2.a_ref, bf16[1536,1536]{1,0:T(8,128)(2,1)S(1)} %whole_out.1.w_ref, f32[1,1536]{1,0:T(1,128)S(1)} %copy-done.2, bf16[384,1536]{1,0:T(8,128)(2,1)} %bitcast.31), custom_call_target="tpu_custom_call" | custom-call | flops 905969664 | bytes 6494208 | tf_op jit(solution)/shard_map/project_out/pallas_call | solution.py:83
  133.5 8.7 %attend.3.a_ref = bf16[192,1536]{1,0:T(8,128)(2,1)S(1)} custom-call(s32[1]{0:T(128)} %bitcast.at_ref, s32[4]{0:T(128)S(1)} %bitcast.28, s32[1]{0:T(128)S(6)} %copy.21.live_ref, bf16[384,1536]{1,0:T(8,128)(2,1)S(1)} %project_query.1.q_ref, bf16[5,384,3072]{2,1,0:T(8,128)(2,1)S(1)} %near_tile.9.window_ref), custom_call_target="tpu_custom_call" | custom-call | flops 1811939328 | bytes 12976152 | tf_op jit(solution)/shard_map/attend/pallas_call | solution.py:83
  142.2 1.9 %project_out.3 = bf16[192,1536]{1,0:T(8,128)(2,1)S(1)} custom-call(bf16[192,1536]{1,0:T(8,128)(2,1)S(1)} %attend.3.a_ref, bf16[1536,1536]{1,0:T(8,128)(2,1)S(1)} %whole_out.1.w_ref, f32[1,1536]{1,0:T(1,128)S(1)} %copy-done.2, bf16[384,1536]{1,0:T(8,128)(2,1)} %bitcast.32), custom_call_target="tpu_custom_call" | custom-call | flops 905969664 | bytes 6494208 | tf_op jit(solution)/shard_map/project_out/pallas_call | solution.py:83
  144.1 1.6 %collective-permute-start.21 = (bf16[192,1536]{1,0:T(8,128)(2,1)S(1)}, bf16[192,1536]{1,0:T(8,128)(2,1)S(1)}, u32[]{:S(2)}, u32[]{:S(2)}) collective-permute-start(bf16[192,1536]{1,0:T(8,128)(2,1)S(1)} %project_out.3), channel_id=1, source_target_pairs={{0,32},{32,64},{64,96},{96,128},{128,160},{160,192},{192,224},{224... | collective-permute-start | bytes 1769480 | tf_op jit(solution)/shard_map/ppermute | solution.py:58
  145.7 1.1 pad.4
  146.8 7.9 %collective-permute-done.21 = bf16[192,1536]{1,0:T(8,128)(2,1)S(1)} collective-permute-done((bf16[192,1536]{1,0:T(8,128)(2,1)S(1)}, bf16[192,1536]{1,0:T(8,128)(2,1)S(1)}, u32[]{:S(2)}, u32[]{:S(2)}) %collective-permute-start.21) | collective-permute-done | bytes 589856 | tf_op jit(solution)/shard_map/ppermute | solution.py:58
  154.6 0.9 bitcast_dynamic-update-slice_fusion
  (27 shorter events, 0.2 us)
Async XLA Ops:
  0.0 33.1 %collective-permute-start.11 = (bf16[384,1536]{1,0:T(8,128)(2,1)}, bf16[384,1536]{1,0:T(8,128)(2,1)S(1)}, u32[]{:S(2)}, u32[]{:S(2)}) collective-permute-start(bf16[384,1536]{1,0:T(8,128)(2,1)} %bitcast.29), channel_id=1, source_target_pairs={{7,15},{15,23},{23,31},{8,0},{16,8},{24,16},{39,47},{47,55},{55,63... | collective-permute-start | bytes 3538952 | tf_op jit(solution)/shard_map/ppermute | solution.py:53
  3.7 11.5 %collective-permute-start = (bf16[96,1536]{1,0:T(8,128)(2,1)S(1)}, bf16[96,1536]{1,0:T(8,128)(2,1)S(1)}, u32[]{:S(2)}, u32[]{:S(2)}) collective-permute-start(bf16[96,1536]{1,0:T(8,128)(2,1)S(1)} %pad_maximum_fusion.refs_2_), channel_id=1, source_target_pairs={{0,1},{1,2},{2,3},{3,4},{4,5},{5,6},{6,7},{7,0},{8,9},{9,10},{10,1... | collective-permute-start | bytes 884744 | tf_op jit(solution)/shard_map/ppermute | solution.py:31
  3.8 11.4 %collective-permute-start.3 = (bf16[96,1536]{1,0:T(8,128)(2,1)S(1)}, bf16[96,1536]{1,0:T(8,128)(2,1)S(1)}, u32[]{:S(2)}, u32[]{:S(2)}) collective-permute-start(bf16[96,1536]{1,0:T(8,128)(2,1)S(1)} %pad_maximum_fusion.refs_2_), channel_id=1, source_target_pairs={{0,7},{1,0},{2,1},{3,2},{4,3},{5,4},{6,5},{7,6},{8,15},{9,8},{10,9... | collective-permute-start | bytes 884744 | tf_op jit(solution)/shard_map/ppermute | solution.py:31
  15.2 9.4 %collective-permute-start.1 = (bf16[96,1536]{1,0:T(8,128)(2,1)S(1)}, bf16[96,1536]{1,0:T(8,128)(2,1)S(1)}, u32[]{:S(2)}, u32[]{:S(2)}) collective-permute-start(bf16[96,1536]{1,0:T(8,128)(2,1)S(1)} %collective-permute-done.refs_1_), channel_id=1, source_target_pairs={{0,1},{1,2},{2,3},{3,4},{4,5},{5,6},{6,7},{7,0},{8,9},{9,10},{10,1... | collective-permute-start | bytes 884744 | tf_op jit(solution)/shard_map/ppermute | solution.py:31
  15.2 9.4 %collective-permute-start.4 = (bf16[96,1536]{1,0:T(8,128)(2,1)S(1)}, bf16[96,1536]{1,0:T(8,128)(2,1)S(1)}, u32[]{:S(2)}, u32[]{:S(2)}) collective-permute-start(bf16[96,1536]{1,0:T(8,128)(2,1)S(1)} %collective-permute-done.3.refs_3_), channel_id=1, source_target_pairs={{0,7},{1,0},{2,1},{3,2},{4,3},{5,4},{6,5},{7,6},{8,15},{9,8},{10,9... | collective-permute-start | bytes 884744 | tf_op jit(solution)/shard_map/ppermute | solution.py:31
  24.6 8.5 %collective-permute-start.2 = (bf16[96,1536]{1,0:T(8,128)(2,1)S(1)}, bf16[96,1536]{1,0:T(8,128)(2,1)S(1)}, u32[]{:S(2)}, u32[]{:S(2)}) collective-permute-start(bf16[96,1536]{1,0:T(8,128)(2,1)S(1)} %collective-permute-done.1.refs_0_), channel_id=1, source_target_pairs={{0,1},{1,2},{2,3},{3,4},{4,5},{5,6},{6,7},{7,0},{8,9},{9,10},{10,1... | collective-permute-start | bytes 884744 | tf_op jit(solution)/shard_map/ppermute | solution.py:31
  24.6 8.5 %copy-start.3 = (bf16[1,1,384,1536]{3,2,1,0:T(8,128)(2,1)S(1)}, bf16[1,1,384,1536]{3,2,1,0:T(8,128)(2,1)}, u32[]{:S(2)}) copy-start(bf16[1,1,384,1536]{3,2,1,0:T(8,128)(2,1)} %param.9) | copy-start | bytes 3538948
  24.8 20.2 %copy-start.4 = (f32[1,2,1536]{2,1,0:T(2,128)S(1)}, f32[1,2,1536]{2,1,0:T(2,128)}, u32[]{:S(2)}) copy-start(f32[1,2,1536]{2,1,0:T(2,128)} %param.15) | copy-start | bytes 36868
  24.8 35.3 %collective-permute-start.7 = (bf16[480,1536]{1,0:T(8,128)(2,1)S(1)}, bf16[480,1536]{1,0:T(8,128)(2,1)S(1)}, u32[]{:S(2)}, u32[]{:S(2)}) collective-permute-start(bf16[480,1536]{1,0:T(8,128)(2,1)S(1)} %join.2.refs_0_), channel_id=1, source_target_pairs={{0,8},{1,9},{2,10},{3,11},{4,12},{5,13},{6,14},{7,15},{8,16},{9,17... | collective-permute-start | bytes 4423688 | tf_op jit(solution)/shard_map/ppermute | solution.py:40
  26.7 33.4 %collective-permute-start.8 = (bf16[480,1536]{1,0:T(8,128)(2,1)S(1)}, bf16[480,1536]{1,0:T(8,128)(2,1)S(1)}, u32[]{:S(2)}, u32[]{:S(2)}) collective-permute-start(bf16[480,1536]{1,0:T(8,128)(2,1)S(1)} %join.2.refs_0_), channel_id=1, source_target_pairs={{0,24},{1,25},{2,26},{3,27},{4,28},{5,29},{6,30},{7,31},{8,0},{9,1... | collective-permute-start | bytes 4423688 | tf_op jit(solution)/shard_map/ppermute | solution.py:40
  27.0 7.5 %collective-permute-start.6 = (bf16[96,1536]{1,0:T(8,128)(2,1)S(1)}, bf16[96,1536]{1,0:T(8,128)(2,1)S(1)}, u32[]{:S(2)}, u32[]{:S(2)}) collective-permute-start(bf16[96,1536]{1,0:T(8,128)(2,1)S(1)} %collective-permute-done.4.refs_4_), channel_id=1, source_target_pairs={{0,7},{1,0},{2,1},{3,2},{4,3},{5,4},{6,5},{7,6},{8,15},{9,8},{10,9... | collective-permute-start | bytes 884744 | tf_op jit(solution)/shard_map/ppermute | solution.py:31
  33.1 7.9 %collective-permute-start.5 = (bf16[96,1536]{1,0:T(8,128)(2,1)S(1)}, bf16[96,1536]{1,0:T(8,128)(2,1)S(1)}, u32[]{:S(2)}, u32[]{:S(2)}) collective-permute-start(bf16[96,1536]{1,0:T(8,128)(2,1)S(1)} %collective-permute-done.2.refs_1_), channel_id=1, source_target_pairs={{0,1},{1,2},{2,3},{3,4},{4,5},{5,6},{6,7},{7,0},{8,9},{9,10},{10,1... | collective-permute-start | bytes 884744 | tf_op jit(solution)/shard_map/ppermute | solution.py:31
  33.3 13.4 %copy-start = (f32[1,2,1536]{2,1,0:T(2,128)S(1)}, f32[1,2,1536]{2,1,0:T(2,128)}, u32[]{:S(2)}) copy-start(f32[1,2,1536]{2,1,0:T(2,128)} %param.10) | copy-start | bytes 36868
  41.1 25.7 %collective-permute-start.13 = (bf16[384,1536]{1,0:T(8,128)(2,1)S(1)}, bf16[384,1536]{1,0:T(8,128)(2,1)S(1)}, u32[]{:S(2)}, u32[]{:S(2)}) collective-permute-start(bf16[384,1536]{1,0:T(8,128)(2,1)S(1)} %get-tuple-element.35), channel_id=1, source_target_pairs={{0,1},{1,2},{2,3},{3,4},{4,5},{5,6},{6,7},{7,0},{8,9},{9,10},{10,1... | collective-permute-start | bytes 3538952 | tf_op jit(solution)/shard_map/ppermute | solution.py:31
  41.1 27.0 %collective-permute-start.12 = (bf16[384,1536]{1,0:T(8,128)(2,1)S(1)}, bf16[384,1536]{1,0:T(8,128)(2,1)S(1)}, u32[]{:S(2)}, u32[]{:S(2)}) collective-permute-start(bf16[384,1536]{1,0:T(8,128)(2,1)S(1)} %get-tuple-element.33), channel_id=1, source_target_pairs={{0,7},{1,0},{2,1},{3,2},{4,3},{5,4},{6,5},{7,6},{8,15},{9,8},{10,9... | collective-permute-start | bytes 3538952 | tf_op jit(solution)/shard_map/ppermute | solution.py:31
  45.0 35.9 %collective-permute-start.9 = (bf16[288,1536]{1,0:T(8,128)(2,1)S(1)}, bf16[288,1536]{1,0:T(8,128)(2,1)S(1)}, u32[]{:S(2)}, u32[]{:S(2)}) collective-permute-start(bf16[288,1536]{1,0:T(8,128)(2,1)S(1)} %join.3.refs_3_), channel_id=1, source_target_pairs={{0,8},{1,9},{2,10},{3,11},{4,12},{5,13},{6,14},{7,15},{8,16},{9,17... | collective-permute-start | bytes 2654216 | tf_op jit(solution)/shard_map/ppermute | solution.py:40
  60.1 9.5 %copy-start.1 = (s32[1,4]{1,0:T(1,128)S(1)}, s32[1,4]{1,0:T(1,128)}, u32[]{:S(2)}) copy-start(s32[1,4]{1,0:T(1,128)} %param.16) | copy-start | bytes 52
  60.1 21.3 %collective-permute-start.10 = (bf16[288,1536]{1,0:T(8,128)(2,1)S(1)}, bf16[288,1536]{1,0:T(8,128)(2,1)S(1)}, u32[]{:S(2)}, u32[]{:S(2)}) collective-permute-start(bf16[288,1536]{1,0:T(8,128)(2,1)S(1)} %join.3.refs_3_), channel_id=1, source_target_pairs={{0,24},{1,25},{2,26},{3,27},{4,28},{5,29},{6,30},{7,31},{8,0},{9,1... | collective-permute-start | bytes 2654216 | tf_op jit(solution)/shard_map/ppermute | solution.py:40
  66.7 26.0 %collective-permute-start.16 = (bf16[384,1536]{1,0:T(8,128)(2,1)S(1)}, bf16[384,1536]{1,0:T(8,128)(2,1)S(1)}, u32[]{:S(2)}, u32[]{:S(2)}) collective-permute-start(bf16[384,1536]{1,0:T(8,128)(2,1)S(1)} %collective-permute-done.13.x_ref), channel_id=1, source_target_pairs={{0,1},{1,2},{2,3},{3,4},{4,5},{5,6},{6,7},{8,9},{9,10},{10,11},{11... | collective-permute-start | bytes 3538952 | tf_op jit(solution)/shard_map/ppermute | solution.py:31
  68.1 27.2 %collective-permute-start.15 = (bf16[384,1536]{1,0:T(8,128)(2,1)S(1)}, bf16[384,1536]{1,0:T(8,128)(2,1)S(1)}, u32[]{:S(2)}, u32[]{:S(2)}) collective-permute-start(bf16[384,1536]{1,0:T(8,128)(2,1)S(1)} %collective-permute-done.12.x_ref), channel_id=1, source_target_pairs={{1,0},{2,1},{3,2},{4,3},{5,4},{6,5},{7,6},{9,8},{10,9},{11,10},{12... | collective-permute-start | bytes 3538952 | tf_op jit(solution)/shard_map/ppermute | solution.py:31
  81.6 30.2 %collective-permute-start.14 = (bf16[384,1536]{1,0:T(8,128)(2,1)S(1)}, bf16[384,1536]{1,0:T(8,128)(2,1)S(1)}, u32[]{:S(2)}, u32[]{:S(2)}) collective-permute-start(bf16[384,1536]{1,0:T(8,128)(2,1)S(1)} %get-tuple-element.41), channel_id=1, source_target_pairs={{0,24},{1,25},{2,26},{3,27},{4,12},{5,13},{6,14},{7,15},{8,0},{9,1... | collective-permute-start | bytes 3538952 | tf_op jit(solution)/shard_map/ppermute | solution.py:47
  82.9 32.5 %collective-permute-start.17 = (bf16[384,1536]{1,0:T(8,128)(2,1)S(1)}, bf16[384,1536]{1,0:T(8,128)(2,1)S(1)}, u32[]{:S(2)}, u32[]{:S(2)}) collective-permute-start(bf16[384,1536]{1,0:T(8,128)(2,1)S(1)} %broadcast_select_fusion.1), channel_id=1, source_target_pairs={{7,8},{15,16},{23,24},{8,7},{16,15},{24,23},{39,40},{47,48},{55,56... | collective-permute-start | bytes 3538952 | tf_op jit(solution)/shard_map/ppermute | solution.py:36
  92.6 38.5 %collective-permute-start.18 = (bf16[240,1536]{1,0:T(8,128)(2,1)S(1)}, bf16[240,1536]{1,0:T(8,128)(2,1)S(1)}, u32[]{:S(2)}, u32[]{:S(2)}) collective-permute-start(bf16[240,1536]{1,0:T(8,128)(2,1)S(1)} %get-tuple-element.46), channel_id=1, source_target_pairs={{0,8},{1,9},{2,10},{3,11},{4,28},{5,29},{6,30},{7,31},{8,16},{9,17... | collective-permute-start | bytes 2211848 | tf_op jit(solution)/shard_map/ppermute | solution.py:47
  92.7 37.1 %collective-permute-start.19 = (bf16[144,1536]{1,0:T(8,128)(2,1)S(1)}, bf16[144,1536]{1,0:T(8,128)(2,1)S(1)}, u32[]{:S(2)}, u32[]{:S(2)}) collective-permute-start(bf16[144,1536]{1,0:T(8,128)(2,1)S(1)} %get-tuple-element.47), channel_id=1, source_target_pairs={{0,24},{1,9},{2,10},{3,11},{4,28},{5,29},{6,30},{7,15},{8,0},{9,17... | collective-permute-start | bytes 1327112 | tf_op jit(solution)/shard_map/ppermute | solution.py:47
  129.8 1.7 %copy-start.2 = (f32[1,1536]{1,0:T(1,128)S(1)}, f32[1,1536]{1,0:T(1,128)}, u32[]{:S(2)}) copy-start(f32[1,1536]{1,0:T(1,128)} %gate_ref.3) | copy-start | bytes 18436
  133.5 10.6 %collective-permute-start.20 = (bf16[192,1536]{1,0:T(8,128)(2,1)S(1)}, bf16[192,1536]{1,0:T(8,128)(2,1)S(1)}, u32[]{:S(2)}, u32[]{:S(2)}) collective-permute-start(bf16[192,1536]{1,0:T(8,128)(2,1)S(1)} %project_out.2), channel_id=1, source_target_pairs={{0,32},{32,64},{64,96},{96,128},{128,160},{160,192},{192,224},{224... | collective-permute-start | bytes 1769480 | tf_op jit(solution)/shard_map/ppermute | solution.py:58
  144.1 10.5 %collective-permute-start.21 = (bf16[192,1536]{1,0:T(8,128)(2,1)S(1)}, bf16[192,1536]{1,0:T(8,128)(2,1)S(1)}, u32[]{:S(2)}, u32[]{:S(2)}) collective-permute-start(bf16[192,1536]{1,0:T(8,128)(2,1)S(1)} %project_out.3), channel_id=1, source_target_pairs={{0,32},{32,64},{64,96},{96,128},{128,160},{160,192},{192,224},{224... | collective-permute-start | bytes 1769480 | tf_op jit(solution)/shard_map/ppermute | solution.py:58
